TPU v7x, 32 devices: a whole 2x2x4 slice. The times are simulated.
32 devices in a mesh: groups: 2 (over y), col: 4 (over z), row: 2 (over x), sub: 2 (over core).
Axes of the slice: x: 2, y: 2, z: 4, core: 2. Of those that a mesh axis runs over, the one named last changes fastest.
Arguments:
- pair: float32 [16, 256, 128], P(('groups', 'row', 'sub'), 'col'), parts along dimension 0, may hold values from -6 to 6
- w_query: float32 [128, 128], replicated, may hold values from -0.5 to 0.5
- w_key: float32 [128, 128], replicated, may hold values from -0.5 to 0.5
- w_value: float32 [128, 128], replicated, may hold values from -0.5 to 0.5
- bias: bfloat16 [8, 256, 256], P('groups', 'col', ('row', 'sub')), parts along dimension 0, may hold values from -6 to 6
- grad_out: float32 [16, 256, 128], P(('groups', 'row', 'sub'), 'col'), parts along dimension 0, may hold values from -6 to 6
- log_total: float32 [4, 16, 256], P(None, ('groups', 'row', 'sub'), 'col'), parts along dimension 1, may hold values from 7 to 9
- row_corr: float32 [4, 16, 256], P(None, ('groups', 'row', 'sub'), 'col'), parts along dimension 1, may hold values from -3 to 3
Outputs:
- query_grad: float32 [16, 256, 128], P(('groups', 'row', 'sub'), 'col'), parts along dimension 0
- key_pair_grad: float32 [16, 256, 128], P(('groups', 'row', 'sub'), 'col'), parts along dimension 0
- bias_grad: float32 [8, 256, 256], P('groups', 'col', ('row', 'sub')), parts along dimension 0
There are 2 independent parts, one for each index of `groups`. A program takes and returns all parts, laid end to end along the dimension named above; an argument that names none is the same for every part. Nothing has to cross between parts.
All inputs are finite; a program needn't handle non-finite values.
Results may differ from a plain program's by a relative error of at most 0.0003.
Values may be sent and summed in bfloat16 or wider, within the bound.
No kernel may reach another device: no remote copies, remote signals or barrier semaphores. Data moves between devices by JAX's collectives and lax.ppermute only.
A program may use at most 64 MiB of HBM per device.

v0:
```python
import jax
import jax.numpy as jnp
from jax import lax
from jax.sharding import PartitionSpec as P

HIGH = lax.Precision.HIGHEST


def on_device(pair, w_query, w_key, w_value, bias, grad_out, log_total, row_corr):
    rows, cols, width = pair.shape
    heads = log_total.shape[0]
    proj = w_query.shape[1]
    head_dim = proj // heads
    scale = head_dim ** (-0.5)
    w_both = jnp.concatenate([w_key, w_value], axis=1)
    key_vals = jnp.einsum(
        "rkc,cd->rkd", lax.all_gather(pair, "col", axis=1, tiled=True), w_both, precision=HIGH
    )
    bias_rows = lax.all_gather(bias, ("row", "sub"), axis=2, tiled=True).astype(jnp.float32)
    total_keys = key_vals.shape[1]
    query = jnp.einsum("rjc,cd->rjd", pair, w_query, precision=HIGH)
    dscore_sum = jnp.zeros((heads, cols, total_keys), jnp.float32)
    dquery_rows = []
    dkey_rows = []
    for index in range(rows):
        keys = key_vals[index, :, :proj].reshape(total_keys, heads, head_dim)
        values = key_vals[index, :, proj:].reshape(total_keys, heads, head_dim)
        query_row = query[index].reshape(cols, heads, head_dim)
        grads = grad_out[index].reshape(cols, heads, head_dim)
        scores = jnp.einsum("jhd,khd->hjk", query_row, keys, precision=HIGH) * scale + bias_rows
        probs = jnp.exp(scores - log_total[:, index, :, None])
        dprobs = jnp.einsum("jhd,khd->hjk", grads, values, precision=HIGH)
        dscores = probs * (dprobs - row_corr[:, index, :, None])
        dquery = jnp.einsum("hjk,khd->jhd", dscores, keys, precision=HIGH) * scale
        dkeys = jnp.einsum("hjk,jhd->khd", dscores, query_row, precision=HIGH) * scale
        dvalues = jnp.einsum("hjk,jhd->khd", probs, grads, precision=HIGH)
        dscore_sum = dscore_sum + dscores
        dquery_rows.append(dquery.reshape(cols, proj))
        dkey_rows.append(
            jnp.concatenate(
                [dkeys.reshape(total_keys, proj), dvalues.reshape(total_keys, proj)], axis=1
            )
        )
    dquery_all = jnp.stack(dquery_rows, axis=0)
    dkv_all = jnp.stack(dkey_rows, axis=0)
    query_grad = jnp.einsum("rjd,cd->rjc", dquery_all, w_query, precision=HIGH)
    terms = jnp.einsum("rkd,cd->rkc", dkv_all, w_both, precision=HIGH)
    key_pair_grad = lax.psum_scatter(terms, "col", scatter_dimension=1, tiled=True)
    bias_grad = lax.psum_scatter(dscore_sum, ("row", "sub"), scatter_dimension=2, tiled=True)
    return (query_grad, key_pair_grad, bias_grad)


def solution(mesh):
    placed = (
        P(("groups", "row", "sub"), "col", None),
        P(),
        P(),
        P(),
        P("groups", "col", ("row", "sub")),
        P(("groups", "row", "sub"), "col", None),
        P(None, ("groups", "row", "sub"), "col"),
        P(None, ("groups", "row", "sub"), "col"),
    )
    return jax.shard_map(
        on_device,
        mesh=mesh,
        in_specs=placed,
        out_specs=(
            P(("groups", "row", "sub"), "col", None),
            P(("groups", "row", "sub"), "col", None),
            P("groups", "col", ("row", "sub")),
        ),
        check_vma=False,
    )
```

profile of v0, /device:TPU:0, one launch (start us, length us, event | category | flops | bytes accessed | tf_op | source)
XLA Modules:
  0.0 88.9 jit_solution(5323842607077840408)
XLA Ops:
  7.2 0.8 fusion.28
  8.0 1.0 %copy.39 = f32[128,128]{0,1:T(8,128)S(1)} copy(f32[128,128]{1,0:T(8,128)} %param.10) | data formatting | bytes 131072 | tf_op args[2]
  9.1 0.7 copy-done.3
  10.0 0.7 copy-done.1
  10.7 15.6 %all_gather.6 = f32[2,256,128]{2,1,0:T(8,128)S(1)} all-gather(f32[2,64,128]{2,1,0:T(8,128)S(1)} %copy-done.1), channel_id=1, replica_groups=mesh['groups'=2,'col'=4,'row'=2,'sub'=2] {'col'}, dimensions={1}, use_global_device_ids=true | all-gather | bytes 327680 | tf_op jit(solution)/shard_map/all_gather | solution.py:17
  26.8 0.7 copy-done.4
  27.7 5.8 %all_gather.7 = bf16[4,64,256]{1,0,2:T(4,128)(2,1)S(1)} all-gather(bf16[4,64,64]{1,0,2:T(4,128)(2,1)S(1)} %copy.42), channel_id=1, replica_groups=mesh['groups'=2,'col'=4,'row'=2,'sub'=2] {'row','sub'}, dimensions={2}, use_global_device_ids=true | all-gather | bytes 163840 | tf_op jit(solution)/shard_map/all_gather | solution.py:19
  33.6 0.6 convolution_bitcast_fusion
  34.3 0.5 fusion.4
  34.7 0.5 fusion.9
  35.2 0.4 fusion.1
  35.7 0.4 fusion.29
  36.3 1.0 %reshape.29 = f32[256,256]{1,0:T(8,128)} reshape(f32[256,4,64]{2,1,0:T(4,128)S(1)} %bitcast.78) | data formatting | bytes 524288
  37.5 0.3 fusion.31
  38.0 0.3 fusion.30
  38.6 0.3 convolution_multiply_fusion.3
  39.0 1.3 %fusion.10 = f32[2,256,128]{2,1,0:T(8,128)} fusion(f32[1,256,256]{2,1,0:T(8,128)S(1)} %get-tuple-element.18, f32[1,256,256]{2,1,0:T(8,128)S(1)} %get-tuple-element.17, f32[128,128]{0,1:T(8,128)S(1)} %copy.40, f32[128,128]{0,1:T(8,128)S(1)} %copy.39), kind=kOutput, calls=%fused_computation.19 | convolution fusion | flops 201490432 | bytes 917504 | tf_op jit(solution)/shard_map/rkd,cd->rkc/dot_general | solution.py:47
  40.3 0.3 convolution_multiply_fusion.4
  40.7 0.4 convolution_multiply_fusion.5
  41.2 0.9 %fusion.14 = f32[2,64,128]{2,1,0:T(8,128)} fusion(f32[1,64,128]{2,1,0:T(8,128)S(1)} %copy.48, f32[1,64,128]{2,1,0:T(8,128)S(1)} %copy.47, f32[128,128]{1,0:T(8,128)S(1)} %copy-done), kind=kOutput, calls=%fused_computation.26 | convolution fusion | flops 25182208 | bytes 196608 | tf_op jit(solution)/shard_map/rjd,cd->rjc/dot_general | solution.py:46
  42.1 17.1 %reduce-scatter.7.cloned.1.call-done = f32[64,256]{1,0:T(8,128)} async-done(((f32[256,256]{1,0:T(8,128)}), f32[64,256]{1,0:T(8,128)}) %reduce-scatter.7.cloned.1.call-update) | async-done | bytes 65552
  59.2 0.9 %reshape.30 = f32[64,4,64]{2,1,0:T(4,128)S(1)} reshape(f32[64,256]{1,0:T(8,128)} %reduce-scatter.7.cloned.1.call-done) | data formatting | bytes 131072
  60.1 0.8 copy.57
  60.9 21.2 %reduce-scatter.5.cloned.1.call-done = f32[2,64,128]{2,1,0:T(8,128)} async-done(((f32[2,256,128]{2,1,0:T(8,128)}), f32[2,64,128]{2,1,0:T(8,128)}) %reduce-scatter.5.cloned.1.call-update) | async-done | bytes 65552 | tf_op jit(solution)/shard_map/reduce_scatter | solution.py:48
  (34 shorter events, 2.1 us)
Async XLA Ops:
  7.2 19.2 %copy-start = (f32[128,128]{1,0:T(8,128)S(1)}, f32[128,128]{1,0:T(8,128)}, u32[]{:S(2)}) copy-start(f32[128,128]{1,0:T(8,128)} %param.9) | copy-start | bytes 196612
  7.2 0.8 copy-start.5
  7.2 52.0 %reduce-scatter.7.cloned.1.call-start = ((), (), s32[]{:S(2)}) async-start(), calls=%async_computation.3 | async-start | bytes 327680
  8.0 1.0 %copy-start.2 = (f32[128,128]{1,0:T(8,128)S(1)}, f32[128,128]{1,0:T(8,128)}, u32[]{:S(2)}) copy-start(f32[128,128]{1,0:T(8,128)} %param.11) | copy-start | bytes 196612
  9.0 0.8 copy-start.3
  9.8 0.8 copy-start.1
  26.7 0.8 copy-start.4
  37.4 44.6 %reduce-scatter.5.cloned.1.call-start = ((), (), s32[]{:S(2)}) async-start(), calls=%async_computation.2 | async-start | bytes 327680 | tf_op jit(solution)/shard_map/reduce_scatter | solution.py:48
Sparse Core Ops, SparseCore 0:
  37.5 21.5 reduce-scatter.6
  62.0 19.9 reduce-scatter.4
where the time goes:
time: 89.3 us; the launch traced here: 88.9 us
  waiting for transfers between devices  38.3 us (43%)
  blocking collectives  21.4 us (24%)
  between operations  14.3 us (16%)
  local copies, waits for them, and re-layouts  8.2 us (9%)
  matrix products  6.56 us (7%)
    reduce_scatter x1, waiting for transfers between devices, on_device(): lax.psum_scatter(terms, 'col', scatter_dimension=1, tiled=True)  21.2 us
    unnamed x3, waiting for transfers between devices  17.1 us
    all_gather x1, blocking collectives, on_device(): lax.all_gather(pair, 'col', axis=1, tiled=True)  15.6 us
    unnamed x19, local copies, waits for them, and re-layouts  6.37 us
    all_gather x1, blocking collectives, on_device(): lax.all_gather(bias, ('row', 'sub'), axis=2, tiled=True).astype(jnp.float32)  5.78 us
  transfers between devices with their start and end apart: 2, of which 2 were waited for; matrix products, arithmetic and copies ran while one was open for 7% of the time, Pallas kernels for 0%

commit v1 on v0

v1 whole, which is shorter than its diff:
```python
import functools

import jax
import jax.numpy as jnp
from jax import lax
from jax.experimental import pallas as pl
from jax.experimental.pallas import tpu as pltpu
from jax.sharding import PartitionSpec as P

NN = (((1,), (0,)), ((), ()))
NT = (((1,), (1,)), ((), ()))
TN = (((0,), (0,)), ((), ()))


def split(x):
    high = x.astype(jnp.bfloat16)
    return high, (x - high.astype(jnp.float32)).astype(jnp.bfloat16)


def dot3(a, b, dims):
    def one(x, y):
        return lax.dot_general(x, y, dims, preferred_element_type=jnp.float32)

    return one(a[0], b[0]) + one(a[0], b[1]) + one(a[1], b[0])


def attend(where_ref, *refs, count, heads, head_dim):
    blocks = refs[:count]
    biases = refs[count : 2 * count]
    wq_ref, wk_ref, wv_ref, grad_ref, lse_ref, corr_ref = refs[2 * count : 2 * count + 6]
    query_ref, own_ref = refs[2 * count + 6 : 2 * count + 8]
    terms_refs = refs[2 * count + 8 : 3 * count + 7]
    dbias_ref = refs[3 * count + 7]
    bias_scr = refs[3 * count + 8]
    rows, cols, width = blocks[0].shape
    proj = heads * head_dim
    wide = heads * cols
    scale = head_dim ** (-0.5)
    shift = where_ref[0]

    wq = split(wq_ref[...])
    wk = split(wk_ref[...])
    wv = split(wv_ref[...])
    for slot in range(count):
        for head in range(heads):
            bias_scr[slot, :, head * cols : (head + 1) * cols] = biases[slot][head].astype(jnp.float32)

    lane_head = lax.broadcasted_iota(jnp.int32, (cols, wide), 1) // cols

    def widen(ref, row):
        stack = jnp.concatenate([ref[head, row : row + 1, :] for head in range(heads)], axis=0)
        stack = jnp.concatenate([stack, jnp.zeros((8 - heads % 8, cols), jnp.float32)], axis=0)
        turned = stack.T
        out = jnp.broadcast_to(turned[:, 0:1], (cols, wide))
        for head in range(1, heads):
            out = jnp.where(lane_head == head, turned[:, head : head + 1], out)
        return out

    row_head = lax.broadcasted_iota(jnp.int32, (wide, proj), 0) // cols
    chan_head = lax.broadcasted_iota(jnp.int32, (wide, proj), 1) // head_dim
    diag = row_head == chan_head
    fold_mask = lax.broadcasted_iota(jnp.int32, (cols, proj), 1) // head_dim

    def spread(pieces):
        return tuple(
            jnp.where(diag, jnp.concatenate([p] * heads, axis=0), jnp.zeros((), p.dtype)) for p in pieces
        )

    def fold(x):
        out = x[:cols]
        for head in range(1, heads):
            out = jnp.where(fold_mask == head, x[head * cols : (head + 1) * cols], out)
        return out

    own = split(blocks[0][...].reshape(rows * cols, width))
    query = dot3(own, wq, NN) * scale
    qs = [split(query[r * cols : (r + 1) * cols]) for r in range(rows)]
    gs = [split(grad_ref[r]) for r in range(rows)]
    lse = [widen(lse_ref, r) for r in range(rows)]
    corr = [widen(corr_ref, r) for r in range(rows)]
    dquery = [None] * rows
    for slot in range(count):
        piece = own if slot == 0 else split(blocks[slot][...].reshape(rows * cols, width))
        key = dot3(piece, wk, NN)
        val = dot3(piece, wv, NN)
        index = shift ^ slot
        bias = bias_scr[index]
        total = None
        dks = []
        dvs = []
        for r in range(rows):
            kb = spread(split(key[r * cols : (r + 1) * cols]))
            vb = spread(split(val[r * cols : (r + 1) * cols]))
            probs = jnp.exp(dot3(qs[r], kb, NT) + bias - lse[r])
            ds = probs * (dot3(gs[r], vb, NT) - corr[r])
            total = ds if total is None else total + ds
            dsp = split(ds)
            part = dot3(dsp, kb, NN)
            dquery[r] = part if dquery[r] is None else dquery[r] + part
            dks.append(fold(dot3(dsp, qs[r], TN)))
            dvs.append(fold(dot3(split(probs), gs[r], TN)))
        term = dot3(split(jnp.concatenate(dks, axis=0)), wk, NT) + dot3(
            split(jnp.concatenate(dvs, axis=0)), wv, NT
        )
        dest = own_ref if slot == 0 else terms_refs[slot - 1]
        dest[...] = term.reshape(rows, cols, width)
        for head in range(heads):
            dbias_ref[index, head] = total[:, head * cols : (head + 1) * cols]
    dq = jnp.concatenate(dquery, axis=0) * scale
    query_ref[...] = dot3(split(dq), wq, NT).reshape(rows, cols, width)


def combine(*refs, count):
    own_ref, dbias_ref = refs[:2]
    terms = refs[2 : count + 1]
    dbs = refs[count + 1 : 2 * count]
    key_ref, bias_ref = refs[2 * count :]
    total = own_ref[...]
    for ref in terms:
        total = total + ref[...]
    key_ref[...] = total
    total = dbias_ref[0]
    for ref in dbs:
        total = total + ref[...]
    bias_ref[...] = total


def xor_pairs(size, mask):
    return [(i, i ^ mask) for i in range(size)]


def on_device(ncol, nrow, nsub, pair, w_query, w_key, w_value, bias, grad_out, log_total, row_corr):
    rows, cols, width = pair.shape
    heads = log_total.shape[0]
    head_dim = w_query.shape[1] // heads
    nrs = nrow * nsub
    count = ncol
    tile = ("row", "sub")
    blocks = [pair] + [lax.ppermute(pair, "col", xor_pairs(ncol, k)) for k in range(1, ncol)]
    biases = [bias] + [lax.ppermute(bias, tile, xor_pairs(nrs, k)) for k in range(1, nrs)]
    place = lax.axis_index("col") ^ (lax.axis_index("row") * nsub + lax.axis_index("sub"))
    f32 = jnp.float32
    part = jax.ShapeDtypeStruct((rows, cols, width), f32)
    vmem = pl.BlockSpec(memory_space=pltpu.VMEM)
    outs = pl.pallas_call(
        functools.partial(attend, count=count, heads=heads, head_dim=head_dim),
        out_shape=[part] * (count + 1) + [jax.ShapeDtypeStruct((nrs, heads, cols, cols), f32)],
        in_specs=[pl.BlockSpec(memory_space=pltpu.SMEM)] + [vmem] * (2 * count + 6),
        out_specs=[vmem] * (count + 2),
        scratch_shapes=[pltpu.VMEM((nrs, cols, heads * cols), f32)],
        name="attend",
    )(place.reshape(1), *blocks, *biases, w_query, w_key, w_value, grad_out, log_total, row_corr)
    query_grad, own = outs[:2]
    terms = outs[2 : count + 1]
    dbias = outs[count + 1]
    got = [lax.ppermute(terms[k - 1], "col", xor_pairs(ncol, k)) for k in range(1, ncol)]
    dgot = [lax.ppermute(dbias[k], tile, xor_pairs(nrs, k)) for k in range(1, nrs)]
    key_grad, bias_grad = pl.pallas_call(
        functools.partial(combine, count=count),
        out_shape=[part, jax.ShapeDtypeStruct((heads, cols, cols), f32)],
        in_specs=[vmem] * (2 * count),
        out_specs=[vmem] * 2,
        name="combine",
    )(own, dbias, *got, *dgot)
    return query_grad, key_grad, bias_grad


def solution(mesh):
    size = mesh.shape
    placed = (
        P(("groups", "row", "sub"), "col", None),
        P(),
        P(),
        P(),
        P("groups", "col", ("row", "sub")),
        P(("groups", "row", "sub"), "col", None),
        P(None, ("groups", "row", "sub"), "col"),
        P(None, ("groups", "row", "sub"), "col"),
    )
    return jax.shard_map(
        functools.partial(on_device, size["col"], size["row"], size["sub"]),
        mesh=mesh,
        in_specs=placed,
        out_specs=(
            P(("groups", "row", "sub"), "col", None),
            P(("groups", "row", "sub"), "col", None),
            P("groups", "col", ("row", "sub")),
        ),
        check_vma=False,
    )
```

time: 89.3 us -> 36.6 us (0.41)
  waiting for transfers between devices: 38.3 us -> 10.5 us
  blocking collectives: 21.4 us -> 0 us
  starting transfers between devices: 0.08 us -> 14.1 us
  between operations: 14.3 us -> 0.73 us
  Pallas kernels: 0 us -> 8.42 us
  matrix products: 6.56 us -> 0 us
  local copies, waits for them, and re-layouts: 8.2 us -> 2.35 us
    all_gather x2 -> x0, blocking collectives: 21.4 us -> none  [the longest x1 15.6 us: on_device(): lax.all_gather(pair, 'col', axis=1, tiled=True)]
    reduce_scatter x1 -> x0, waiting for transfers between devices: 21.2 us -> none  [on_device(): lax.psum_scatter(terms, 'col', scatter_dimension=1, tiled=True)]
    unnamed x3 -> x0, waiting for transfers between devices: 17.1 us -> none
    ppermute x0 -> x12, starting transfers between devices: none -> 14.1 us  [the longest x3 4.39 us: on_device(): lax.ppermute(pair, 'col', xor_pairs(ncol, k))]
    ppermute x0 -> x12, waiting for transfers between devices: none -> 10.5 us  [the longest x3 3.77 us: on_device(): lax.ppermute(dbias[k], tile, xor_pairs(nrs, k))]
    pallas_call x0 -> x2, Pallas kernels: none -> 8.42 us  [the longest x1 6.51 us: on_device(): pl.pallas_call(functools.partial(attend, count=count, heads=heads, head_d...]
    dot_general x14 -> x0, matrix products: 6.56 us -> none  [the longest x1 1.28 us: on_device(): terms = jnp.einsum('rkd,cd->rkc', dkv_all, w_both, precision=HIGH)]
    unnamed x19 -> x24, local copies, waits for them, and re-layouts: 6.37 us -> 1.29 us
  transfers between devices with their start and end apart: 2 -> 12, of which waited for: 2 -> 6; matrix products, arithmetic and copies ran while one was open for 7% -> 3% of each run, Pallas kernels for 0% -> 0%
where the time goes in v1:
time: 36.6 us; the launch traced here: 36.1 us
  starting transfers between devices  14.1 us (39%)
  waiting for transfers between devices  10.5 us (29%)
  Pallas kernels  8.42 us (23%)
  local copies, waits for them, and re-layouts  2.35 us (6%)
  between operations  0.73 us (2%)
    pallas_call x1, Pallas kernels, on_device(): pl.pallas_call(functools.partial(attend, count=count, heads=heads, head_d...  6.51 us
    ppermute x3, starting transfers between devices, on_device(): lax.ppermute(pair, 'col', xor_pairs(ncol, k))  4.39 us
    ppermute x3, starting transfers between devices, on_device(): lax.ppermute(terms[k - 1], 'col', xor_pairs(ncol, k))  4.38 us
    ppermute x3, waiting for transfers between devices, on_device(): lax.ppermute(dbias[k], tile, xor_pairs(nrs, k))  3.77 us
    ppermute x3, waiting for transfers between devices, on_device(): lax.ppermute(bias, tile, xor_pairs(nrs, k))  3.62 us
    ppermute x3, starting transfers between devices, on_device(): lax.ppermute(bias, tile, xor_pairs(nrs, k))  3.46 us
    ppermute x3, waiting for transfers between devices, on_device(): lax.ppermute(pair, 'col', xor_pairs(ncol, k))  1.97 us
    ppermute x3, starting transfers between devices, on_device(): lax.ppermute(dbias[k], tile, xor_pairs(nrs, k))  1.92 us
  transfers between devices with their start and end apart: 12, of which 6 were waited for; matrix products, arithmetic and copies ran while one was open for 3% of the time, Pallas kernels for 0%

profile of v1, /device:TPU:0, one launch (start us, length us, event | category | flops | bytes accessed | tf_op | source)
XLA Modules:
  0.0 36.1 jit_solution(7638926304240724252)
XLA Ops:
  0.6 3.0 %collective-permute-start.4 = (bf16[4,64,64]{2,1,0:T(8,128)(2,1)}, bf16[4,64,64]{2,1,0:T(8,128)(2,1)S(1)}, u32[]{:S(2)}, u32[]{:S(2)}) collective-permute-start(bf16[4,64,64]{2,1,0:T(8,128)(2,1)} %refs_4_.1), channel_id=1, source_target_pairs={{0,2},{1,3},{2,0},{3,1},{4,6},{5,7},{6,4},{7,5},{8,10},{9,11},{10,... | collective-permute-start | bytes 98312 | tf_op jit(solution)/shard_map/ppermute | solution.py:140
  3.7 2.6 %collective-permute-start.1 = (f32[2,64,128]{2,1,0:T(8,128)}, f32[2,64,128]{2,1,0:T(8,128)S(1)}, u32[]{:S(2)}, u32[]{:S(2)}) collective-permute-start(f32[2,64,128]{2,1,0:T(8,128)} %refs_0_.1), channel_id=1, source_target_pairs={{0,8},{4,12},{8,0},{12,4},{1,9},{5,13},{9,1},{13,5},{2,10},{6,14},... | collective-permute-start | bytes 196616 | tf_op jit(solution)/shard_map/ppermute | solution.py:139
  6.3 1.6 %collective-permute-start = (f32[2,64,128]{2,1,0:T(8,128)}, f32[2,64,128]{2,1,0:T(8,128)S(1)}, u32[]{:S(2)}, u32[]{:S(2)}) collective-permute-start(f32[2,64,128]{2,1,0:T(8,128)} %refs_0_.1), channel_id=1, source_target_pairs={{0,4},{4,0},{8,12},{12,8},{1,5},{5,1},{9,13},{13,9},{2,6},{6,2},{1... | collective-permute-start | bytes 196616 | tf_op jit(solution)/shard_map/ppermute | solution.py:139
  7.8 0.2 collective-permute-start.2
  8.1 0.0 collective-permute-done.4.refs_6_
  8.1 0.4 %collective-permute-start.5 = (bf16[4,64,64]{2,1,0:T(8,128)(2,1)}, bf16[4,64,64]{2,1,0:T(8,128)(2,1)S(1)}, u32[]{:S(2)}, u32[]{:S(2)}) collective-permute-start(bf16[4,64,64]{2,1,0:T(8,128)(2,1)} %refs_4_.1), channel_id=1, source_target_pairs={{0,3},{1,2},{2,1},{3,0},{4,7},{5,6},{6,5},{7,4},{8,11},{9,10},{10,... | collective-permute-start | bytes 98312 | tf_op jit(solution)/shard_map/ppermute | solution.py:140
  8.5 1.0 %collective-permute-done.3.refs_5_ = bf16[4,64,64]{2,1,0:T(8,128)(2,1)S(1)} collective-permute-done((bf16[4,64,64]{2,1,0:T(8,128)(2,1)}, bf16[4,64,64]{2,1,0:T(8,128)(2,1)S(1)}, u32[]{:S(2)}, u32[]{:S(2)}) %collective-permute-start.3) | collective-permute-done | bytes 32800 | tf_op jit(solution)/shard_map/ppermute | solution.py:140
  9.5 2.6 %collective-permute-done.5.refs_7_ = bf16[4,64,64]{2,1,0:T(8,128)(2,1)S(1)} collective-permute-done((bf16[4,64,64]{2,1,0:T(8,128)(2,1)}, bf16[4,64,64]{2,1,0:T(8,128)(2,1)S(1)}, u32[]{:S(2)}, u32[]{:S(2)}) %collective-permute-start.5) | collective-permute-done | bytes 32800 | tf_op jit(solution)/shard_map/ppermute | solution.py:140
  12.1 0.0 copy-start.8
  12.1 2.0 %collective-permute-done.2.refs_3_ = f32[2,64,128]{2,1,0:T(8,128)S(1)} collective-permute-done((f32[2,64,128]{2,1,0:T(8,128)}, f32[2,64,128]{2,1,0:T(8,128)S(1)}, u32[]{:S(2)}, u32[]{:S(2)}) %collective-permute-start.2) | collective-permute-done | bytes 65568 | tf_op jit(solution)/shard_map/ppermute | solution.py:139
  14.1 0.6 %copy-done.9 = f32[2,64,128]{2,1,0:T(8,128)} copy-done((f32[2,64,128]{2,1,0:T(8,128)}, f32[2,64,128]{2,1,0:T(8,128)S(1)}, u32[]{:S(2)}) %copy-start.9) | copy-done | bytes 65560
  14.7 6.5 %attend.1 = (f32[2,64,128]{2,1,0:T(8,128)}, f32[2,64,128]{2,1,0:T(8,128)}, f32[2,64,128]{2,1,0:T(8,128)}, f32[2,64,128]{2,1,0:T(8,128)}, f32[2,64,128]{2,1,0:T(8,128)}, /*index=5*/f32[4,4,64,64]{3,2,1,0:T(8,128)}) custom-call(s32[1]{0:T(128)} %bitcast.where_ref, f32[2,64,128]{2,1,0:T(8,128)} %refs_0_.1, f32[2,64,128]{2,1,0:T(8,128)} %copy-done.8, ...), custom_call_target="tpu_custom_call" | custom-call | tf_op jit(solution)/shard_map/attend/pallas_call | solution.py:145
  21.2 2.2 %collective-permute-start.7 = (f32[2,64,128]{2,1,0:T(8,128)}, f32[2,64,128]{2,1,0:T(8,128)S(1)}, u32[]{:S(2)}, u32[]{:S(2)}) collective-permute-start(f32[2,64,128]{2,1,0:T(8,128)} %get-tuple-element.15), channel_id=1, source_target_pairs={{0,8},{4,12},{8,0},{12,4},{1,9},{5,13},{9,1},{13,5},{2,10},{6,14},... | collective-permute-start | bytes 196616 | tf_op jit(solution)/shard_map/ppermute | solution.py:156
  23.5 2.2 %collective-permute-start.8 = (f32[2,64,128]{2,1,0:T(8,128)}, f32[2,64,128]{2,1,0:T(8,128)S(1)}, u32[]{:S(2)}, u32[]{:S(2)}) collective-permute-start(f32[2,64,128]{2,1,0:T(8,128)} %get-tuple-element.16), channel_id=1, source_target_pairs={{0,12},{4,8},{8,4},{12,0},{1,13},{5,9},{9,5},{13,1},{2,14},{6,10},... | collective-permute-start | bytes 196616 | tf_op jit(solution)/shard_map/ppermute | solution.py:156
  25.6 1.1 %slice_bitcast_fusion = (f32[4,64,64]{2,1,0:T(8,128)S(1)}, f32[4,64,64]{2,1,0:T(8,128)S(1)}, f32[4,64,64]{2,1,0:T(8,128)S(1)}) fusion(f32[4,4,64,64]{3,2,1,0:T(8,128)} %get-tuple-element.13.refs_1_), kind=kLoop, calls=%fused_computation | loop fusion | bytes 393216 | tf_op jit(solution)/shard_map/squeeze | solution.py:157
  26.7 0.1 collective-permute-start.11
  26.8 0.6 %collective-permute-start.10 = (f32[4,64,64]{2,1,0:T(8,128)S(1)}, f32[4,64,64]{2,1,0:T(8,128)S(1)}, u32[]{:S(2)}, u32[]{:S(2)}) collective-permute-start(f32[4,64,64]{2,1,0:T(8,128)S(1)} %get-tuple-element.20), channel_id=1, source_target_pairs={{0,2},{1,3},{2,0},{3,1},{4,6},{5,7},{6,4},{7,5},{8,10},{9,11},{10,... | collective-permute-start | bytes 196616 | tf_op jit(solution)/shard_map/ppermute | solution.py:157
  27.4 1.3 %collective-permute-start.9 = (f32[4,64,64]{2,1,0:T(8,128)S(1)}, f32[4,64,64]{2,1,0:T(8,128)S(1)}, u32[]{:S(2)}, u32[]{:S(2)}) collective-permute-start(f32[4,64,64]{2,1,0:T(8,128)S(1)} %get-tuple-element.21), channel_id=1, source_target_pairs={{0,1},{1,0},{2,3},{3,2},{4,5},{5,4},{6,7},{7,6},{8,9},{9,8},{10,11... | collective-permute-start | bytes 196616 | tf_op jit(solution)/shard_map/ppermute | solution.py:157
  28.6 1.1 %collective-permute-done.8.refs_4_ = f32[2,64,128]{2,1,0:T(8,128)S(1)} collective-permute-done((f32[2,64,128]{2,1,0:T(8,128)}, f32[2,64,128]{2,1,0:T(8,128)S(1)}, u32[]{:S(2)}, u32[]{:S(2)}) %collective-permute-start.8) | collective-permute-done | bytes 65568 | tf_op jit(solution)/shard_map/ppermute | solution.py:156
  29.7 2.8 %collective-permute-done.11.refs_7_ = f32[4,64,64]{2,1,0:T(8,128)S(1)} collective-permute-done((f32[4,64,64]{2,1,0:T(8,128)S(1)}, f32[4,64,64]{2,1,0:T(8,128)S(1)}, u32[]{:S(2)}, u32[]{:S(2)}) %collective-permute-start.11) | collective-permute-done | bytes 65568 | tf_op jit(solution)/shard_map/ppermute | solution.py:157
  32.5 1.0 %collective-permute-done.10.refs_6_ = f32[4,64,64]{2,1,0:T(8,128)S(1)} collective-permute-done((f32[4,64,64]{2,1,0:T(8,128)S(1)}, f32[4,64,64]{2,1,0:T(8,128)S(1)}, u32[]{:S(2)}, u32[]{:S(2)}) %collective-permute-start.10) | collective-permute-done | bytes 65568 | tf_op jit(solution)/shard_map/ppermute | solution.py:157
  33.6 0.6 %copy-done.1 = f32[4,64,64]{2,1,0:T(8,128)} copy-done((f32[4,64,64]{2,1,0:T(8,128)}, f32[4,64,64]{2,1,0:T(8,128)S(1)}, u32[]{:S(2)}) %copy-start.1) | copy-done | bytes 65560
  34.2 0.1 copy-done.2
  34.2 1.9 %combine.1 = (f32[2,64,128]{2,1,0:T(8,128)}, f32[4,64,64]{2,1,0:T(8,128)}) custom-call(f32[2,64,128]{2,1,0:T(8,128)} %get-tuple-element.12.refs_0_, f32[4,4,64,64]{3,2,1,0:T(8,128)} %get-tuple-element.13.refs_1_, f32[2,64,128]{2,1,0:T(8,128)} %copy-done.3, f32[2,64,128]{2,1,0:T(8,128)} %copy-done.4, f32[2,64,128]{2,1,0:T(8,128)} %copy-done.5, ...), custom_call_target="tpu_custom_call" | custom-call | tf_op jit(solution)/shard_map/combine/pallas_call | solution.py:158
  (27 shorter events, 0.1 us)
Async XLA Ops:
  0.6 7.4 %collective-permute-start.4 = (bf16[4,64,64]{2,1,0:T(8,128)(2,1)}, bf16[4,64,64]{2,1,0:T(8,128)(2,1)S(1)}, u32[]{:S(2)}, u32[]{:S(2)}) collective-permute-start(bf16[4,64,64]{2,1,0:T(8,128)(2,1)} %refs_4_.1), channel_id=1, source_target_pairs={{0,2},{1,3},{2,0},{3,1},{4,6},{5,7},{6,4},{7,5},{8,10},{9,11},{10,... | collective-permute-start | bytes 98312 | tf_op jit(solution)/shard_map/ppermute | solution.py:140
  3.7 8.5 %collective-permute-start.1 = (f32[2,64,128]{2,1,0:T(8,128)}, f32[2,64,128]{2,1,0:T(8,128)S(1)}, u32[]{:S(2)}, u32[]{:S(2)}) collective-permute-start(f32[2,64,128]{2,1,0:T(8,128)} %refs_0_.1), channel_id=1, source_target_pairs={{0,8},{4,12},{8,0},{12,4},{1,9},{5,13},{9,1},{13,5},{2,10},{6,14},... | collective-permute-start | bytes 196616 | tf_op jit(solution)/shard_map/ppermute | solution.py:139
  6.3 5.9 %collective-permute-start = (f32[2,64,128]{2,1,0:T(8,128)}, f32[2,64,128]{2,1,0:T(8,128)S(1)}, u32[]{:S(2)}, u32[]{:S(2)}) collective-permute-start(f32[2,64,128]{2,1,0:T(8,128)} %refs_0_.1), channel_id=1, source_target_pairs={{0,4},{4,0},{8,12},{12,8},{1,5},{5,1},{9,13},{13,9},{2,6},{6,2},{1... | collective-permute-start | bytes 196616 | tf_op jit(solution)/shard_map/ppermute | solution.py:139
  7.8 6.3 %collective-permute-start.2 = (f32[2,64,128]{2,1,0:T(8,128)}, f32[2,64,128]{2,1,0:T(8,128)S(1)}, u32[]{:S(2)}, u32[]{:S(2)}) collective-permute-start(f32[2,64,128]{2,1,0:T(8,128)} %refs_0_.1), channel_id=1, source_target_pairs={{0,12},{4,8},{8,4},{12,0},{1,13},{5,9},{9,5},{13,1},{2,14},{6,10},... | collective-permute-start | bytes 196616 | tf_op jit(solution)/shard_map/ppermute | solution.py:139
  8.1 1.5 %collective-permute-start.3 = (bf16[4,64,64]{2,1,0:T(8,128)(2,1)}, bf16[4,64,64]{2,1,0:T(8,128)(2,1)S(1)}, u32[]{:S(2)}, u32[]{:S(2)}) collective-permute-start(bf16[4,64,64]{2,1,0:T(8,128)(2,1)} %refs_4_.1), channel_id=1, source_target_pairs={{0,1},{1,0},{2,3},{3,2},{4,5},{5,4},{6,7},{7,6},{8,9},{9,8},{10,11... | collective-permute-start | bytes 98312 | tf_op jit(solution)/shard_map/ppermute | solution.py:140
  8.1 6.1 %copy-start.6 = (bf16[4,64,64]{2,1,0:T(8,128)(2,1)}, bf16[4,64,64]{2,1,0:T(8,128)(2,1)S(1)}, u32[]{:S(2)}) copy-start(bf16[4,64,64]{2,1,0:T(8,128)(2,1)S(1)} %collective-permute-done.4.refs_6_) | copy-start | bytes 98308
  8.1 4.0 %collective-permute-start.5 = (bf16[4,64,64]{2,1,0:T(8,128)(2,1)}, bf16[4,64,64]{2,1,0:T(8,128)(2,1)S(1)}, u32[]{:S(2)}, u32[]{:S(2)}) collective-permute-start(bf16[4,64,64]{2,1,0:T(8,128)(2,1)} %refs_4_.1), channel_id=1, source_target_pairs={{0,3},{1,2},{2,1},{3,0},{4,7},{5,6},{6,5},{7,4},{8,11},{9,10},{10,... | collective-permute-start | bytes 98312 | tf_op jit(solution)/shard_map/ppermute | solution.py:140
  9.5 4.6 %copy-start.10 = (bf16[4,64,64]{2,1,0:T(8,128)(2,1)}, bf16[4,64,64]{2,1,0:T(8,128)(2,1)S(1)}, u32[]{:S(2)}) copy-start(bf16[4,64,64]{2,1,0:T(8,128)(2,1)S(1)} %collective-permute-done.3.refs_5_) | copy-start | bytes 98308
  12.1 2.0 %copy-start.11 = (bf16[4,64,64]{2,1,0:T(8,128)(2,1)}, bf16[4,64,64]{2,1,0:T(8,128)(2,1)S(1)}, u32[]{:S(2)}) copy-start(bf16[4,64,64]{2,1,0:T(8,128)(2,1)S(1)} %collective-permute-done.5.refs_7_) | copy-start | bytes 98308
  12.1 2.0 %copy-start.7 = (f32[2,64,128]{2,1,0:T(8,128)}, f32[2,64,128]{2,1,0:T(8,128)S(1)}, u32[]{:S(2)}) copy-start(f32[2,64,128]{2,1,0:T(8,128)S(1)} %collective-permute-done.1.refs_2_) | copy-start | bytes 196612
  12.1 2.0 %copy-start.8 = (f32[2,64,128]{2,1,0:T(8,128)}, f32[2,64,128]{2,1,0:T(8,128)S(1)}, u32[]{:S(2)}) copy-start(f32[2,64,128]{2,1,0:T(8,128)S(1)} %collective-permute-done.refs_1_) | copy-start | bytes 196612
  14.1 0.6 %copy-start.9 = (f32[2,64,128]{2,1,0:T(8,128)}, f32[2,64,128]{2,1,0:T(8,128)S(1)}, u32[]{:S(2)}) copy-start(f32[2,64,128]{2,1,0:T(8,128)S(1)} %collective-permute-done.2.refs_3_) | copy-start | bytes 196612
  21.2 6.1 %collective-permute-start.6 = (f32[2,64,128]{2,1,0:T(8,128)}, f32[2,64,128]{2,1,0:T(8,128)S(1)}, u32[]{:S(2)}, u32[]{:S(2)}) collective-permute-start(f32[2,64,128]{2,1,0:T(8,128)} %get-tuple-element.14), channel_id=1, source_target_pairs={{0,4},{4,0},{8,12},{12,8},{1,5},{5,1},{9,13},{13,9},{2,6},{6,2},{1... | collective-permute-start | bytes 196616 | tf_op jit(solution)/shard_map/ppermute | solution.py:156
  21.2 7.4 %collective-permute-start.7 = (f32[2,64,128]{2,1,0:T(8,128)}, f32[2,64,128]{2,1,0:T(8,128)S(1)}, u32[]{:S(2)}, u32[]{:S(2)}) collective-permute-start(f32[2,64,128]{2,1,0:T(8,128)} %get-tuple-element.15), channel_id=1, source_target_pairs={{0,8},{4,12},{8,0},{12,4},{1,9},{5,13},{9,1},{13,5},{2,10},{6,14},... | collective-permute-start | bytes 196616 | tf_op jit(solution)/shard_map/ppermute | solution.py:156
  23.5 6.3 %collective-permute-start.8 = (f32[2,64,128]{2,1,0:T(8,128)}, f32[2,64,128]{2,1,0:T(8,128)S(1)}, u32[]{:S(2)}, u32[]{:S(2)}) collective-permute-start(f32[2,64,128]{2,1,0:T(8,128)} %get-tuple-element.16), channel_id=1, source_target_pairs={{0,12},{4,8},{8,4},{12,0},{1,13},{5,9},{9,5},{13,1},{2,14},{6,10},... | collective-permute-start | bytes 196616 | tf_op jit(solution)/shard_map/ppermute | solution.py:156
  26.7 5.9 %collective-permute-start.11 = (f32[4,64,64]{2,1,0:T(8,128)S(1)}, f32[4,64,64]{2,1,0:T(8,128)S(1)}, u32[]{:S(2)}, u32[]{:S(2)}) collective-permute-start(f32[4,64,64]{2,1,0:T(8,128)S(1)} %get-tuple-element.19), channel_id=1, source_target_pairs={{0,3},{1,2},{2,1},{3,0},{4,7},{5,6},{6,5},{7,4},{8,11},{9,10},{10,... | collective-permute-start | bytes 196616 | tf_op jit(solution)/shard_map/ppermute | solution.py:157
  26.8 6.8 %collective-permute-start.10 = (f32[4,64,64]{2,1,0:T(8,128)S(1)}, f32[4,64,64]{2,1,0:T(8,128)S(1)}, u32[]{:S(2)}, u32[]{:S(2)}) collective-permute-start(f32[4,64,64]{2,1,0:T(8,128)S(1)} %get-tuple-element.20), channel_id=1, source_target_pairs={{0,2},{1,3},{2,0},{3,1},{4,6},{5,7},{6,4},{7,5},{8,10},{9,11},{10,... | collective-permute-start | bytes 196616 | tf_op jit(solution)/shard_map/ppermute | solution.py:157
  27.4 6.2 %copy-start.3 = (f32[2,64,128]{2,1,0:T(8,128)}, f32[2,64,128]{2,1,0:T(8,128)S(1)}, u32[]{:S(2)}) copy-start(f32[2,64,128]{2,1,0:T(8,128)S(1)} %collective-permute-done.6.refs_2_) | copy-start | bytes 196612
  27.4 6.2 %collective-permute-start.9 = (f32[4,64,64]{2,1,0:T(8,128)S(1)}, f32[4,64,64]{2,1,0:T(8,128)S(1)}, u32[]{:S(2)}, u32[]{:S(2)}) collective-permute-start(f32[4,64,64]{2,1,0:T(8,128)S(1)} %get-tuple-element.21), channel_id=1, source_target_pairs={{0,1},{1,0},{2,3},{3,2},{4,5},{5,4},{6,7},{7,6},{8,9},{9,8},{10,11... | collective-permute-start | bytes 196616 | tf_op jit(solution)/shard_map/ppermute | solution.py:157
  28.6 4.9 %copy-start.4 = (f32[2,64,128]{2,1,0:T(8,128)}, f32[2,64,128]{2,1,0:T(8,128)S(1)}, u32[]{:S(2)}) copy-start(f32[2,64,128]{2,1,0:T(8,128)S(1)} %collective-permute-done.7.refs_3_) | copy-start | bytes 196612
  29.7 3.8 %copy-start.5 = (f32[2,64,128]{2,1,0:T(8,128)}, f32[2,64,128]{2,1,0:T(8,128)S(1)}, u32[]{:S(2)}) copy-start(f32[2,64,128]{2,1,0:T(8,128)S(1)} %collective-permute-done.8.refs_4_) | copy-start | bytes 196612
  32.5 1.0 %copy-start = (f32[4,64,64]{2,1,0:T(8,128)}, f32[4,64,64]{2,1,0:T(8,128)S(1)}, u32[]{:S(2)}) copy-start(f32[4,64,64]{2,1,0:T(8,128)S(1)} %collective-permute-done.11.refs_7_) | copy-start | bytes 196612
  33.5 0.7 %copy-start.1 = (f32[4,64,64]{2,1,0:T(8,128)}, f32[4,64,64]{2,1,0:T(8,128)S(1)}, u32[]{:S(2)}) copy-start(f32[4,64,64]{2,1,0:T(8,128)S(1)} %collective-permute-done.10.refs_6_) | copy-start | bytes 196612
  33.5 0.7 %copy-start.2 = (f32[4,64,64]{2,1,0:T(8,128)}, f32[4,64,64]{2,1,0:T(8,128)S(1)}, u32[]{:S(2)}) copy-start(f32[4,64,64]{2,1,0:T(8,128)S(1)} %collective-permute-done.9.refs_5_) | copy-start | bytes 196612

commit v2 on v0

v2 whole, which is shorter than its diff:
```python
import functools

import jax
import jax.numpy as jnp
from jax import lax
from jax.experimental import pallas as pl
from jax.experimental.pallas import tpu as pltpu
from jax.sharding import PartitionSpec as P

NN = (((1,), (0,)), ((), ()))
NT = (((1,), (1,)), ((), ()))
TN = (((0,), (0,)), ((), ()))
F32 = jnp.float32
BF16 = jnp.bfloat16


def split(x):
    high = x.astype(BF16)
    return high, (x - high.astype(F32)).astype(BF16)


def dot3(a, b, dims):
    def one(x, y):
        return lax.dot_general(x, y, dims, preferred_element_type=F32)

    return one(a[0], b[0]) + one(a[0], b[1]) + one(a[1], b[0])


def pair_of(ref):
    return ref[0], ref[1]


def store(ref, pieces):
    ref[0] = pieces[0]
    ref[1] = pieces[1]


class Shape:
    def __init__(self, rows, cols, width, heads, head_dim):
        self.rows, self.cols, self.width = rows, cols, width
        self.heads, self.head_dim = heads, head_dim
        self.proj, self.wide, self.flat = heads * head_dim, heads * cols, rows * cols


def prep(pair_ref, wq_ref, wk_ref, wv_ref, grad_ref, lse_ref, corr_ref, *outs, s):
    q_out, g_out, wq_out, wk_out, wv_out, lse_out, corr_out, key_out, val_out = outs
    wq = split(wq_ref[...])
    wk = split(wk_ref[...])
    wv = split(wv_ref[...])
    store(wq_out, wq)
    store(wk_out, wk)
    store(wv_out, wv)
    own = split(pair_ref[...].reshape(s.flat, s.width))
    store(q_out, split(dot3(own, wq, NN) * (s.head_dim ** (-0.5))))
    store(key_out, split(dot3(own, wk, NN)))
    store(val_out, split(dot3(own, wv, NN)))
    store(g_out, split(grad_ref[...].reshape(s.flat, s.proj)))
    lane_head = lax.broadcasted_iota(jnp.int32, (s.cols, s.wide), 1) // s.cols

    def widen(ref, row):
        stack = jnp.concatenate([ref[head, row : row + 1, :] for head in range(s.heads)], axis=0)
        stack = jnp.concatenate([stack, jnp.zeros((8 - s.heads % 8, s.cols), F32)], axis=0)
        turned = stack.T
        out = jnp.broadcast_to(turned[:, 0:1], (s.cols, s.wide))
        for head in range(1, s.heads):
            out = jnp.where(lane_head == head, turned[:, head : head + 1], out)
        return out

    for r in range(s.rows):
        lse_out[r] = widen(lse_ref, r)
        corr_out[r] = widen(corr_ref, r)


def process(s, refs, slots, bias_of, dquery):
    q_ref, g_ref, wk_ref, wv_ref, lse_ref, corr_ref = refs
    row_head = lax.broadcasted_iota(jnp.int32, (s.wide, s.proj), 0) // s.cols
    chan_head = lax.broadcasted_iota(jnp.int32, (s.wide, s.proj), 1) // s.head_dim
    diag = row_head == chan_head
    fold_mask = lax.broadcasted_iota(jnp.int32, (s.cols, s.proj), 1) // s.head_dim

    def spread(pieces):
        return tuple(
            jnp.where(diag, jnp.concatenate([p] * s.heads, axis=0), jnp.zeros((), p.dtype)) for p in pieces
        )

    def fold(x):
        out = x[: s.cols]
        for head in range(1, s.heads):
            out = jnp.where(fold_mask == head, x[head * s.cols : (head + 1) * s.cols], out)
        return out

    def rows_of(pieces, r):
        return tuple(p[r * s.cols : (r + 1) * s.cols] for p in pieces)

    wk = pair_of(wk_ref)
    wv = pair_of(wv_ref)
    query = pair_of(q_ref)
    grads = pair_of(g_ref)
    for slot, keyval in slots:
        key, val = keyval(wk, wv)
        bias = bias_of(slot)
        total = None
        dks = []
        dvs = []
        for r in range(s.rows):
            qs = rows_of(query, r)
            gs = rows_of(grads, r)
            kb = spread(rows_of(key, r))
            vb = spread(rows_of(val, r))
            probs = jnp.exp(dot3(qs, kb, NT) + bias - lse_ref[r])
            ds = probs * (dot3(gs, vb, NT) - corr_ref[r])
            total = ds if total is None else total + ds
            dsp = split(ds)
            part = dot3(dsp, kb, NN)
            dquery[r] = part if dquery[r] is None else dquery[r] + part
            dks.append(fold(dot3(dsp, qs, TN)))
            dvs.append(fold(dot3(split(probs), gs, TN)))
        term = dot3(split(jnp.concatenate(dks, axis=0)), wk, NT) + dot3(
            split(jnp.concatenate(dvs, axis=0)), wv, NT
        )
        yield slot, term.reshape(s.rows, s.cols, s.width), total


def from_block(s, ref):
    def keyval(wk, wv):
        piece = split(ref[...].reshape(s.flat, s.width))
        return split(dot3(piece, wk, NN)), split(dot3(piece, wv, NN))

    return keyval


def near(where_ref, key_ref, val_ref, *refs, s, slots, nrs):
    common = refs[:6]
    blocks = refs[6 : 5 + slots]
    biases = refs[5 + slots : 5 + slots + nrs]
    bias_out, dq_out, *outs = refs[5 + slots + nrs :]
    terms, totals = outs[:slots], outs[slots:]
    for m in range(nrs):
        for head in range(s.heads):
            bias_out[m, :, head * s.cols : (head + 1) * s.cols] = biases[m][head].astype(F32)
    shift = where_ref[0]
    work = [(0, lambda wk, wv: (pair_of(key_ref), pair_of(val_ref)))]
    work += [(k, from_block(s, blocks[k - 1])) for k in range(1, slots)]
    dquery = [None] * s.rows
    for slot, term, total in process(s, common, work, lambda k: bias_out[shift ^ k], dquery):
        terms[slot][...] = term
        totals[slot][...] = total
    for r in range(s.rows):
        dq_out[r] = dquery[r]


def far(where_ref, bias_ref, dq_ref, *refs, s, done, count):
    common = refs[:6]
    totals = refs[6 : 6 + done]
    left = count - done
    blocks = refs[6 + done : 6 + done + left]
    dq_out, *outs = refs[6 + done + left : -1]
    spot = refs[-1]
    terms, dbs = outs[:left], outs[left:]
    shift = where_ref[0]
    for k in range(done):
        spot[shift ^ k] = totals[k][...]
    work = [(done + k, from_block(s, blocks[k])) for k in range(left)]
    dquery = [dq_ref[r] for r in range(s.rows)]
    for slot, term, total in process(s, common, work, lambda k: bias_ref[shift ^ k], dquery):
        terms[slot - done][...] = term
        spot[shift ^ slot] = total
    for r in range(s.rows):
        dq_out[r] = dquery[r]
    for m, ref in enumerate(dbs):
        for head in range(s.heads):
            ref[head] = spot[m, :, head * s.cols : (head + 1) * s.cols]


def tail(dq_ref, wq_ref, out_ref, *, s):
    dq = dq_ref[...].reshape(s.flat, s.proj) * (s.head_dim ** (-0.5))
    out_ref[...] = dot3(split(dq), pair_of(wq_ref), NT).reshape(s.rows, s.cols, s.width)


def add_up(*refs):
    total = refs[0][...]
    for ref in refs[1:-1]:
        total = total + ref[...]
    refs[-1][...] = total


def xor_pairs(size, mask):
    return [(i, i ^ mask) for i in range(size)]


def here(x):
    return pltpu.with_memory_space_constraint(x, pltpu.VMEM)


def call(body, outs, args, scratch=(), scalar=False):
    vmem = pl.BlockSpec(memory_space=pltpu.VMEM)
    specs = [vmem] * len(args)
    if scalar:
        specs[0] = pl.BlockSpec(memory_space=pltpu.SMEM)
    return pl.pallas_call(
        body,
        out_shape=outs,
        in_specs=specs,
        out_specs=[vmem] * len(outs),
        scratch_shapes=list(scratch),
        compiler_params=pltpu.CompilerParams(vmem_limit_bytes=16 << 20),
    )(*args)


NEAR = 2


def on_device(ncol, nrow, nsub, pair, w_query, w_key, w_value, bias, grad_out, log_total, row_corr):
    rows, cols, width = pair.shape
    heads = log_total.shape[0]
    s = Shape(rows, cols, width, heads, w_query.shape[1] // heads)
    nrs = nrow * nsub
    count = ncol
    tile = ("row", "sub")

    def move(x, axis, size, mask):
        return lax.ppermute(x, axis, xor_pairs(size, mask))

    part = jax.ShapeDtypeStruct((rows, cols, width), F32)
    vpart = pltpu.VMEM((rows, cols, width), F32)
    blocks = [here(move(pair, "col", ncol, k)) for k in range(1, ncol)]
    biases = [bias] + [here(move(bias, tile, nrs, k)) for k in range(1, nrs)]
    place = lax.axis_index("col") ^ (lax.axis_index("row") * nsub + lax.axis_index("sub"))
    place = place.reshape(1)
    two = pltpu.VMEM((2, s.flat, s.proj), BF16)
    wtwo = pltpu.VMEM((2, width, s.proj), BF16)
    wide = pltpu.VMEM((rows, cols, s.wide), F32)
    q, g, wq, wk, wv, lse, corr, key, val = map(
        here,
        call(
            functools.partial(prep, s=s),
            [two, two, wtwo, wtwo, wtwo, wide, wide, two, two],
            [pair, w_query, w_key, w_value, grad_out, log_total, row_corr],
        ),
    )
    common = [q, g, wk, wv, lse, corr]
    total = pltpu.VMEM((cols, s.wide), F32)
    dq_shape = pltpu.VMEM((rows, cols, s.proj), F32)
    bias_wide, dq, *rest = call(
        functools.partial(near, s=s, slots=NEAR, nrs=nrs),
        [pltpu.VMEM((nrs, cols, s.wide), F32), dq_shape] + [vpart] * NEAR + [total] * NEAR,
        [place, key, val, *common, *blocks[: NEAR - 1], *biases],
        scalar=True,
    )
    terms, totals = rest[:NEAR], rest[NEAR:]
    dbs = [pltpu.VMEM((heads, cols, cols), F32)] * nrs
    dq, *rest = call(
        functools.partial(far, s=s, done=NEAR, count=count),
        [dq_shape] + [vpart] * (count - NEAR) + dbs,
        [place, here(bias_wide), here(dq), *common, *map(here, totals), *blocks[NEAR - 1 :]],
        scratch=[pltpu.VMEM((nrs, cols, s.wide), F32)],
        scalar=True,
    )
    terms = terms + rest[: count - NEAR]
    dbias = rest[count - NEAR :]
    got = [here(move(terms[k], "col", ncol, k)) for k in range(1, ncol)]
    dgot = [here(move(dbias[k], tile, nrs, k)) for k in range(1, nrs)]
    (query_grad,) = call(functools.partial(tail, s=s), [part], [here(dq), wq])
    (key_grad,) = call(add_up, [part], [here(terms[0]), *got])
    (bias_grad,) = call(
        add_up, [jax.ShapeDtypeStruct((heads, cols, cols), F32)], [here(dbias[0]), *dgot]
    )
    return query_grad, key_grad, bias_grad


def solution(mesh):
    size = mesh.shape
    placed = (
        P(("groups", "row", "sub"), "col", None),
        P(),
        P(),
        P(),
        P("groups", "col", ("row", "sub")),
        P(("groups", "row", "sub"), "col", None),
        P(None, ("groups", "row", "sub"), "col"),
        P(None, ("groups", "row", "sub"), "col"),
    )
    return jax.shard_map(
        functools.partial(on_device, size["col"], size["row"], size["sub"]),
        mesh=mesh,
        in_specs=placed,
        out_specs=(
            P(("groups", "row", "sub"), "col", None),
            P(("groups", "row", "sub"), "col", None),
            P("groups", "col", ("row", "sub")),
        ),
        check_vma=False,
    )
```

time: 89.3 us -> 32.9 us (0.37)
  waiting for transfers between devices: 38.3 us -> 5.42 us
  blocking collectives: 21.4 us -> 0 us
  between operations: 14.3 us -> 0.72 us
  starting transfers between devices: 0.08 us -> 13.6 us
  Pallas kernels: 0 us -> 7.4 us
  matrix products: 6.56 us -> 0 us
  local copies, waits for them, and re-layouts: 8.2 us -> 5.32 us
    all_gather x2 -> x0, blocking collectives: 21.4 us -> none  [the longest x1 15.6 us: on_device(): lax.all_gather(pair, 'col', axis=1, tiled=True)]
    reduce_scatter x1 -> x0, waiting for transfers between devices: 21.2 us -> none  [on_device(): lax.psum_scatter(terms, 'col', scatter_dimension=1, tiled=True)]
    unnamed x3 -> x0, waiting for transfers between devices: 17.1 us -> none
    ppermute x0 -> x12, starting transfers between devices: none -> 13.6 us  [move(): return lax.ppermute(x, axis, xor_pairs(size, mask))]
    pallas_call x0 -> x6, Pallas kernels: none -> 7.4 us  [call(): pl.pallas_call(body, out_shape=outs, in_specs=specs, out_specs=[vmem] * l...]
    dot_general x14 -> x0, matrix products: 6.56 us -> none  [the longest x1 1.28 us: on_device(): terms = jnp.einsum('rkd,cd->rkc', dkv_all, w_both, precision=HIGH)]
    ppermute x0 -> x12, waiting for transfers between devices: none -> 5.42 us  [move(): return lax.ppermute(x, axis, xor_pairs(size, mask))]
    slice x9 -> x0, local copies, waits for them, and re-layouts: 1.19 us -> none  [the longest x1 0.77 us: on_device(): probs = jnp.exp(scores - log_total[:, index, :, None])]
  transfers between devices with their start and end apart: 2 -> 12, of which waited for: 2 -> 5; matrix products, arithmetic and copies ran while one was open for 7% -> 0% of each run, Pallas kernels for 0% -> 13%
where the time goes in v2:
time: 32.9 us; the launch traced here: 32.4 us
  starting transfers between devices  13.6 us (41%)
  Pallas kernels  7.4 us (22%)
  waiting for transfers between devices  5.42 us (16%)
  local copies, waits for them, and re-layouts  5.32 us (16%)
  between operations  0.72 us (2%)
    ppermute x12, starting transfers between devices, move(): return lax.ppermute(x, axis, xor_pairs(size, mask))  13.6 us
    pallas_call x6, Pallas kernels, call(): pl.pallas_call(body, out_shape=outs, in_specs=specs, out_specs=[vmem] * l...  7.4 us
    ppermute x12, waiting for transfers between devices, move(): return lax.ppermute(x, axis, xor_pairs(size, mask))  5.42 us
    unnamed x16, local copies, waits for them, and re-layouts  5.32 us
  transfers between devices with their start and end apart: 12, of which 5 were waited for; matrix products, arithmetic and copies ran while one was open for 0% of the time, Pallas kernels for 13%

profile of v2, /device:TPU:0, one launch (start us, length us, event | category | flops | bytes accessed | tf_op | source)
XLA Modules:
  0.0 32.4 jit_solution(11444883612173855882)
XLA Ops:
  0.6 3.0 %collective-permute-start.2 = (bf16[4,64,64]{2,1,0:T(8,128)(2,1)}, bf16[4,64,64]{2,1,0:T(8,128)(2,1)S(1)}, u32[]{:S(2)}, u32[]{:S(2)}) collective-permute-start(bf16[4,64,64]{2,1,0:T(8,128)(2,1)} %refs_7_.1), channel_id=1, source_target_pairs={{0,2},{1,3},{2,0},{3,1},{4,6},{5,7},{6,4},{7,5},{8,10},{9,11},{10,... | collective-permute-start | bytes 98312 | tf_op jit(solution)/shard_map/ppermute | solution.py:222
  3.7 1.6 %collective-permute-start = (f32[2,64,128]{2,1,0:T(8,128)}, f32[2,64,128]{2,1,0:T(8,128)S(1)}, u32[]{:S(2)}, u32[]{:S(2)}) collective-permute-start(f32[2,64,128]{2,1,0:T(8,128)} %pair_ref.1), channel_id=1, source_target_pairs={{0,4},{4,0},{8,12},{12,8},{1,5},{5,1},{9,13},{13,9},{2,6},{6,2},{1... | collective-permute-start | bytes 196616 | tf_op jit(solution)/shard_map/ppermute | solution.py:222
  5.2 2.5 %collective-permute-start.5 = (f32[2,64,128]{2,1,0:T(8,128)}, f32[2,64,128]{2,1,0:T(8,128)S(1)}, u32[]{:S(2)}, u32[]{:S(2)}) collective-permute-start(f32[2,64,128]{2,1,0:T(8,128)} %pair_ref.1), channel_id=1, source_target_pairs={{0,12},{4,8},{8,4},{12,0},{1,13},{5,9},{9,5},{13,1},{2,14},{6,10},... | collective-permute-start | bytes 196616 | tf_op jit(solution)/shard_map/ppermute | solution.py:222
  7.8 0.6 %collective-permute-start.3 = (bf16[4,64,64]{2,1,0:T(8,128)(2,1)}, bf16[4,64,64]{2,1,0:T(8,128)(2,1)S(1)}, u32[]{:S(2)}, u32[]{:S(2)}) collective-permute-start(bf16[4,64,64]{2,1,0:T(8,128)(2,1)} %refs_7_.1), channel_id=1, source_target_pairs={{0,3},{1,2},{2,1},{3,0},{4,7},{5,6},{6,5},{7,4},{8,11},{9,10},{10,... | collective-permute-start | bytes 98312 | tf_op jit(solution)/shard_map/ppermute | solution.py:222
  8.5 0.7 %copy-done.7 = f32[4,2,64]{2,1,0:T(2,128)S(1)} copy-done((f32[4,2,64]{2,1,0:T(2,128)S(1)}, f32[4,2,64]{2,1,0:T(2,128)}, u32[]{:S(2)}) %copy-start.7) | copy-done | bytes 2072
  9.2 0.8 %copy-done.1 = f32[128,128]{1,0:T(8,128)S(1)} copy-done((f32[128,128]{1,0:T(8,128)S(1)}, f32[128,128]{1,0:T(8,128)}, u32[]{:S(2)}) %copy-start.1) | copy-done | bytes 65560
  10.0 0.8 %copy-done.2 = f32[128,128]{1,0:T(8,128)S(1)} copy-done((f32[128,128]{1,0:T(8,128)S(1)}, f32[128,128]{1,0:T(8,128)}, u32[]{:S(2)}) %copy-start.2) | copy-done | bytes 65560
  10.9 0.8 %copy-done.3 = f32[128,128]{1,0:T(8,128)S(1)} copy-done((f32[128,128]{1,0:T(8,128)S(1)}, f32[128,128]{1,0:T(8,128)}, u32[]{:S(2)}) %copy-start.3) | copy-done | bytes 65560
  11.7 0.8 %copy-done.4 = f32[2,64,128]{2,1,0:T(8,128)S(1)} copy-done((f32[2,64,128]{2,1,0:T(8,128)S(1)}, f32[2,64,128]{2,1,0:T(8,128)}, u32[]{:S(2)}) %copy-start.4) | copy-done | bytes 65560
  12.6 0.8 %copy-done.5 = f32[2,64,128]{2,1,0:T(8,128)S(1)} copy-done((f32[2,64,128]{2,1,0:T(8,128)S(1)}, f32[2,64,128]{2,1,0:T(8,128)}, u32[]{:S(2)}) %copy-start.5) | copy-done | bytes 65560
  13.4 0.4 %shard_map.103 = (bf16[2,128,128]{2,1,0:T(8,128)(2,1)S(1)}, bf16[2,128,128]{2,1,0:T(8,128)(2,1)S(1)}, bf16[2,128,128]{2,1,0:T(8,128)(2,1)S(1)}, bf16[2,128,128]{...) custom-call(f32[2,64,128]{2,1,0:T(8,128)S(1)} %copy-done.5, ...), custom_call_target="tpu_custom_call" | custom-call | tf_op jit(solution)/shard_map/pallas_call | solution.py:200
  13.8 0.4 %copy-done = bf16[4,64,64]{2,1,0:T(8,128)(2,1)S(1)} copy-done((bf16[4,64,64]{2,1,0:T(8,128)(2,1)S(1)}, bf16[4,64,64]{2,1,0:T(8,128)(2,1)}, u32[]{:S(2)}) %copy-start) | copy-done | bytes 32792
  14.2 2.3 %shard_map.104 = (f32[4,64,256]{2,1,0:T(8,128)S(1)}, f32[2,64,128]{2,1,0:T(8,128)S(1)}, f32[2,64,128]{2,1,0:T(8,128)S(1)}, f32[2,64,128]{2,1,0:T(8,128)S(1)}, f3...) custom-call(s32[1]{0:T(128)} %bitcast.where_ref, bf16[2,128,128]{2,1,0:T(8,128)(2,1)S(1)} %get-tuple-element.25.key_ref, ...), custom_call_target="tpu_custom_call" | custom-call | tf_op jit(solution)/shard_map/pallas_call | solution.py:200
  16.6 2.5 %shard_map.105 = (f32[2,64,128]{2,1,0:T(8,128)S(1)}, f32[2,64,128]{2,1,0:T(8,128)S(1)}, f32[2,64,128]{2,1,0:T(8,128)S(1)}, f32[4,64,64]{2,1,0:T(8,128)S(1)}, f32...) custom-call(s32[1]{0:T(128)} %bitcast.where_ref, ...), custom_call_target="tpu_custom_call" | custom-call | tf_op jit(solution)/shard_map/pallas_call | solution.py:200
  19.1 2.9 %collective-permute-start.7 = (f32[2,64,128]{2,1,0:T(8,128)S(1)}, f32[2,64,128]{2,1,0:T(8,128)S(1)}, u32[]{:S(2)}, u32[]{:S(2)}) collective-permute-start(f32[2,64,128]{2,1,0:T(8,128)S(1)} %get-tuple-element.41), channel_id=1, source_target_pairs={{0,8},{4,12},{8,0},{12,4},{1,9},{5,13},{9,1},{13,5},{2,10},{6,14},... | collective-permute-start | bytes 196616 | tf_op jit(solution)/shard_map/ppermute | solution.py:222
  22.0 1.4 %collective-permute-start.8 = (f32[2,64,128]{2,1,0:T(8,128)S(1)}, f32[2,64,128]{2,1,0:T(8,128)S(1)}, u32[]{:S(2)}, u32[]{:S(2)}) collective-permute-start(f32[2,64,128]{2,1,0:T(8,128)S(1)} %get-tuple-element.42), channel_id=1, source_target_pairs={{0,12},{4,8},{8,4},{12,0},{1,13},{5,9},{9,5},{13,1},{2,14},{6,10},... | collective-permute-start | bytes 196616 | tf_op jit(solution)/shard_map/ppermute | solution.py:222
  23.4 1.5 %collective-permute-start.10 = (f32[4,64,64]{2,1,0:T(8,128)S(1)}, f32[4,64,64]{2,1,0:T(8,128)S(1)}, u32[]{:S(2)}, u32[]{:S(2)}) collective-permute-start(f32[4,64,64]{2,1,0:T(8,128)S(1)} %get-tuple-element.45), channel_id=1, source_target_pairs={{0,2},{1,3},{2,0},{3,1},{4,6},{5,7},{6,4},{7,5},{8,10},{9,11},{10,... | collective-permute-start | bytes 196616 | tf_op jit(solution)/shard_map/ppermute | solution.py:222
  24.9 1.1 %collective-permute-done.7.refs_2_ = f32[2,64,128]{2,1,0:T(8,128)S(1)} collective-permute-done((f32[2,64,128]{2,1,0:T(8,128)S(1)}, f32[2,64,128]{2,1,0:T(8,128)S(1)}, u32[]{:S(2)}, u32[]{:S(2)}) %collective-permute-start.7) | collective-permute-done | bytes 65568 | tf_op jit(solution)/shard_map/ppermute | solution.py:222
  25.9 0.8 %shard_map.106 = f32[2,64,128]{2,1,0:T(8,128)} custom-call(f32[2,64,128]{2,1,0:T(8,128)S(1)} %get-tuple-element.37.dq_ref, bf16[2,128,128]{2,1,0:T(8,128)(2,1)S(1)} %get-tuple-element.38.wq_ref), custom_call_target="tpu_custom_call" | custom-call | tf_op jit(solution)/shard_map/pallas_call | solution.py:200
  26.8 1.5 %collective-permute-done.8.refs_3_ = f32[2,64,128]{2,1,0:T(8,128)S(1)} collective-permute-done((f32[2,64,128]{2,1,0:T(8,128)S(1)}, f32[2,64,128]{2,1,0:T(8,128)S(1)}, u32[]{:S(2)}, u32[]{:S(2)}) %collective-permute-start.8) | collective-permute-done | bytes 65568 | tf_op jit(solution)/shard_map/ppermute | solution.py:222
  28.4 0.6 %shard_map.107 = f32[2,64,128]{2,1,0:T(8,128)} custom-call(f32[2,64,128]{2,1,0:T(8,128)S(1)} %get-tuple-element.39.refs_0_, f32[2,64,128]{2,1,0:T(8,128)S(1)} %collective-permute-done.6.refs_1_, f32[2,64,128]{2,1,0:T(8,128)S(1)} %collective-permute-done.7.refs_2_, f32[2,64,128]{2,1,0:T(8,128)S(1)} %collective-permute-done.8.refs_3_), custom_call_target="tpu_custom_call" | custom-call | tf_op jit(solution)/shard_map/pallas_call | solution.py:200
  29.0 0.6 %collective-permute-done.10.refs_2_ = f32[4,64,64]{2,1,0:T(8,128)S(1)} collective-permute-done((f32[4,64,64]{2,1,0:T(8,128)S(1)}, f32[4,64,64]{2,1,0:T(8,128)S(1)}, u32[]{:S(2)}, u32[]{:S(2)}) %collective-permute-start.10) | collective-permute-done | bytes 65568 | tf_op jit(solution)/shard_map/ppermute | solution.py:222
  29.6 2.1 %collective-permute-done.11.refs_3_ = f32[4,64,64]{2,1,0:T(8,128)S(1)} collective-permute-done((f32[4,64,64]{2,1,0:T(8,128)S(1)}, f32[4,64,64]{2,1,0:T(8,128)S(1)}, u32[]{:S(2)}, u32[]{:S(2)}) %collective-permute-start.11) | collective-permute-done | bytes 65568 | tf_op jit(solution)/shard_map/ppermute | solution.py:222
  31.7 0.7 %shard_map.108 = f32[4,64,64]{2,1,0:T(8,128)} custom-call(f32[4,64,64]{2,1,0:T(8,128)S(1)} %get-tuple-element.43.refs_0_, f32[4,64,64]{2,1,0:T(8,128)S(1)} %collective-permute-done.9.refs_1_, f32[4,64,64]{2,1,0:T(8,128)S(1)} %collective-permute-done.10.refs_2_, f32[4,64,64]{2,1,0:T(8,128)S(1)} %collective-permute-done.11.refs_3_), custom_call_target="tpu_custom_call" | custom-call | tf_op jit(solution)/shard_map/pallas_call | solution.py:200
  (22 shorter events, 0.3 us)
Async XLA Ops:
  0.6 7.2 %collective-permute-start.2 = (bf16[4,64,64]{2,1,0:T(8,128)(2,1)}, bf16[4,64,64]{2,1,0:T(8,128)(2,1)S(1)}, u32[]{:S(2)}, u32[]{:S(2)}) collective-permute-start(bf16[4,64,64]{2,1,0:T(8,128)(2,1)} %refs_7_.1), channel_id=1, source_target_pairs={{0,2},{1,3},{2,0},{3,1},{4,6},{5,7},{6,4},{7,5},{8,10},{9,11},{10,... | collective-permute-start | bytes 98312 | tf_op jit(solution)/shard_map/ppermute | solution.py:222
  3.7 10.1 %collective-permute-start = (f32[2,64,128]{2,1,0:T(8,128)}, f32[2,64,128]{2,1,0:T(8,128)S(1)}, u32[]{:S(2)}, u32[]{:S(2)}) collective-permute-start(f32[2,64,128]{2,1,0:T(8,128)} %pair_ref.1), channel_id=1, source_target_pairs={{0,4},{4,0},{8,12},{12,8},{1,5},{5,1},{9,13},{13,9},{2,6},{6,2},{1... | collective-permute-start | bytes 196616 | tf_op jit(solution)/shard_map/ppermute | solution.py:222
  5.2 11.3 %collective-permute-start.5 = (f32[2,64,128]{2,1,0:T(8,128)}, f32[2,64,128]{2,1,0:T(8,128)S(1)}, u32[]{:S(2)}, u32[]{:S(2)}) collective-permute-start(f32[2,64,128]{2,1,0:T(8,128)} %pair_ref.1), channel_id=1, source_target_pairs={{0,12},{4,8},{8,4},{12,0},{1,13},{5,9},{9,5},{13,1},{2,14},{6,10},... | collective-permute-start | bytes 196616 | tf_op jit(solution)/shard_map/ppermute | solution.py:222
  7.7 8.9 %collective-permute-start.4 = (f32[2,64,128]{2,1,0:T(8,128)}, f32[2,64,128]{2,1,0:T(8,128)S(1)}, u32[]{:S(2)}, u32[]{:S(2)}) collective-permute-start(f32[2,64,128]{2,1,0:T(8,128)} %pair_ref.1), channel_id=1, source_target_pairs={{0,8},{4,12},{8,0},{12,4},{1,9},{5,13},{9,1},{13,5},{2,10},{6,14},... | collective-permute-start | bytes 196616 | tf_op jit(solution)/shard_map/ppermute | solution.py:222
  7.8 5.9 %collective-permute-start.1 = (bf16[4,64,64]{2,1,0:T(8,128)(2,1)}, bf16[4,64,64]{2,1,0:T(8,128)(2,1)S(1)}, u32[]{:S(2)}, u32[]{:S(2)}) collective-permute-start(bf16[4,64,64]{2,1,0:T(8,128)(2,1)} %refs_7_.1), channel_id=1, source_target_pairs={{0,1},{1,0},{2,3},{3,2},{4,5},{5,4},{6,7},{7,6},{8,9},{9,8},{10,11... | collective-permute-start | bytes 98312 | tf_op jit(solution)/shard_map/ppermute | solution.py:222
  7.8 5.9 %collective-permute-start.3 = (bf16[4,64,64]{2,1,0:T(8,128)(2,1)}, bf16[4,64,64]{2,1,0:T(8,128)(2,1)S(1)}, u32[]{:S(2)}, u32[]{:S(2)}) collective-permute-start(bf16[4,64,64]{2,1,0:T(8,128)(2,1)} %refs_7_.1), channel_id=1, source_target_pairs={{0,3},{1,2},{2,1},{3,0},{4,7},{5,6},{6,5},{7,4},{8,11},{9,10},{10,... | collective-permute-start | bytes 98312 | tf_op jit(solution)/shard_map/ppermute | solution.py:222
  8.5 0.7 %copy-start.7 = (f32[4,2,64]{2,1,0:T(2,128)S(1)}, f32[4,2,64]{2,1,0:T(2,128)}, u32[]{:S(2)}) copy-start(f32[4,2,64]{2,1,0:T(2,128)} %corr_ref.1) | copy-start | bytes 6148
  8.5 0.7 %copy-start.6 = (f32[4,2,64]{2,1,0:T(2,128)S(1)}, f32[4,2,64]{2,1,0:T(2,128)}, u32[]{:S(2)}) copy-start(f32[4,2,64]{2,1,0:T(2,128)} %lse_ref.1) | copy-start | bytes 6148
  9.2 0.8 %copy-start.1 = (f32[128,128]{1,0:T(8,128)S(1)}, f32[128,128]{1,0:T(8,128)}, u32[]{:S(2)}) copy-start(f32[128,128]{1,0:T(8,128)} %wq_ref.1) | copy-start | bytes 196612
  10.0 0.8 %copy-start.2 = (f32[128,128]{1,0:T(8,128)S(1)}, f32[128,128]{1,0:T(8,128)}, u32[]{:S(2)}) copy-start(f32[128,128]{1,0:T(8,128)} %wk_ref.1) | copy-start | bytes 196612
  10.9 0.8 %copy-start.3 = (f32[128,128]{1,0:T(8,128)S(1)}, f32[128,128]{1,0:T(8,128)}, u32[]{:S(2)}) copy-start(f32[128,128]{1,0:T(8,128)} %wv_ref.1) | copy-start | bytes 196612
  11.7 0.8 %copy-start.4 = (f32[2,64,128]{2,1,0:T(8,128)S(1)}, f32[2,64,128]{2,1,0:T(8,128)}, u32[]{:S(2)}) copy-start(f32[2,64,128]{2,1,0:T(8,128)} %grad_ref.1) | copy-start | bytes 196612
  12.6 0.8 %copy-start.5 = (f32[2,64,128]{2,1,0:T(8,128)S(1)}, f32[2,64,128]{2,1,0:T(8,128)}, u32[]{:S(2)}) copy-start(f32[2,64,128]{2,1,0:T(8,128)} %pair_ref.1) | copy-start | bytes 196612
  13.4 0.8 %copy-start = (bf16[4,64,64]{2,1,0:T(8,128)(2,1)S(1)}, bf16[4,64,64]{2,1,0:T(8,128)(2,1)}, u32[]{:S(2)}) copy-start(bf16[4,64,64]{2,1,0:T(8,128)(2,1)} %refs_7_.1) | copy-start | bytes 98308
  19.1 6.8 %collective-permute-start.7 = (f32[2,64,128]{2,1,0:T(8,128)S(1)}, f32[2,64,128]{2,1,0:T(8,128)S(1)}, u32[]{:S(2)}, u32[]{:S(2)}) collective-permute-start(f32[2,64,128]{2,1,0:T(8,128)S(1)} %get-tuple-element.41), channel_id=1, source_target_pairs={{0,8},{4,12},{8,0},{12,4},{1,9},{5,13},{9,1},{13,5},{2,10},{6,14},... | collective-permute-start | bytes 196616 | tf_op jit(solution)/shard_map/ppermute | solution.py:222
  22.0 6.2 %collective-permute-start.8 = (f32[2,64,128]{2,1,0:T(8,128)S(1)}, f32[2,64,128]{2,1,0:T(8,128)S(1)}, u32[]{:S(2)}, u32[]{:S(2)}) collective-permute-start(f32[2,64,128]{2,1,0:T(8,128)S(1)} %get-tuple-element.42), channel_id=1, source_target_pairs={{0,12},{4,8},{8,4},{12,0},{1,13},{5,9},{9,5},{13,1},{2,14},{6,10},... | collective-permute-start | bytes 196616 | tf_op jit(solution)/shard_map/ppermute | solution.py:222
  23.4 5.0 %collective-permute-start.6 = (f32[2,64,128]{2,1,0:T(8,128)S(1)}, f32[2,64,128]{2,1,0:T(8,128)S(1)}, u32[]{:S(2)}, u32[]{:S(2)}) collective-permute-start(f32[2,64,128]{2,1,0:T(8,128)S(1)} %get-tuple-element.40), channel_id=1, source_target_pairs={{0,4},{4,0},{8,12},{12,8},{1,5},{5,1},{9,13},{13,9},{2,6},{6,2},{1... | collective-permute-start | bytes 196616 | tf_op jit(solution)/shard_map/ppermute | solution.py:222
  23.4 5.7 %collective-permute-start.9 = (f32[4,64,64]{2,1,0:T(8,128)S(1)}, f32[4,64,64]{2,1,0:T(8,128)S(1)}, u32[]{:S(2)}, u32[]{:S(2)}) collective-permute-start(f32[4,64,64]{2,1,0:T(8,128)S(1)} %get-tuple-element.44), channel_id=1, source_target_pairs={{0,1},{1,0},{2,3},{3,2},{4,5},{5,4},{6,7},{7,6},{8,9},{9,8},{10,11... | collective-permute-start | bytes 196616 | tf_op jit(solution)/shard_map/ppermute | solution.py:222
  23.4 6.2 %collective-permute-start.10 = (f32[4,64,64]{2,1,0:T(8,128)S(1)}, f32[4,64,64]{2,1,0:T(8,128)S(1)}, u32[]{:S(2)}, u32[]{:S(2)}) collective-permute-start(f32[4,64,64]{2,1,0:T(8,128)S(1)} %get-tuple-element.45), channel_id=1, source_target_pairs={{0,2},{1,3},{2,0},{3,1},{4,6},{5,7},{6,4},{7,5},{8,10},{9,11},{10,... | collective-permute-start | bytes 196616 | tf_op jit(solution)/shard_map/ppermute | solution.py:222
  25.9 5.8 %collective-permute-start.11 = (f32[4,64,64]{2,1,0:T(8,128)S(1)}, f32[4,64,64]{2,1,0:T(8,128)S(1)}, u32[]{:S(2)}, u32[]{:S(2)}) collective-permute-start(f32[4,64,64]{2,1,0:T(8,128)S(1)} %get-tuple-element.46), channel_id=1, source_target_pairs={{0,3},{1,2},{2,1},{3,0},{4,7},{5,6},{6,5},{7,4},{8,11},{9,10},{10,... | collective-permute-start | bytes 196616 | tf_op jit(solution)/shard_map/ppermute | solution.py:222

commit v3 on v2

--- a/solution.py
+++ b/solution.py
@@ -42,7 +42,15 @@
         self.proj, self.wide, self.flat = heads * head_dim, heads * cols, rows * cols
 
 
-def prep(pair_ref, wq_ref, wk_ref, wv_ref, grad_ref, lse_ref, corr_ref, *outs, s):
+def prep(*refs, s):
+    sources, outs = refs[:7], refs[7:16]
+    buffers, sem = refs[16:23], refs[23]
+    copies = [pltpu.make_async_copy(src, dst, sem.at[i]) for i, (src, dst) in enumerate(zip(sources, buffers))]
+    for copy in copies:
+        copy.start()
+    for copy in copies:
+        copy.wait()
+    pair_ref, wq_ref, wk_ref, wv_ref, grad_ref, lse_ref, corr_ref = buffers
     q_out, g_out, wq_out, wk_out, wv_out, lse_out, corr_out, key_out, val_out = outs
     wq = split(wq_ref[...])
     wk = split(wk_ref[...])
@@ -118,7 +126,7 @@
         term = dot3(split(jnp.concatenate(dks, axis=0)), wk, NT) + dot3(
             split(jnp.concatenate(dvs, axis=0)), wv, NT
         )
-        yield slot, term.reshape(s.rows, s.cols, s.width), total
+        yield slot, term, total
 
 
 def from_block(s, ref):
@@ -129,27 +137,62 @@
     return keyval
 
 
-def near(where_ref, key_ref, val_ref, *refs, s, slots, nrs):
+LEVEL = 235.0
+
+
+def encode(ref, x):
+    rows, lanes = x.shape
+    peak = jnp.max(jnp.max(jnp.abs(x), axis=1, keepdims=True), axis=0, keepdims=True)
+    top = jnp.maximum(peak, 1e-30).astype(BF16)
+    z = x * (LEVEL / top.astype(F32))
+    z2 = z * z
+    z4 = z2 * z2
+    z8 = z4 * z4
+    z16 = z8 * z8
+    ref[0:rows] = jnp.where(x < 0, -z16, z16).astype(BF16)
+    ref[rows : rows + 16] = jnp.broadcast_to(top, (16, lanes))
+
+
+def decode(ref):
+    rows = ref.shape[0] - 16
+    code = ref[0:rows].astype(F32)
+    top = ref[rows : rows + 16].astype(F32)[0:1]
+    size = jnp.abs(code)
+    for _ in range(4):
+        size = jnp.sqrt(size)
+    return jnp.where(code < 0, -size, size) * (top * (1.0 / LEVEL))
+
+
+def pack(*refs, s, nsub):
+    out = refs[-1]
+    for m in range(nsub):
+        for head in range(s.heads):
+            out[m, :, head * s.cols : (head + 1) * s.cols] = refs[m][head]
+
+
+def near(where_ref, key_ref, val_ref, *refs, s, slots, nrow, nsub):
     common = refs[:6]
     blocks = refs[6 : 5 + slots]
-    biases = refs[5 + slots : 5 + slots + nrs]
-    bias_out, dq_out, *outs = refs[5 + slots + nrs :]
+    packed = refs[5 + slots : 5 + slots + nrow]
+    bias_out, dq_out, *outs = refs[5 + slots + nrow :]
     terms, totals = outs[:slots], outs[slots:]
-    for m in range(nrs):
-        for head in range(s.heads):
-            bias_out[m, :, head * s.cols : (head + 1) * s.cols] = biases[m][head].astype(F32)
+    for m in range(nrow):
+        bias_out[m * nsub : (m + 1) * nsub] = packed[m][...]
     shift = where_ref[0]
     work = [(0, lambda wk, wv: (pair_of(key_ref), pair_of(val_ref)))]
     work += [(k, from_block(s, blocks[k - 1])) for k in range(1, slots)]
     dquery = [None] * s.rows
-    for slot, term, total in process(s, common, work, lambda k: bias_out[shift ^ k], dquery):
-        terms[slot][...] = term
+    for slot, term, total in process(s, common, work, lambda k: bias_out[shift ^ k].astype(F32), dquery):
+        if slot == 0:
+            terms[0][...] = term
+        else:
+            encode(terms[slot], term)
         totals[slot][...] = total
     for r in range(s.rows):
         dq_out[r] = dquery[r]
 
 
-def far(where_ref, bias_ref, dq_ref, *refs, s, done, count):
+def far(where_ref, bias_ref, dq_ref, *refs, s, done, count, nrow, nsub):
     common = refs[:6]
     totals = refs[6 : 6 + done]
     left = count - done
@@ -162,14 +205,25 @@
         spot[shift ^ k] = totals[k][...]
     work = [(done + k, from_block(s, blocks[k])) for k in range(left)]
     dquery = [dq_ref[r] for r in range(s.rows)]
-    for slot, term, total in process(s, common, work, lambda k: bias_ref[shift ^ k], dquery):
-        terms[slot - done][...] = term
+    for slot, term, total in process(s, common, work, lambda k: bias_ref[shift ^ k].astype(F32), dquery):
+        encode(terms[slot - done], term)
         spot[shift ^ slot] = total
     for r in range(s.rows):
         dq_out[r] = dquery[r]
-    for m, ref in enumerate(dbs):
-        for head in range(s.heads):
-            ref[head] = spot[m, :, head * s.cols : (head + 1) * s.cols]
+    for m in range(nrow * nsub):
+        dbs[m % nsub][m // nsub] = spot[m]
+
+
+def middle(*refs, nrow, nsub):
+    parts, outs = refs[:nsub], refs[nsub:]
+    for m in range(nrow):
+        total = parts[0][m]
+        for ref in parts[1:]:
+            total = total + ref[m]
+        if m == 0:
+            outs[0][...] = total
+        else:
+            encode(outs[m], total)
 
 
 def tail(dq_ref, wq_ref, out_ref, *, s):
@@ -177,11 +231,19 @@
     out_ref[...] = dot3(split(dq), pair_of(wq_ref), NT).reshape(s.rows, s.cols, s.width)
 
 
-def add_up(*refs):
-    total = refs[0][...]
-    for ref in refs[1:-1]:
-        total = total + ref[...]
-    refs[-1][...] = total
+def add_keys(own_ref, *refs, s):
+    total = own_ref[...]
+    for ref in refs[:-1]:
+        total = total + decode(ref)
+    refs[-1][...] = total.reshape(s.rows, s.cols, s.width)
+
+
+def add_bias(own_ref, *refs, s):
+    total = own_ref[...]
+    for ref in refs[:-1]:
+        total = total + decode(ref)
+    for head in range(s.heads):
+        refs[-1][head] = total[:, head * s.cols : (head + 1) * s.cols]
 
 
 def xor_pairs(size, mask):
@@ -192,9 +254,9 @@
     return pltpu.with_memory_space_constraint(x, pltpu.VMEM)
 
 
-def call(body, outs, args, scratch=(), scalar=False):
+def call(body, outs, args, scratch=(), scalar=False, kept=pltpu.VMEM):
+    specs = [pl.BlockSpec(memory_space=pltpu.VMEM if kept is pltpu.VMEM else pl.ANY)] * len(args)
     vmem = pl.BlockSpec(memory_space=pltpu.VMEM)
-    specs = [vmem] * len(args)
     if scalar:
         specs[0] = pl.BlockSpec(memory_space=pltpu.SMEM)
     return pl.pallas_call(
@@ -216,55 +278,68 @@
     s = Shape(rows, cols, width, heads, w_query.shape[1] // heads)
     nrs = nrow * nsub
     count = ncol
-    tile = ("row", "sub")
 
     def move(x, axis, size, mask):
         return lax.ppermute(x, axis, xor_pairs(size, mask))
 
-    part = jax.ShapeDtypeStruct((rows, cols, width), F32)
-    vpart = pltpu.VMEM((rows, cols, width), F32)
     blocks = [here(move(pair, "col", ncol, k)) for k in range(1, ncol)]
-    biases = [bias] + [here(move(bias, tile, nrs, k)) for k in range(1, nrs)]
+    biases = [bias] + [here(move(bias, "sub", nsub, k)) for k in range(1, nsub)]
+    packed_shape = pltpu.VMEM((nsub, cols, s.wide), BF16)
+    (packed,) = call(functools.partial(pack, s=s, nsub=nsub), [packed_shape], biases)
+    groups = [here(packed)] + [here(move(packed, "row", nrow, k)) for k in range(1, nrow)]
     place = lax.axis_index("col") ^ (lax.axis_index("row") * nsub + lax.axis_index("sub"))
     place = place.reshape(1)
     two = pltpu.VMEM((2, s.flat, s.proj), BF16)
     wtwo = pltpu.VMEM((2, width, s.proj), BF16)
     wide = pltpu.VMEM((rows, cols, s.wide), F32)
+    params = [pair, w_query, w_key, w_value, grad_out, log_total, row_corr]
     q, g, wq, wk, wv, lse, corr, key, val = map(
         here,
         call(
             functools.partial(prep, s=s),
             [two, two, wtwo, wtwo, wtwo, wide, wide, two, two],
-            [pair, w_query, w_key, w_value, grad_out, log_total, row_corr],
+            [pltpu.with_memory_space_constraint(x, pltpu.HBM) for x in params],
+            scratch=[pltpu.VMEM(x.shape, F32) for x in params]
+            + [pltpu.SemaphoreType.DMA((len(params),))],
+            kept=pltpu.HBM,
         ),
     )
     common = [q, g, wk, wv, lse, corr]
     total = pltpu.VMEM((cols, s.wide), F32)
     dq_shape = pltpu.VMEM((rows, cols, s.proj), F32)
+    own_term = pltpu.VMEM((s.flat, width), F32)
+    term = pltpu.VMEM((s.flat + 16, width), BF16)
     bias_wide, dq, *rest = call(
-        functools.partial(near, s=s, slots=NEAR, nrs=nrs),
-        [pltpu.VMEM((nrs, cols, s.wide), F32), dq_shape] + [vpart] * NEAR + [total] * NEAR,
-        [place, key, val, *common, *blocks[: NEAR - 1], *biases],
+        functools.partial(near, s=s, slots=NEAR, nrow=nrow, nsub=nsub),
+        [pltpu.VMEM((nrs, cols, s.wide), BF16), dq_shape, own_term]
+        + [term] * (NEAR - 1)
+        + [total] * NEAR,
+        [place, key, val, *common, *blocks[: NEAR - 1], *groups],
         scalar=True,
     )
     terms, totals = rest[:NEAR], rest[NEAR:]
-    dbs = [pltpu.VMEM((heads, cols, cols), F32)] * nrs
     dq, *rest = call(
-        functools.partial(far, s=s, done=NEAR, count=count),
-        [dq_shape] + [vpart] * (count - NEAR) + dbs,
+        functools.partial(far, s=s, done=NEAR, count=count, nrow=nrow, nsub=nsub),
+        [dq_shape] + [term] * (count - NEAR) + [pltpu.VMEM((nrow, cols, s.wide), F32)] * nsub,
         [place, here(bias_wide), here(dq), *common, *map(here, totals), *blocks[NEAR - 1 :]],
         scratch=[pltpu.VMEM((nrs, cols, s.wide), F32)],
         scalar=True,
     )
     terms = terms + rest[: count - NEAR]
-    dbias = rest[count - NEAR :]
+    halves = rest[count - NEAR :]
     got = [here(move(terms[k], "col", ncol, k)) for k in range(1, ncol)]
-    dgot = [here(move(dbias[k], tile, nrs, k)) for k in range(1, nrs)]
+    halves = [here(halves[0])] + [here(move(halves[k], "sub", nsub, k)) for k in range(1, nsub)]
+    sums = call(
+        functools.partial(middle, nrow=nrow, nsub=nsub),
+        [total] + [pltpu.VMEM((cols + 16, s.wide), BF16)] * (nrow - 1),
+        halves,
+    )
+    dgot = [here(move(sums[k], "row", nrow, k)) for k in range(1, nrow)]
+    part = jax.ShapeDtypeStruct((rows, cols, width), F32)
     (query_grad,) = call(functools.partial(tail, s=s), [part], [here(dq), wq])
-    (key_grad,) = call(add_up, [part], [here(terms[0]), *got])
-    (bias_grad,) = call(
-        add_up, [jax.ShapeDtypeStruct((heads, cols, cols), F32)], [here(dbias[0]), *dgot]
-    )
+    (key_grad,) = call(functools.partial(add_keys, s=s), [part], [here(terms[0]), *got])
+    dshape = jax.ShapeDtypeStruct((heads, cols, cols), F32)
+    (bias_grad,) = call(functools.partial(add_bias, s=s), [dshape], [here(sums[0]), *dgot])
     return query_grad, key_grad, bias_grad
 
 

time: 32.9 us -> 29.5 us (0.90)
  local copies, waits for them, and re-layouts: 5.32 us -> 0.84 us
  Pallas kernels: 7.4 us -> 9.23 us
  starting transfers between devices: 13.6 us -> 12.6 us
  waiting for transfers between devices: 5.42 us -> 5.92 us
    unnamed x16 -> x4, local copies, waits for them, and re-layouts: 5.32 us -> 0.84 us
    pallas_call x6 -> x8, Pallas kernels: 7.4 us -> 9.23 us  [call(): pl.pallas_call(body, out_shape=outs, in_specs=specs, out_specs=[vmem] * l...]
    ppermute x12 -> x10, starting transfers between devices: 13.6 us -> 12.6 us  [move(): return lax.ppermute(x, axis, xor_pairs(size, mask))]
    ppermute x12 -> x10, waiting for transfers between devices: 5.42 us -> 5.92 us  [move(): return lax.ppermute(x, axis, xor_pairs(size, mask))]
  transfers between devices with their start and end apart: 12 -> 10, of which waited for: 5 -> 5; matrix products, arithmetic and copies ran while one was open for 0% -> 0% of each run, Pallas kernels for 13% -> 19%
where the time goes in v3:
time: 29.5 us; the launch traced here: 29.3 us
  starting transfers between devices  12.6 us (43%)
  Pallas kernels  9.23 us (31%)
  waiting for transfers between devices  5.92 us (20%)
  local copies, waits for them, and re-layouts  0.84 us (3%)
  between operations  0.71 us (2%)
    ppermute x10, starting transfers between devices, move(): return lax.ppermute(x, axis, xor_pairs(size, mask))  12.6 us
    pallas_call x8, Pallas kernels, call(): pl.pallas_call(body, out_shape=outs, in_specs=specs, out_specs=[vmem] * l...  9.23 us
    ppermute x10, waiting for transfers between devices, move(): return lax.ppermute(x, axis, xor_pairs(size, mask))  5.92 us
    unnamed x4, local copies, waits for them, and re-layouts  0.84 us
  transfers between devices with their start and end apart: 10, of which 5 were waited for; matrix products, arithmetic and copies ran while one was open for 0% of the time, Pallas kernels for 19%

profile of v3, /device:TPU:0, one launch (start us, length us, event | category | flops | bytes accessed | tf_op | source)
XLA Modules:
  0.0 29.3 jit_solution(6841559524286095410)
XLA Ops:
  0.6 0.6 %collective-permute-start.1 = (bf16[4,64,64]{2,1,0:T(8,128)(2,1)}, bf16[4,64,64]{2,1,0:T(8,128)(2,1)S(1)}, u32[]{:S(2)}, u32[]{:S(2)}) collective-permute-start(bf16[4,64,64]{2,1,0:T(8,128)(2,1)} %refs_0_.3), channel_id=1, source_target_pairs={{0,1},{1,0},{2,3},{3,2},{4,5},{5,4},{6,7},{7,6},{8,9},{9,8},{10,11... | collective-permute-start | bytes 98312 | tf_op jit(solution)/shard_map/ppermute | solution.py:283
  1.2 2.6 %collective-permute-start = (f32[2,64,128]{2,1,0:T(8,128)}, f32[2,64,128]{2,1,0:T(8,128)S(1)}, u32[]{:S(2)}, u32[]{:S(2)}) collective-permute-start(f32[2,64,128]{2,1,0:T(8,128)} %refs_0_.2), channel_id=1, source_target_pairs={{0,4},{4,0},{8,12},{12,8},{1,5},{5,1},{9,13},{13,9},{2,6},{6,2},{1... | collective-permute-start | bytes 196616 | tf_op jit(solution)/shard_map/ppermute | solution.py:283
  3.8 0.8 %copy-done = bf16[4,64,64]{2,1,0:T(8,128)(2,1)S(1)} copy-done((bf16[4,64,64]{2,1,0:T(8,128)(2,1)S(1)}, bf16[4,64,64]{2,1,0:T(8,128)(2,1)}, u32[]{:S(2)}) %copy-start) | copy-done | bytes 32792
  4.7 0.1 shard_map.104.refs_7_
  4.8 1.6 %collective-permute-start.2 = (bf16[2,64,256]{2,1,0:T(8,128)(2,1)S(1)}, bf16[2,64,256]{2,1,0:T(8,128)(2,1)S(1)}, u32[]{:S(2)}, u32[]{:S(2)}) collective-permute-start(bf16[2,64,256]{2,1,0:T(8,128)(2,1)S(1)} %shard_map.104.refs_7_), channel_id=1, source_target_pairs={{0,2},{2,0},{1,3},{3,1},{4,6},{6,4},{5,7},{7,5},{8,10},{10,8},{9,1... | collective-permute-start | bytes 196616 | tf_op jit(solution)/shard_map/ppermute | solution.py:283
  6.3 3.4 %collective-permute-start.4 = (f32[2,64,128]{2,1,0:T(8,128)S(1)}, f32[2,64,128]{2,1,0:T(8,128)S(1)}, u32[]{:S(2)}, u32[]{:S(2)}) collective-permute-start(f32[2,64,128]{2,1,0:T(8,128)S(1)} %copy-done.1), channel_id=1, source_target_pairs={{0,12},{4,8},{8,4},{12,0},{1,13},{5,9},{9,5},{13,1},{2,14},{6,10},... | collective-permute-start | bytes 196616 | tf_op jit(solution)/shard_map/ppermute | solution.py:283
  9.7 0.0 collective-permute-start.3
  9.7 1.4 %shard_map.103 = (bf16[2,128,128]{2,1,0:T(8,128)(2,1)S(1)}, bf16[2,128,128]{2,1,0:T(8,128)(2,1)S(1)}, bf16[2,128,128]{2,1,0:T(8,128)(2,1)S(1)}, bf16[2,128,128]{...) custom-call(f32[2,64,128]{2,1,0:T(8,128)} %refs_0_.2, ...), custom_call_target="tpu_custom_call" | custom-call | tf_op jit(solution)/shard_map/pallas_call | solution.py:262
  11.2 2.4 %shard_map.105 = (bf16[4,64,256]{2,1,0:T(8,128)(2,1)S(1)}, f32[2,64,128]{2,1,0:T(8,128)S(1)}, f32[128,128]{1,0:T(8,128)S(1)}, bf16[144,128]{1,0:T(8,128)(2,1)S(1...) custom-call(s32[1]{0:T(128)} %bitcast.where_ref, bf16[2,128,128]{2,1,0:T(8,128)(2,1)S(1)} %get-tuple-element.25.key_ref, ...), custom_call_target="tpu_custom_call" | custom-call | tf_op jit(solution)/shard_map/pallas_call | solution.py:262
  13.6 1.9 %collective-permute-done.3.refs_8_ = f32[2,64,128]{2,1,0:T(8,128)S(1)} collective-permute-done((f32[2,64,128]{2,1,0:T(8,128)S(1)}, f32[2,64,128]{2,1,0:T(8,128)S(1)}, u32[]{:S(2)}, u32[]{:S(2)}) %collective-permute-start.3) | collective-permute-done | bytes 65568 | tf_op jit(solution)/shard_map/ppermute | solution.py:283
  15.5 2.6 %shard_map.106 = (f32[2,64,128]{2,1,0:T(8,128)S(1)}, bf16[144,128]{1,0:T(8,128)(2,1)S(1)}, bf16[144,128]{1,0:T(8,128)(2,1)S(1)}, f32[2,64,256]{2,1,0:T(8,128)S(1)}, f32[2,64,256]{2,1,0:T(8,128)S(1)}) custom-call(s32[1]{0:T(128)} %bitcast.where_ref, bf16[4,64,256]{2,1,0:T(8,128)(2,1)S(1)} %get-tuple-element.33.bias_ref, ...), custom_call_target="tpu_custom_call" | custom-call | tf_op jit(solution)/shard_map/pallas_call | solution.py:262
  18.2 0.1 collective-permute-start.8
  18.2 1.3 %collective-permute-done.8.refs_1_ = f32[2,64,256]{2,1,0:T(8,128)S(1)} collective-permute-done((f32[2,64,256]{2,1,0:T(8,128)S(1)}, f32[2,64,256]{2,1,0:T(8,128)S(1)}, u32[]{:S(2)}, u32[]{:S(2)}) %collective-permute-start.8) | collective-permute-done | bytes 131104 | tf_op jit(solution)/shard_map/ppermute | solution.py:283
  19.6 0.1 shard_map.109
  19.7 0.9 %collective-permute-start.9 = (bf16[80,256]{1,0:T(8,128)(2,1)S(1)}, bf16[80,256]{1,0:T(8,128)(2,1)S(1)}, u32[]{:S(2)}, u32[]{:S(2)}) collective-permute-start(bf16[80,256]{1,0:T(8,128)(2,1)S(1)} %get-tuple-element.46), channel_id=1, source_target_pairs={{0,2},{2,0},{1,3},{3,1},{4,6},{6,4},{5,7},{7,5},{8,10},{10,8},{9,1... | collective-permute-start | bytes 122888 | tf_op jit(solution)/shard_map/ppermute | solution.py:283
  20.6 1.0 %collective-permute-start.6 = (bf16[144,128]{1,0:T(8,128)(2,1)S(1)}, bf16[144,128]{1,0:T(8,128)(2,1)S(1)}, u32[]{:S(2)}, u32[]{:S(2)}) collective-permute-start(bf16[144,128]{1,0:T(8,128)(2,1)S(1)} %get-tuple-element.41), channel_id=1, source_target_pairs={{0,8},{4,12},{8,0},{12,4},{1,9},{5,13},{9,1},{13,5},{2,10},{6,14},... | collective-permute-start | bytes 110600 | tf_op jit(solution)/shard_map/ppermute | solution.py:283
  21.5 1.7 %collective-permute-start.7 = (bf16[144,128]{1,0:T(8,128)(2,1)S(1)}, bf16[144,128]{1,0:T(8,128)(2,1)S(1)}, u32[]{:S(2)}, u32[]{:S(2)}) collective-permute-start(bf16[144,128]{1,0:T(8,128)(2,1)S(1)} %get-tuple-element.42), channel_id=1, source_target_pairs={{0,12},{4,8},{8,4},{12,0},{1,13},{5,9},{9,5},{13,1},{2,14},{6,10},... | collective-permute-start | bytes 110600 | tf_op jit(solution)/shard_map/ppermute | solution.py:283
  23.2 0.8 %collective-permute-start.5 = (bf16[144,128]{1,0:T(8,128)(2,1)S(1)}, bf16[144,128]{1,0:T(8,128)(2,1)S(1)}, u32[]{:S(2)}, u32[]{:S(2)}) collective-permute-start(bf16[144,128]{1,0:T(8,128)(2,1)S(1)} %get-tuple-element.40), channel_id=1, source_target_pairs={{0,4},{4,0},{8,12},{12,8},{1,5},{5,1},{9,13},{13,9},{2,6},{6,2},{1... | collective-permute-start | bytes 110600 | tf_op jit(solution)/shard_map/ppermute | solution.py:283
  24.1 0.8 %shard_map.107 = f32[2,64,128]{2,1,0:T(8,128)} custom-call(f32[2,64,128]{2,1,0:T(8,128)S(1)} %get-tuple-element.37.dq_ref, bf16[2,128,128]{2,1,0:T(8,128)(2,1)S(1)} %get-tuple-element.38.wq_ref), custom_call_target="tpu_custom_call" | custom-call | tf_op jit(solution)/shard_map/pallas_call | solution.py:262
  24.9 1.2 %collective-permute-done.6.refs_1_ = bf16[144,128]{1,0:T(8,128)(2,1)S(1)} collective-permute-done((bf16[144,128]{1,0:T(8,128)(2,1)S(1)}, bf16[144,128]{1,0:T(8,128)(2,1)S(1)}, u32[]{:S(2)}, u32[]{:S(2)}) %collective-permute-start.6) | collective-permute-done | bytes 36896 | tf_op jit(solution)/shard_map/ppermute | solution.py:283
  26.1 1.4 %collective-permute-done.7.refs_2_ = bf16[144,128]{1,0:T(8,128)(2,1)S(1)} collective-permute-done((bf16[144,128]{1,0:T(8,128)(2,1)S(1)}, bf16[144,128]{1,0:T(8,128)(2,1)S(1)}, u32[]{:S(2)}, u32[]{:S(2)}) %collective-permute-start.7) | collective-permute-done | bytes 36896 | tf_op jit(solution)/shard_map/ppermute | solution.py:283
  27.5 0.1 collective-permute-done.5.refs_0_
  27.6 0.9 %shard_map.108 = f32[2,64,128]{2,1,0:T(8,128)} custom-call(f32[128,128]{1,0:T(8,128)S(1)} %get-tuple-element.39.own_ref, bf16[144,128]{1,0:T(8,128)(2,1)S(1)} %collective-permute-done.5.refs_0_, bf16[144,128]{1,0:T(8,128)(2,1)S(1)} %collective-permute-done.6.refs_1_, bf16[144,128]{1,0:T(8,128)(2,1)S(1)} %collective-permute-done.7.refs_2_), custom_call_target="tpu_custom_call" | custom-call | tf_op jit(solution)/shard_map/pallas_call | solution.py:262
  28.5 0.8 %shard_map.110 = f32[4,64,64]{2,1,0:T(8,128)} custom-call(f32[64,256]{1,0:T(8,128)S(1)} %get-tuple-element.45.own_ref, bf16[80,256]{1,0:T(8,128)(2,1)S(1)} %collective-permute-done.9.refs_0_), custom_call_target="tpu_custom_call" | custom-call | tf_op jit(solution)/shard_map/pallas_call | solution.py:262
  (8 shorter events, 0.0 us)
Async XLA Ops:
  0.6 3.2 %collective-permute-start.1 = (bf16[4,64,64]{2,1,0:T(8,128)(2,1)}, bf16[4,64,64]{2,1,0:T(8,128)(2,1)S(1)}, u32[]{:S(2)}, u32[]{:S(2)}) collective-permute-start(bf16[4,64,64]{2,1,0:T(8,128)(2,1)} %refs_0_.3), channel_id=1, source_target_pairs={{0,1},{1,0},{2,3},{3,2},{4,5},{5,4},{6,7},{7,6},{8,9},{9,8},{10,11... | collective-permute-start | bytes 98312 | tf_op jit(solution)/shard_map/ppermute | solution.py:283
  1.2 10.0 %collective-permute-start = (f32[2,64,128]{2,1,0:T(8,128)}, f32[2,64,128]{2,1,0:T(8,128)S(1)}, u32[]{:S(2)}, u32[]{:S(2)}) collective-permute-start(f32[2,64,128]{2,1,0:T(8,128)} %refs_0_.2), channel_id=1, source_target_pairs={{0,4},{4,0},{8,12},{12,8},{1,5},{5,1},{9,13},{13,9},{2,6},{6,2},{1... | collective-permute-start | bytes 196616 | tf_op jit(solution)/shard_map/ppermute | solution.py:283
  3.8 0.8 %copy-start = (bf16[4,64,64]{2,1,0:T(8,128)(2,1)S(1)}, bf16[4,64,64]{2,1,0:T(8,128)(2,1)}, u32[]{:S(2)}) copy-start(bf16[4,64,64]{2,1,0:T(8,128)(2,1)} %refs_0_.3) | copy-start | bytes 98308
  4.7 1.7 %copy-start.1 = (f32[2,64,128]{2,1,0:T(8,128)S(1)}, f32[2,64,128]{2,1,0:T(8,128)}, u32[]{:S(2)}) copy-start(f32[2,64,128]{2,1,0:T(8,128)} %refs_0_.2) | copy-start | bytes 196612
  4.8 6.4 %collective-permute-start.2 = (bf16[2,64,256]{2,1,0:T(8,128)(2,1)S(1)}, bf16[2,64,256]{2,1,0:T(8,128)(2,1)S(1)}, u32[]{:S(2)}, u32[]{:S(2)}) collective-permute-start(bf16[2,64,256]{2,1,0:T(8,128)(2,1)S(1)} %shard_map.104.refs_7_), channel_id=1, source_target_pairs={{0,2},{2,0},{1,3},{3,1},{4,6},{6,4},{5,7},{7,5},{8,10},{10,8},{9,1... | collective-permute-start | bytes 196616 | tf_op jit(solution)/shard_map/ppermute | solution.py:283
  6.3 7.3 %collective-permute-start.4 = (f32[2,64,128]{2,1,0:T(8,128)S(1)}, f32[2,64,128]{2,1,0:T(8,128)S(1)}, u32[]{:S(2)}, u32[]{:S(2)}) collective-permute-start(f32[2,64,128]{2,1,0:T(8,128)S(1)} %copy-done.1), channel_id=1, source_target_pairs={{0,12},{4,8},{8,4},{12,0},{1,13},{5,9},{9,5},{13,1},{2,14},{6,10},... | collective-permute-start | bytes 196616 | tf_op jit(solution)/shard_map/ppermute | solution.py:283
  9.7 5.8 %collective-permute-start.3 = (f32[2,64,128]{2,1,0:T(8,128)S(1)}, f32[2,64,128]{2,1,0:T(8,128)S(1)}, u32[]{:S(2)}, u32[]{:S(2)}) collective-permute-start(f32[2,64,128]{2,1,0:T(8,128)S(1)} %copy-done.1), channel_id=1, source_target_pairs={{0,8},{4,12},{8,0},{12,4},{1,9},{5,13},{9,1},{13,5},{2,10},{6,14},... | collective-permute-start | bytes 196616 | tf_op jit(solution)/shard_map/ppermute | solution.py:283
  18.2 1.4 %collective-permute-start.8 = (f32[2,64,256]{2,1,0:T(8,128)S(1)}, f32[2,64,256]{2,1,0:T(8,128)S(1)}, u32[]{:S(2)}, u32[]{:S(2)}) collective-permute-start(f32[2,64,256]{2,1,0:T(8,128)S(1)} %get-tuple-element.44), channel_id=1, source_target_pairs={{0,1},{1,0},{2,3},{3,2},{4,5},{5,4},{6,7},{7,6},{8,9},{9,8},{10,11... | collective-permute-start | bytes 393224 | tf_op jit(solution)/shard_map/ppermute | solution.py:283
  19.7 8.8 %collective-permute-start.9 = (bf16[80,256]{1,0:T(8,128)(2,1)S(1)}, bf16[80,256]{1,0:T(8,128)(2,1)S(1)}, u32[]{:S(2)}, u32[]{:S(2)}) collective-permute-start(bf16[80,256]{1,0:T(8,128)(2,1)S(1)} %get-tuple-element.46), channel_id=1, source_target_pairs={{0,2},{2,0},{1,3},{3,1},{4,6},{6,4},{5,7},{7,5},{8,10},{10,8},{9,1... | collective-permute-start | bytes 122888 | tf_op jit(solution)/shard_map/ppermute | solution.py:283
  20.6 5.5 %collective-permute-start.6 = (bf16[144,128]{1,0:T(8,128)(2,1)S(1)}, bf16[144,128]{1,0:T(8,128)(2,1)S(1)}, u32[]{:S(2)}, u32[]{:S(2)}) collective-permute-start(bf16[144,128]{1,0:T(8,128)(2,1)S(1)} %get-tuple-element.41), channel_id=1, source_target_pairs={{0,8},{4,12},{8,0},{12,4},{1,9},{5,13},{9,1},{13,5},{2,10},{6,14},... | collective-permute-start | bytes 110600 | tf_op jit(solution)/shard_map/ppermute | solution.py:283
  21.5 6.0 %collective-permute-start.7 = (bf16[144,128]{1,0:T(8,128)(2,1)S(1)}, bf16[144,128]{1,0:T(8,128)(2,1)S(1)}, u32[]{:S(2)}, u32[]{:S(2)}) collective-permute-start(bf16[144,128]{1,0:T(8,128)(2,1)S(1)} %get-tuple-element.42), channel_id=1, source_target_pairs={{0,12},{4,8},{8,4},{12,0},{1,13},{5,9},{9,5},{13,1},{2,14},{6,10},... | collective-permute-start | bytes 110600 | tf_op jit(solution)/shard_map/ppermute | solution.py:283
  23.2 4.4 %collective-permute-start.5 = (bf16[144,128]{1,0:T(8,128)(2,1)S(1)}, bf16[144,128]{1,0:T(8,128)(2,1)S(1)}, u32[]{:S(2)}, u32[]{:S(2)}) collective-permute-start(bf16[144,128]{1,0:T(8,128)(2,1)S(1)} %get-tuple-element.40), channel_id=1, source_target_pairs={{0,4},{4,0},{8,12},{12,8},{1,5},{5,1},{9,13},{13,9},{2,6},{6,2},{1... | collective-permute-start | bytes 110600 | tf_op jit(solution)/shard_map/ppermute | solution.py:283

commit v4 on v0

v4 whole, which is shorter than its diff:
```python
import functools

import jax
import jax.numpy as jnp
from jax import lax
from jax.experimental import pallas as pl
from jax.experimental.pallas import tpu as pltpu
from jax.sharding import PartitionSpec as P

NN = (((1,), (0,)), ((), ()))
NT = (((1,), (1,)), ((), ()))
TN = (((0,), (0,)), ((), ()))
F32 = jnp.float32
BF16 = jnp.bfloat16
LEVEL = 235.0


def split(x):
    high = x.astype(BF16)
    return high, (x - high.astype(F32)).astype(BF16)


def one(x, y, dims):
    return lax.dot_general(x, y, dims, preferred_element_type=F32)


def dot3(a, b, dims):
    axis = 0 if dims is NT else 1
    size = b[0].shape[axis]
    both = one(a[0], jnp.concatenate(b, axis=axis), dims)
    return both[:, :size] + both[:, size:] + one(a[1], b[0], dims)


def pair_of(ref, *index):
    return ref[(0, *index)], ref[(1, *index)]


def store(ref, pieces, *index):
    ref[(0, *index)] = pieces[0]
    ref[(1, *index)] = pieces[1]


class Shape:
    def __init__(self, rows, cols, width, heads, head_dim):
        self.rows, self.cols, self.width = rows, cols, width
        self.heads, self.head_dim = heads, head_dim
        self.proj, self.wide = heads * head_dim, heads * cols
        self.flat, self.two = rows * cols, 2 * cols


def encode(ref, x):
    rows, lanes = x.shape
    peak = jnp.max(jnp.max(jnp.abs(x), axis=1, keepdims=True), axis=0, keepdims=True)
    top = jnp.maximum(peak, 1e-30).astype(BF16)
    z = x * (LEVEL / top.astype(F32))
    z2 = z * z
    z4 = z2 * z2
    z8 = z4 * z4
    z16 = z8 * z8
    ref[0:rows] = jnp.where(x < 0, -z16, z16).astype(BF16)
    ref[rows : rows + 16] = jnp.broadcast_to(top, (16, lanes))


def decode(ref):
    rows = ref.shape[0] - 16
    code = ref[0:rows].astype(F32)
    top = ref[rows : rows + 16].astype(F32)[0:1]
    size = jnp.abs(code)
    for _ in range(4):
        size = jnp.sqrt(size)
    return jnp.where(code < 0, -size, size) * (top * (1.0 / LEVEL))


def half_join(low, high, width):
    lane = lax.broadcasted_iota(jnp.int32, low.shape, 1)
    return jnp.where(lane < width, low, high)


def pack(own_ref, other_ref, out_ref, *, s):
    out_ref[:, 0 : s.cols] = own_ref[...].reshape(s.wide, s.cols)
    out_ref[:, s.cols : s.two] = other_ref[...].reshape(s.wide, s.cols)


def prep(*refs, s):
    sources, outs = refs[:7], refs[7:14]
    buffers, sem = refs[14:21], refs[21]
    copies = [pltpu.make_async_copy(src, dst, sem.at[i]) for i, (src, dst) in enumerate(zip(sources, buffers))]
    for copy in copies:
        copy.start()
    for copy in copies:
        copy.wait()
    pair_ref, wq_ref, wk_ref, wv_ref, grad_ref, lse_ref, corr_ref = buffers
    q_out, g_out, wq_out, w_out, lse_out, corr_out, kv_out = outs
    wq = split(wq_ref[...])
    both = split(jnp.concatenate([wk_ref[...], wv_ref[...]], axis=1))
    store(wq_out, wq)
    store(w_out, both)
    own = split(pair_ref[...].reshape(s.flat, s.width))
    query = split(dot3(own, wq, NN) * (s.head_dim ** (-0.5)))
    kv_out[...] = dot3(own, both, NN)
    grads = split(grad_ref[...].reshape(s.flat, s.proj))
    row_head = lax.broadcasted_iota(jnp.int32, (s.wide, s.proj), 0) // s.cols
    chan_head = lax.broadcasted_iota(jnp.int32, (s.wide, s.proj), 1) // s.head_dim
    diag = row_head == chan_head

    def spread(piece):
        return jnp.where(diag, jnp.concatenate([piece] * s.heads, axis=0), jnp.zeros((), piece.dtype))

    def widen(ref, row):
        stack = jnp.concatenate([ref[head, row : row + 1, :] for head in range(s.heads)], axis=0)
        stack = jnp.concatenate([stack, jnp.zeros((8 - s.heads % 8, s.cols), F32)], axis=0)
        turned = stack.T
        return jnp.concatenate(
            [jnp.broadcast_to(turned[:, head : head + 1], (s.cols, s.two)) for head in range(s.heads)], axis=0
        )

    for r in range(s.rows):
        rows = slice(r * s.cols, (r + 1) * s.cols)
        store(q_out, [spread(x[rows]) for x in query], r)
        store(g_out, [spread(x[rows]) for x in grads], r)
        lse_out[r] = widen(lse_ref, r)
        corr_out[r] = widen(corr_ref, r)


def from_block(s, ref):
    return lambda both: dot3(split(ref[...].reshape(s.flat, s.width)), both, NN)


def scores(where_ref, *refs, s, pairs, own):
    q_ref, g_ref, w_ref, lse_ref, corr_ref = refs[:5]
    blocks = refs[5 : 5 + 2 * pairs]
    key_out, score_out, cot_out, kv_scr = refs[5 + 2 * pairs :]
    both = pair_of(w_ref)
    odd = where_ref[0] & 1
    for p in range(pairs):
        for slot in range(2):
            ref = blocks[2 * p + slot]
            value = ref[...] if own and p == 0 and slot == 0 else from_block(s, ref)(both)
            for r in range(s.rows):
                kv_scr[p, r, pl.ds((odd ^ slot) * s.cols, s.cols)] = value[r * s.cols : (r + 1) * s.cols]
        for r in range(s.rows):
            key = split(kv_scr[p, r, :, 0 : s.proj])
            val = split(kv_scr[p, r, :, s.proj : 2 * s.proj])
            store(key_out, key, p, r)
            score_out[p, r] = dot3(pair_of(q_ref, r), key, NT) - lse_ref[r]
            cot_out[p, r] = dot3(pair_of(g_ref, r), val, NT) - corr_ref[r]


def back(where_ref, *refs, s, nrow):
    q_ref, g_ref, w_ref = refs[:3]
    groups = refs[3 : 3 + nrow]
    sets = [refs[3 + nrow : 6 + nrow], refs[6 + nrow : 9 + nrow]]
    outs = refs[9 + nrow :]
    own_out, terms_out = outs[0], outs[1 : 2 * nrow]
    send_out, keep_out, dq_out, bias_scr, term_scr, spot = outs[2 * nrow :]
    shift = where_ref[0]
    odd = shift & 1
    both = pair_of(w_ref)
    for m, ref in enumerate(groups):
        bias_scr[m] = ref[...]
    dquery = [None] * s.rows
    for p in range(nrow):
        key_ref, score_ref, cot_ref = sets[min(p, 1)]
        at = max(p - 1, 0)
        group = (shift >> 1) ^ p
        bias = bias_scr[group].astype(F32)
        total = None
        grads = []
        for r in range(s.rows):
            query = pair_of(q_ref, r)
            cot = pair_of(g_ref, r)
            probs = jnp.exp(score_ref[at, r] + bias)
            ds = probs * cot_ref[at, r]
            total = ds if total is None else total + ds
            dsp = split(ds)
            part = dot3(dsp, pair_of(key_ref, at, r), NN)
            dquery[r] = part if dquery[r] is None else dquery[r] + part
            grads.append(jnp.concatenate([dot3(dsp, query, TN), dot3(split(probs), cot, TN)], axis=1))
        spot[group] = total
        term = dot3(split(jnp.concatenate(grads, axis=0)), both, NT)
        term_scr[p] = term.reshape(s.rows, s.two, s.width)
        for slot in range(2):
            value = jnp.concatenate(
                [term_scr[p, r, pl.ds((odd ^ slot) * s.cols, s.cols)] for r in range(s.rows)], axis=0
            )
            if p == 0 and slot == 0:
                own_out[...] = value
            else:
                encode(terms_out[2 * p + slot - 1], value)
    for r in range(s.rows):
        dq_out[r] = dquery[r]
    for p in range(nrow // 2):
        low, high = spot[2 * p], spot[2 * p + 1]
        keep_out[p] = half_join(low, pltpu.roll(high, s.cols, 1), s.cols)
        send_out[p] = half_join(pltpu.roll(low, s.cols, 1), high, s.cols)


def middle(keep_ref, got_ref, *outs, s, nrow):
    half = s.wide // 2
    for m in range(nrow):
        total = keep_ref[m // 2] + got_ref[m // 2]
        if m == 0:
            outs[0][...] = total
            continue
        top, bottom = total[:half], total[half:]
        if m % 2:
            top = pltpu.roll(top, s.cols, 1)
        else:
            bottom = pltpu.roll(bottom, s.cols, 1)
        encode(outs[m], half_join(top, bottom, s.cols))


def tail(dq_ref, wq_ref, out_ref, *, s):
    fold_mask = lax.broadcasted_iota(jnp.int32, (s.cols, s.proj), 1) // s.head_dim
    rows = []
    for r in range(s.rows):
        out = dq_ref[r, 0 : s.cols]
        for head in range(1, s.heads):
            out = jnp.where(fold_mask == head, dq_ref[r, head * s.cols : (head + 1) * s.cols], out)
        rows.append(out)
    dq = jnp.concatenate(rows, axis=0) * (s.head_dim ** (-0.5))
    out_ref[...] = dot3(split(dq), pair_of(wq_ref), NT).reshape(s.rows, s.cols, s.width)


def finish(own_ref, sum_ref, *refs, s, ncol, nrow):
    terms, parts = refs[: ncol - 1], refs[ncol - 1 : ncol + nrow - 2]
    key_out, bias_out = refs[ncol + nrow - 2 :]
    total = own_ref[...]
    for ref in terms:
        total = total + decode(ref)
    key_out[...] = total.reshape(s.rows, s.cols, s.width)
    total = None
    for ref in parts:
        value = decode(ref)
        total = value if total is None else total + value
    half = s.wide // 2
    whole = sum_ref[...]
    whole = jnp.concatenate([whole[:half] + total, whole[half:] + pltpu.roll(total, s.cols, 1)], axis=0)
    for head in range(s.heads):
        bias_out[head] = whole[head * s.cols : (head + 1) * s.cols, 0 : s.cols]


def xor_pairs(size, mask):
    return [(i, i ^ mask) for i in range(size)]


def here(x):
    return pltpu.with_memory_space_constraint(x, pltpu.VMEM)


def call(body, outs, args, scratch=(), scalar=False, inputs=pltpu.VMEM):
    specs = [pl.BlockSpec(memory_space=inputs)] * len(args)
    vmem = pl.BlockSpec(memory_space=pltpu.VMEM)
    if scalar:
        specs[0] = pl.BlockSpec(memory_space=pltpu.SMEM)
    return pl.pallas_call(
        body,
        out_shape=outs,
        in_specs=specs,
        out_specs=[vmem] * len(outs),
        scratch_shapes=list(scratch),
        compiler_params=pltpu.CompilerParams(vmem_limit_bytes=16 << 20),
    )(*args)


def on_device(ncol, nrow, nsub, pair, w_query, w_key, w_value, bias, grad_out, log_total, row_corr):
    if nsub != 2 or ncol != 2 * nrow:
        raise ValueError("mesh shape")
    rows, cols, width = pair.shape
    heads = log_total.shape[0]
    s = Shape(rows, cols, width, heads, w_query.shape[1] // heads)

    def move(x, axis, size, mask):
        return lax.ppermute(x, axis, xor_pairs(size, mask))

    blocks = [here(move(pair, "col", ncol, k)) for k in range(1, ncol)]
    other = here(move(bias, "sub", nsub, 1))
    (packed,) = call(functools.partial(pack, s=s), [pltpu.VMEM((s.wide, s.two), BF16)], [here(bias), other])
    groups = [here(packed)] + [here(move(packed, "row", nrow, k)) for k in range(1, nrow)]
    place = lax.axis_index("col") ^ (lax.axis_index("row") * nsub + lax.axis_index("sub"))
    place = place.reshape(1)
    spread = pltpu.VMEM((2, rows, s.wide, s.proj), BF16)
    wide = pltpu.VMEM((rows, s.wide, s.two), F32)
    params = [pair, w_query, w_key, w_value, grad_out, log_total, row_corr]
    q, g, wq, w_both, lse, corr, kv = map(
        here,
        call(
            functools.partial(prep, s=s),
            [
                spread,
                spread,
                pltpu.VMEM((2, width, s.proj), BF16),
                pltpu.VMEM((2, width, 2 * s.proj), BF16),
                wide,
                wide,
                pltpu.VMEM((s.flat, 2 * s.proj), F32),
            ],
            [pltpu.with_memory_space_constraint(x, pltpu.HBM) for x in params],
            scratch=[pltpu.VMEM(x.shape, F32) for x in params]
            + [pltpu.SemaphoreType.DMA((len(params),))],
            inputs=pl.ANY,
        ),
    )
    common = [q, g, w_both, lse, corr]
    total_shape = pltpu.VMEM((s.wide, s.two), F32)
    dq_shape = pltpu.VMEM((rows, s.wide, s.proj), F32)
    own_shape = pltpu.VMEM((s.flat, width), F32)
    term_shape = pltpu.VMEM((s.flat + 16, width), BF16)

    def score(members, pairs, own):
        grid = pltpu.VMEM((pairs, rows, s.wide, s.two), F32)
        outs = call(
            functools.partial(scores, s=s, pairs=pairs, own=own),
            [pltpu.VMEM((2, pairs, rows, s.two, s.proj), BF16), grid, grid],
            [place, *common, *members],
            scratch=[pltpu.VMEM((pairs, rows, s.two, 2 * s.proj), F32)],
            scalar=True,
        )
        return [here(x) for x in outs]

    sets = [*score([kv, blocks[0]], 1, True), *score(blocks[1:], nrow - 1, False)]
    ends = pltpu.VMEM((nrow // 2, s.wide, s.two), F32)
    own, *terms, send, keep, dq = call(
        functools.partial(back, s=s, nrow=nrow),
        [own_shape] + [term_shape] * (ncol - 1) + [ends, ends, dq_shape],
        [place, *common[:3], *groups, *sets],
        scratch=[
            pltpu.VMEM((nrow, s.wide, s.two), BF16),
            pltpu.VMEM((nrow, rows, s.two, width), F32),
            pltpu.VMEM((nrow, s.wide, s.two), F32),
        ],
        scalar=True,
    )
    got = [here(move(terms[k - 1], "col", ncol, k)) for k in range(1, ncol)]
    swapped = here(move(send, "sub", nsub, 1))
    summed, *sums = call(
        functools.partial(middle, s=s, nrow=nrow),
        [total_shape] + [pltpu.VMEM((s.wide // 2 + 16, s.two), BF16)] * (nrow - 1),
        [here(keep), swapped],
    )
    dgot = [here(move(sums[k - 1], "row", nrow, k)) for k in range(1, nrow)]
    part = jax.ShapeDtypeStruct((rows, cols, width), F32)
    (query_grad,) = call(functools.partial(tail, s=s), [part], [here(dq), wq])
    key_grad, bias_grad = call(
        functools.partial(finish, s=s, ncol=ncol, nrow=nrow),
        [part, jax.ShapeDtypeStruct((heads, cols, cols), F32)],
        [here(own), here(summed), *got, *dgot],
    )
    return query_grad, key_grad, bias_grad


def solution(mesh):
    size = mesh.shape
    placed = (
        P(("groups", "row", "sub"), "col", None),
        P(),
        P(),
        P(),
        P("groups", "col", ("row", "sub")),
        P(("groups", "row", "sub"), "col", None),
        P(None, ("groups", "row", "sub"), "col"),
        P(None, ("groups", "row", "sub"), "col"),
    )
    return jax.shard_map(
        functools.partial(on_device, size["col"], size["row"], size["sub"]),
        mesh=mesh,
        in_specs=placed,
        out_specs=(
            P(("groups", "row", "sub"), "col", None),
            P(("groups", "row", "sub"), "col", None),
            P("groups", "col", ("row", "sub")),
        ),
        check_vma=False,
    )
```

time: 89.3 us -> 25.5 us (0.29)
  waiting for transfers between devices: 38.3 us -> 4.31 us
  blocking collectives: 21.4 us -> 0 us
  between operations: 14.3 us -> 0.71 us
  starting transfers between devices: 0.08 us -> 13.4 us
  local copies, waits for them, and re-layouts: 8.2 us -> 0.84 us
  matrix products: 6.56 us -> 0 us
  Pallas kernels: 0 us -> 5.95 us
    all_gather x2 -> x0, blocking collectives: 21.4 us -> none  [the longest x1 15.6 us: on_device(): lax.all_gather(pair, 'col', axis=1, tiled=True)]
    reduce_scatter x1 -> x0, waiting for transfers between devices: 21.2 us -> none  [on_device(): lax.psum_scatter(terms, 'col', scatter_dimension=1, tiled=True)]
    unnamed x3 -> x0, waiting for transfers between devices: 17.1 us -> none
    ppermute x0 -> x10, starting transfers between devices: none -> 13.4 us  [move(): return lax.ppermute(x, axis, xor_pairs(size, mask))]
    dot_general x14 -> x0, matrix products: 6.56 us -> none  [the longest x1 1.28 us: on_device(): terms = jnp.einsum('rkd,cd->rkc', dkv_all, w_both, precision=HIGH)]
    pallas_call x0 -> x8, Pallas kernels: none -> 5.95 us  [call(): pl.pallas_call(body, out_shape=outs, in_specs=specs, out_specs=[vmem] * l...]
    unnamed x19 -> x2, local copies, waits for them, and re-layouts: 6.37 us -> 0.84 us
    ppermute x0 -> x10, waiting for transfers between devices: none -> 4.31 us  [move(): return lax.ppermute(x, axis, xor_pairs(size, mask))]
  transfers between devices with their start and end apart: 2 -> 10, of which waited for: 2 -> 2; matrix products, arithmetic and copies ran while one was open for 7% -> 0% of each run, Pallas kernels for 0% -> 15%
where the time goes in v4:
time: 25.5 us; the launch traced here: 25.2 us
  starting transfers between devices  13.4 us (53%)
  Pallas kernels  5.95 us (23%)
  waiting for transfers between devices  4.31 us (17%)
  local copies, waits for them, and re-layouts  0.84 us (3%)
  between operations  0.71 us (3%)
    ppermute x10, starting transfers between devices, move(): return lax.ppermute(x, axis, xor_pairs(size, mask))  13.4 us
    pallas_call x8, Pallas kernels, call(): pl.pallas_call(body, out_shape=outs, in_specs=specs, out_specs=[vmem] * l...  5.95 us
    ppermute x10, waiting for transfers between devices, move(): return lax.ppermute(x, axis, xor_pairs(size, mask))  4.31 us
    unnamed x2, local copies, waits for them, and re-layouts  0.84 us
  transfers between devices with their start and end apart: 10, of which 2 were waited for; matrix products, arithmetic and copies ran while one was open for 0% of the time, Pallas kernels for 15%

profile of v4, /device:TPU:0, one launch (start us, length us, event | category | flops | bytes accessed | tf_op | source)
XLA Modules:
  0.0 25.2 jit_solution(7544819129353433548)
XLA Ops:
  0.6 0.6 %collective-permute-start = (bf16[4,64,64]{2,1,0:T(8,128)(2,1)}, bf16[4,64,64]{2,1,0:T(8,128)(2,1)S(1)}, u32[]{:S(2)}, u32[]{:S(2)}) collective-permute-start(bf16[4,64,64]{2,1,0:T(8,128)(2,1)} %own_ref.1), channel_id=1, source_target_pairs={{0,1},{1,0},{2,3},{3,2},{4,5},{5,4},{6,7},{7,6},{8,9},{9,8},{10,11... | collective-permute-start | bytes 98312 | tf_op jit(solution)/shard_map/ppermute | solution.py:274
  1.2 2.6 %collective-permute-start.2 = (f32[2,64,128]{2,1,0:T(8,128)}, f32[2,64,128]{2,1,0:T(8,128)S(1)}, u32[]{:S(2)}, u32[]{:S(2)}) collective-permute-start(f32[2,64,128]{2,1,0:T(8,128)} %refs_0_.1), channel_id=1, source_target_pairs={{0,4},{4,0},{8,12},{12,8},{1,5},{5,1},{9,13},{13,9},{2,6},{6,2},{1... | collective-permute-start | bytes 196616 | tf_op jit(solution)/shard_map/ppermute | solution.py:274
  3.8 2.5 %collective-permute-start.4 = (f32[2,64,128]{2,1,0:T(8,128)}, f32[2,64,128]{2,1,0:T(8,128)S(1)}, u32[]{:S(2)}, u32[]{:S(2)}) collective-permute-start(f32[2,64,128]{2,1,0:T(8,128)} %refs_0_.1), channel_id=1, source_target_pairs={{0,12},{4,8},{8,4},{12,0},{1,13},{5,9},{9,5},{13,1},{2,14},{6,10},... | collective-permute-start | bytes 196616 | tf_op jit(solution)/shard_map/ppermute | solution.py:274
  6.3 0.1 collective-permute-start.3
  6.4 0.0 collective-permute-done.other_ref
  6.4 0.8 %copy-done = bf16[4,64,64]{2,1,0:T(8,128)(2,1)S(1)} copy-done((bf16[4,64,64]{2,1,0:T(8,128)(2,1)S(1)}, bf16[4,64,64]{2,1,0:T(8,128)(2,1)}, u32[]{:S(2)}) %copy-start) | copy-done | bytes 32792
  7.3 0.1 shard_map.104.refs_3_
  7.4 1.6 %collective-permute-start.1 = (bf16[256,128]{1,0:T(8,128)(2,1)S(1)}, bf16[256,128]{1,0:T(8,128)(2,1)S(1)}, u32[]{:S(2)}, u32[]{:S(2)}) collective-permute-start(bf16[256,128]{1,0:T(8,128)(2,1)S(1)} %shard_map.104.refs_3_), channel_id=1, source_target_pairs={{0,2},{2,0},{1,3},{3,1},{4,6},{6,4},{5,7},{7,5},{8,10},{10,8},{9,1... | collective-permute-start | bytes 196616 | tf_op jit(solution)/shard_map/ppermute | solution.py:274
  8.9 1.4 %shard_map.103 = (bf16[2,2,256,128]{3,2,1,0:T(8,128)(2,1)S(1)}, bf16[2,2,256,128]{3,2,1,0:T(8,128)(2,1)S(1)}, bf16[2,128,128]{2,1,0:T(8,128)(2,1)S(1)}, bf16[2,1...) custom-call(f32[2,64,128]{2,1,0:T(8,128)} %refs_0_.1, ...), custom_call_target="tpu_custom_call" | custom-call | tf_op jit(solution)/shard_map/pallas_call | solution.py:256
  10.4 0.0 collective-permute-done.2.refs_6_
  10.4 0.6 %shard_map.105 = (bf16[2,1,2,128,128]{4,3,2,1,0:T(8,128)(2,1)S(1)}, f32[1,2,256,128]{3,2,1,0:T(8,128)S(1)}, f32[1,2,256,128]{3,2,1,0:T(8,128)S(1)}) custom-call(s32[1]{0:T(128)} %bitcast.where_ref, bf16[2,2,256,128]{3,2,1,0:T(8,128)(2,1)S(1)} %get-tuple-element.27.refs_0_, bf16[2,2,256,128]{3,2,1,0:T(8,128)(2,1)S(1)} %get-tuple-element.28.refs_1_, ...), custom_call_target="tpu_custom_call" | custom-call | tf_op jit(solution)/shard_map/pallas_call | solution.py:256
  11.0 0.0 collective-permute-done.4.refs_6_
  11.0 2.3 %collective-permute-done.3.refs_5_ = f32[2,64,128]{2,1,0:T(8,128)S(1)} collective-permute-done((f32[2,64,128]{2,1,0:T(8,128)}, f32[2,64,128]{2,1,0:T(8,128)S(1)}, u32[]{:S(2)}, u32[]{:S(2)}) %collective-permute-start.3) | collective-permute-done | bytes 65568 | tf_op jit(solution)/shard_map/ppermute | solution.py:274
  13.3 0.6 %shard_map.106 = (bf16[2,1,2,128,128]{4,3,2,1,0:T(8,128)(2,1)S(1)}, f32[1,2,256,128]{3,2,1,0:T(8,128)S(1)}, f32[1,2,256,128]{3,2,1,0:T(8,128)S(1)}) custom-call(s32[1]{0:T(128)} %bitcast.where_ref, bf16[2,2,256,128]{3,2,1,0:T(8,128)(2,1)S(1)} %get-tuple-element.27.refs_0_, bf16[2,2,256,128]{3,2,1,0:T(8,128)(2,1)S(1)} %get-tuple-element.28.refs_1_, ...), custom_call_target="tpu_custom_call" | custom-call | tf_op jit(solution)/shard_map/pallas_call | solution.py:256
  13.9 1.1 %shard_map.107 = (f32[128,128]{1,0:T(8,128)S(1)}, bf16[144,128]{1,0:T(8,128)(2,1)S(1)}, bf16[144,128]{1,0:T(8,128)(2,1)S(1)}, bf16[144,128]{1,0:T(8,128)(2,1)S(1...) custom-call(s32[1]{0:T(128)} %bitcast.where_ref, ...), custom_call_target="tpu_custom_call" | custom-call | tf_op jit(solution)/shard_map/pallas_call | solution.py:256
  15.1 0.1 collective-permute-start.5
  15.2 0.0 collective-permute-start.6
  15.2 3.3 %collective-permute-start.7 = (bf16[144,128]{1,0:T(8,128)(2,1)S(1)}, bf16[144,128]{1,0:T(8,128)(2,1)S(1)}, u32[]{:S(2)}, u32[]{:S(2)}) collective-permute-start(bf16[144,128]{1,0:T(8,128)(2,1)S(1)} %get-tuple-element.46), channel_id=1, source_target_pairs={{0,8},{4,12},{8,0},{12,4},{1,9},{5,13},{9,1},{13,5},{2,10},{6,14},... | collective-permute-start | bytes 110600 | tf_op jit(solution)/shard_map/ppermute | solution.py:274
  18.5 1.1 %collective-permute-start.8 = (bf16[144,128]{1,0:T(8,128)(2,1)S(1)}, bf16[144,128]{1,0:T(8,128)(2,1)S(1)}, u32[]{:S(2)}, u32[]{:S(2)}) collective-permute-start(bf16[144,128]{1,0:T(8,128)(2,1)S(1)} %get-tuple-element.47), channel_id=1, source_target_pairs={{0,12},{4,8},{8,4},{12,0},{1,13},{5,9},{9,5},{13,1},{2,14},{6,10},... | collective-permute-start | bytes 110600 | tf_op jit(solution)/shard_map/ppermute | solution.py:274
  19.6 0.2 shard_map.109
  19.8 1.6 %collective-permute-start.9 = (bf16[144,128]{1,0:T(8,128)(2,1)S(1)}, bf16[144,128]{1,0:T(8,128)(2,1)S(1)}, u32[]{:S(2)}, u32[]{:S(2)}) collective-permute-start(bf16[144,128]{1,0:T(8,128)(2,1)S(1)} %get-tuple-element.48), channel_id=1, source_target_pairs={{0,2},{2,0},{1,3},{3,1},{4,6},{6,4},{5,7},{7,5},{8,10},{10,8},{9,1... | collective-permute-start | bytes 110600 | tf_op jit(solution)/shard_map/ppermute | solution.py:274
  21.4 0.8 %shard_map.108 = f32[2,64,128]{2,1,0:T(8,128)} custom-call(f32[2,256,128]{2,1,0:T(8,128)S(1)} %get-tuple-element.39.dq_ref, bf16[2,128,128]{2,1,0:T(8,128)(2,1)S(1)} %get-tuple-element.40.wq_ref), custom_call_target="tpu_custom_call" | custom-call | tf_op jit(solution)/shard_map/pallas_call | solution.py:256
  22.2 2.0 %collective-permute-done.8.refs_2_ = bf16[144,128]{1,0:T(8,128)(2,1)S(1)} collective-permute-done((bf16[144,128]{1,0:T(8,128)(2,1)S(1)}, bf16[144,128]{1,0:T(8,128)(2,1)S(1)}, u32[]{:S(2)}, u32[]{:S(2)}) %collective-permute-start.8) | collective-permute-done | bytes 36896 | tf_op jit(solution)/shard_map/ppermute | solution.py:274
  24.2 1.0 %shard_map.110 = (f32[2,64,128]{2,1,0:T(8,128)}, f32[4,64,64]{2,1,0:T(8,128)}) custom-call(f32[128,128]{1,0:T(8,128)S(1)} %get-tuple-element.41.own_ref, f32[256,128]{1,0:T(8,128)S(1)} %get-tuple-element.44.sum_ref, bf16[144,128]{1,0:T(8,128)(2,1)S(1)} %collective-permute-done.6.refs_0_, bf16[144,128]{1,0:T(8,128)(2,1)S(1)} %collective-permute-done.7.refs_1_, ...), custom_call_target="tpu_custom_call" | custom-call | tf_op jit(solution)/shard_map/pallas_call | solution.py:256
  (6 shorter events, 0.0 us)
Async XLA Ops:
  0.6 5.8 %collective-permute-start = (bf16[4,64,64]{2,1,0:T(8,128)(2,1)}, bf16[4,64,64]{2,1,0:T(8,128)(2,1)S(1)}, u32[]{:S(2)}, u32[]{:S(2)}) collective-permute-start(bf16[4,64,64]{2,1,0:T(8,128)(2,1)} %own_ref.1), channel_id=1, source_target_pairs={{0,1},{1,0},{2,3},{3,2},{4,5},{5,4},{6,7},{7,6},{8,9},{9,8},{10,11... | collective-permute-start | bytes 98312 | tf_op jit(solution)/shard_map/ppermute | solution.py:274
  1.2 9.2 %collective-permute-start.2 = (f32[2,64,128]{2,1,0:T(8,128)}, f32[2,64,128]{2,1,0:T(8,128)S(1)}, u32[]{:S(2)}, u32[]{:S(2)}) collective-permute-start(f32[2,64,128]{2,1,0:T(8,128)} %refs_0_.1), channel_id=1, source_target_pairs={{0,4},{4,0},{8,12},{12,8},{1,5},{5,1},{9,13},{13,9},{2,6},{6,2},{1... | collective-permute-start | bytes 196616 | tf_op jit(solution)/shard_map/ppermute | solution.py:274
  3.8 7.2 %collective-permute-start.4 = (f32[2,64,128]{2,1,0:T(8,128)}, f32[2,64,128]{2,1,0:T(8,128)S(1)}, u32[]{:S(2)}, u32[]{:S(2)}) collective-permute-start(f32[2,64,128]{2,1,0:T(8,128)} %refs_0_.1), channel_id=1, source_target_pairs={{0,12},{4,8},{8,4},{12,0},{1,13},{5,9},{9,5},{13,1},{2,14},{6,10},... | collective-permute-start | bytes 196616 | tf_op jit(solution)/shard_map/ppermute | solution.py:274
  6.3 7.0 %collective-permute-start.3 = (f32[2,64,128]{2,1,0:T(8,128)}, f32[2,64,128]{2,1,0:T(8,128)S(1)}, u32[]{:S(2)}, u32[]{:S(2)}) collective-permute-start(f32[2,64,128]{2,1,0:T(8,128)} %refs_0_.1), channel_id=1, source_target_pairs={{0,8},{4,12},{8,0},{12,4},{1,9},{5,13},{9,1},{13,5},{2,10},{6,14},... | collective-permute-start | bytes 196616 | tf_op jit(solution)/shard_map/ppermute | solution.py:274
  6.4 0.8 %copy-start = (bf16[4,64,64]{2,1,0:T(8,128)(2,1)S(1)}, bf16[4,64,64]{2,1,0:T(8,128)(2,1)}, u32[]{:S(2)}) copy-start(bf16[4,64,64]{2,1,0:T(8,128)(2,1)} %own_ref.1) | copy-start | bytes 98308
  7.4 6.6 %collective-permute-start.1 = (bf16[256,128]{1,0:T(8,128)(2,1)S(1)}, bf16[256,128]{1,0:T(8,128)(2,1)S(1)}, u32[]{:S(2)}, u32[]{:S(2)}) collective-permute-start(bf16[256,128]{1,0:T(8,128)(2,1)S(1)} %shard_map.104.refs_3_), channel_id=1, source_target_pairs={{0,2},{2,0},{1,3},{3,1},{4,6},{6,4},{5,7},{7,5},{8,10},{10,8},{9,1... | collective-permute-start | bytes 196616 | tf_op jit(solution)/shard_map/ppermute | solution.py:274
  15.1 4.5 %collective-permute-start.5 = (f32[1,256,128]{2,1,0:T(8,128)S(1)}, f32[1,256,128]{2,1,0:T(8,128)S(1)}, u32[]{:S(2)}, u32[]{:S(2)}) collective-permute-start(f32[1,256,128]{2,1,0:T(8,128)S(1)} %get-tuple-element.43), channel_id=1, source_target_pairs={{0,1},{1,0},{2,3},{3,2},{4,5},{5,4},{6,7},{7,6},{8,9},{9,8},{10,11... | collective-permute-start | bytes 393224 | tf_op jit(solution)/shard_map/ppermute | solution.py:274
  15.2 7.0 %collective-permute-start.6 = (bf16[144,128]{1,0:T(8,128)(2,1)S(1)}, bf16[144,128]{1,0:T(8,128)(2,1)S(1)}, u32[]{:S(2)}, u32[]{:S(2)}) collective-permute-start(bf16[144,128]{1,0:T(8,128)(2,1)S(1)} %get-tuple-element.45), channel_id=1, source_target_pairs={{0,4},{4,0},{8,12},{12,8},{1,5},{5,1},{9,13},{13,9},{2,6},{6,2},{1... | collective-permute-start | bytes 110600 | tf_op jit(solution)/shard_map/ppermute | solution.py:274
  15.2 7.0 %collective-permute-start.7 = (bf16[144,128]{1,0:T(8,128)(2,1)S(1)}, bf16[144,128]{1,0:T(8,128)(2,1)S(1)}, u32[]{:S(2)}, u32[]{:S(2)}) collective-permute-start(bf16[144,128]{1,0:T(8,128)(2,1)S(1)} %get-tuple-element.46), channel_id=1, source_target_pairs={{0,8},{4,12},{8,0},{12,4},{1,9},{5,13},{9,1},{13,5},{2,10},{6,14},... | collective-permute-start | bytes 110600 | tf_op jit(solution)/shard_map/ppermute | solution.py:274
  18.5 5.8 %collective-permute-start.8 = (bf16[144,128]{1,0:T(8,128)(2,1)S(1)}, bf16[144,128]{1,0:T(8,128)(2,1)S(1)}, u32[]{:S(2)}, u32[]{:S(2)}) collective-permute-start(bf16[144,128]{1,0:T(8,128)(2,1)S(1)} %get-tuple-element.47), channel_id=1, source_target_pairs={{0,12},{4,8},{8,4},{12,0},{1,13},{5,9},{9,5},{13,1},{2,14},{6,10},... | collective-permute-start | bytes 110600 | tf_op jit(solution)/shard_map/ppermute | solution.py:274
  19.8 4.4 %collective-permute-start.9 = (bf16[144,128]{1,0:T(8,128)(2,1)S(1)}, bf16[144,128]{1,0:T(8,128)(2,1)S(1)}, u32[]{:S(2)}, u32[]{:S(2)}) collective-permute-start(bf16[144,128]{1,0:T(8,128)(2,1)S(1)} %get-tuple-element.48), channel_id=1, source_target_pairs={{0,2},{2,0},{1,3},{3,1},{4,6},{6,4},{5,7},{7,5},{8,10},{10,8},{9,1... | collective-permute-start | bytes 110600 | tf_op jit(solution)/shard_map/ppermute | solution.py:274

commit v5 on v4

--- a/solution.py
+++ b/solution.py
@@ -65,9 +65,7 @@
     rows = ref.shape[0] - 16
     code = ref[0:rows].astype(F32)
     top = ref[rows : rows + 16].astype(F32)[0:1]
-    size = jnp.abs(code)
-    for _ in range(4):
-        size = jnp.sqrt(size)
+    size = jnp.exp2(jnp.log2(jnp.abs(code)) * 0.0625)
     return jnp.where(code < 0, -size, size) * (top * (1.0 / LEVEL))
 
 
@@ -224,11 +222,13 @@
 
 def finish(own_ref, sum_ref, *refs, s, ncol, nrow):
     terms, parts = refs[: ncol - 1], refs[ncol - 1 : ncol + nrow - 2]
-    key_out, bias_out = refs[ncol + nrow - 2 :]
+    key_hbm, bias_hbm, key_out, bias_out, sem = refs[ncol + nrow - 2 :]
     total = own_ref[...]
     for ref in terms:
         total = total + decode(ref)
     key_out[...] = total.reshape(s.rows, s.cols, s.width)
+    key_copy = pltpu.make_async_copy(key_out, key_hbm, sem.at[0])
+    key_copy.start()
     total = None
     for ref in parts:
         value = decode(ref)
@@ -238,6 +238,10 @@
     whole = jnp.concatenate([whole[:half] + total, whole[half:] + pltpu.roll(total, s.cols, 1)], axis=0)
     for head in range(s.heads):
         bias_out[head] = whole[head * s.cols : (head + 1) * s.cols, 0 : s.cols]
+    bias_copy = pltpu.make_async_copy(bias_out, bias_hbm, sem.at[1])
+    bias_copy.start()
+    key_copy.wait()
+    bias_copy.wait()
 
 
 def xor_pairs(size, mask):
@@ -248,16 +252,15 @@
     return pltpu.with_memory_space_constraint(x, pltpu.VMEM)
 
 
-def call(body, outs, args, scratch=(), scalar=False, inputs=pltpu.VMEM):
+def call(body, outs, args, scratch=(), scalar=False, inputs=pltpu.VMEM, outputs=pltpu.VMEM):
     specs = [pl.BlockSpec(memory_space=inputs)] * len(args)
-    vmem = pl.BlockSpec(memory_space=pltpu.VMEM)
     if scalar:
         specs[0] = pl.BlockSpec(memory_space=pltpu.SMEM)
     return pl.pallas_call(
         body,
         out_shape=outs,
         in_specs=specs,
-        out_specs=[vmem] * len(outs),
+        out_specs=[pl.BlockSpec(memory_space=outputs)] * len(outs),
         scratch_shapes=list(scratch),
         compiler_params=pltpu.CompilerParams(vmem_limit_bytes=16 << 20),
     )(*args)
@@ -343,8 +346,14 @@
     (query_grad,) = call(functools.partial(tail, s=s), [part], [here(dq), wq])
     key_grad, bias_grad = call(
         functools.partial(finish, s=s, ncol=ncol, nrow=nrow),
-        [part, jax.ShapeDtypeStruct((heads, cols, cols), F32)],
+        [pltpu.HBM((rows, cols, width), F32), pltpu.HBM((heads, cols, cols), F32)],
         [here(own), here(summed), *got, *dgot],
+        scratch=[
+            pltpu.VMEM((rows, cols, width), F32),
+            pltpu.VMEM((heads, cols, cols), F32),
+            pltpu.SemaphoreType.DMA((2,)),
+        ],
+        outputs=pl.ANY,
     )
     return query_grad, key_grad, bias_grad
 

time: 25.5 us -> 25.3 us (level)
  no operation moved by 1% of the time
where the time goes in v5:
time: 25.3 us; the launch traced here: 25 us
  starting transfers between devices  13.4 us (53%)
  Pallas kernels  5.75 us (23%)
  waiting for transfers between devices  4.31 us (17%)
  local copies, waits for them, and re-layouts  0.84 us (3%)
  between operations  0.71 us (3%)
    ppermute x10, starting transfers between devices, move(): return lax.ppermute(x, axis, xor_pairs(size, mask))  13.4 us
    pallas_call x8, Pallas kernels, call(): pl.pallas_call(body, out_shape=outs, in_specs=specs, out_specs=[pl.BlockS...  5.75 us
    ppermute x10, waiting for transfers between devices, move(): return lax.ppermute(x, axis, xor_pairs(size, mask))  4.31 us
    unnamed x2, local copies, waits for them, and re-layouts  0.84 us
  transfers between devices with their start and end apart: 10, of which 2 were waited for; matrix products, arithmetic and copies ran while one was open for 0% of the time, Pallas kernels for 15%

profile of v5, /device:TPU:0, one launch (start us, length us, event | category | flops | bytes accessed | tf_op | source)
XLA Modules:
  0.0 25.0 jit_solution(15641492708279054783)
XLA Ops:
  0.6 0.6 %collective-permute-start = (bf16[4,64,64]{2,1,0:T(8,128)(2,1)}, bf16[4,64,64]{2,1,0:T(8,128)(2,1)S(1)}, u32[]{:S(2)}, u32[]{:S(2)}) collective-permute-start(bf16[4,64,64]{2,1,0:T(8,128)(2,1)} %own_ref.1), channel_id=1, source_target_pairs={{0,1},{1,0},{2,3},{3,2},{4,5},{5,4},{6,7},{7,6},{8,9},{9,8},{10,11... | collective-permute-start | bytes 98312 | tf_op jit(solution)/shard_map/ppermute | solution.py:277
  1.2 2.6 %collective-permute-start.2 = (f32[2,64,128]{2,1,0:T(8,128)}, f32[2,64,128]{2,1,0:T(8,128)S(1)}, u32[]{:S(2)}, u32[]{:S(2)}) collective-permute-start(f32[2,64,128]{2,1,0:T(8,128)} %refs_0_.1), channel_id=1, source_target_pairs={{0,4},{4,0},{8,12},{12,8},{1,5},{5,1},{9,13},{13,9},{2,6},{6,2},{1... | collective-permute-start | bytes 196616 | tf_op jit(solution)/shard_map/ppermute | solution.py:277
  3.8 2.5 %collective-permute-start.4 = (f32[2,64,128]{2,1,0:T(8,128)}, f32[2,64,128]{2,1,0:T(8,128)S(1)}, u32[]{:S(2)}, u32[]{:S(2)}) collective-permute-start(f32[2,64,128]{2,1,0:T(8,128)} %refs_0_.1), channel_id=1, source_target_pairs={{0,12},{4,8},{8,4},{12,0},{1,13},{5,9},{9,5},{13,1},{2,14},{6,10},... | collective-permute-start | bytes 196616 | tf_op jit(solution)/shard_map/ppermute | solution.py:277
  6.3 0.1 collective-permute-start.3
  6.4 0.0 collective-permute-done.other_ref
  6.4 0.8 %copy-done = bf16[4,64,64]{2,1,0:T(8,128)(2,1)S(1)} copy-done((bf16[4,64,64]{2,1,0:T(8,128)(2,1)S(1)}, bf16[4,64,64]{2,1,0:T(8,128)(2,1)}, u32[]{:S(2)}) %copy-start) | copy-done | bytes 32792
  7.3 0.1 shard_map.104.refs_3_
  7.4 1.6 %collective-permute-start.1 = (bf16[256,128]{1,0:T(8,128)(2,1)S(1)}, bf16[256,128]{1,0:T(8,128)(2,1)S(1)}, u32[]{:S(2)}, u32[]{:S(2)}) collective-permute-start(bf16[256,128]{1,0:T(8,128)(2,1)S(1)} %shard_map.104.refs_3_), channel_id=1, source_target_pairs={{0,2},{2,0},{1,3},{3,1},{4,6},{6,4},{5,7},{7,5},{8,10},{10,8},{9,1... | collective-permute-start | bytes 196616 | tf_op jit(solution)/shard_map/ppermute | solution.py:277
  8.9 1.4 %shard_map.103 = (bf16[2,2,256,128]{3,2,1,0:T(8,128)(2,1)S(1)}, bf16[2,2,256,128]{3,2,1,0:T(8,128)(2,1)S(1)}, bf16[2,128,128]{2,1,0:T(8,128)(2,1)S(1)}, bf16[2,1...) custom-call(f32[2,64,128]{2,1,0:T(8,128)} %refs_0_.1, ...), custom_call_target="tpu_custom_call" | custom-call | tf_op jit(solution)/shard_map/pallas_call | solution.py:259
  10.4 0.0 collective-permute-done.2.refs_6_
  10.4 0.6 %shard_map.105 = (bf16[2,1,2,128,128]{4,3,2,1,0:T(8,128)(2,1)S(1)}, f32[1,2,256,128]{3,2,1,0:T(8,128)S(1)}, f32[1,2,256,128]{3,2,1,0:T(8,128)S(1)}) custom-call(s32[1]{0:T(128)} %bitcast.where_ref, bf16[2,2,256,128]{3,2,1,0:T(8,128)(2,1)S(1)} %get-tuple-element.27.refs_0_, bf16[2,2,256,128]{3,2,1,0:T(8,128)(2,1)S(1)} %get-tuple-element.28.refs_1_, ...), custom_call_target="tpu_custom_call" | custom-call | tf_op jit(solution)/shard_map/pallas_call | solution.py:259
  11.0 0.0 collective-permute-done.4.refs_6_
  11.0 2.3 %collective-permute-done.3.refs_5_ = f32[2,64,128]{2,1,0:T(8,128)S(1)} collective-permute-done((f32[2,64,128]{2,1,0:T(8,128)}, f32[2,64,128]{2,1,0:T(8,128)S(1)}, u32[]{:S(2)}, u32[]{:S(2)}) %collective-permute-start.3) | collective-permute-done | bytes 65568 | tf_op jit(solution)/shard_map/ppermute | solution.py:277
  13.3 0.6 %shard_map.106 = (bf16[2,1,2,128,128]{4,3,2,1,0:T(8,128)(2,1)S(1)}, f32[1,2,256,128]{3,2,1,0:T(8,128)S(1)}, f32[1,2,256,128]{3,2,1,0:T(8,128)S(1)}) custom-call(s32[1]{0:T(128)} %bitcast.where_ref, bf16[2,2,256,128]{3,2,1,0:T(8,128)(2,1)S(1)} %get-tuple-element.27.refs_0_, bf16[2,2,256,128]{3,2,1,0:T(8,128)(2,1)S(1)} %get-tuple-element.28.refs_1_, ...), custom_call_target="tpu_custom_call" | custom-call | tf_op jit(solution)/shard_map/pallas_call | solution.py:259
  13.9 1.1 %shard_map.107 = (f32[128,128]{1,0:T(8,128)S(1)}, bf16[144,128]{1,0:T(8,128)(2,1)S(1)}, bf16[144,128]{1,0:T(8,128)(2,1)S(1)}, bf16[144,128]{1,0:T(8,128)(2,1)S(1...) custom-call(s32[1]{0:T(128)} %bitcast.where_ref, ...), custom_call_target="tpu_custom_call" | custom-call | tf_op jit(solution)/shard_map/pallas_call | solution.py:259
  15.1 0.1 collective-permute-start.5
  15.2 0.0 collective-permute-start.6
  15.2 3.3 %collective-permute-start.7 = (bf16[144,128]{1,0:T(8,128)(2,1)S(1)}, bf16[144,128]{1,0:T(8,128)(2,1)S(1)}, u32[]{:S(2)}, u32[]{:S(2)}) collective-permute-start(bf16[144,128]{1,0:T(8,128)(2,1)S(1)} %get-tuple-element.46), channel_id=1, source_target_pairs={{0,8},{4,12},{8,0},{12,4},{1,9},{5,13},{9,1},{13,5},{2,10},{6,14},... | collective-permute-start | bytes 110600 | tf_op jit(solution)/shard_map/ppermute | solution.py:277
  18.5 1.1 %collective-permute-start.8 = (bf16[144,128]{1,0:T(8,128)(2,1)S(1)}, bf16[144,128]{1,0:T(8,128)(2,1)S(1)}, u32[]{:S(2)}, u32[]{:S(2)}) collective-permute-start(bf16[144,128]{1,0:T(8,128)(2,1)S(1)} %get-tuple-element.47), channel_id=1, source_target_pairs={{0,12},{4,8},{8,4},{12,0},{1,13},{5,9},{9,5},{13,1},{2,14},{6,10},... | collective-permute-start | bytes 110600 | tf_op jit(solution)/shard_map/ppermute | solution.py:277
  19.6 0.2 shard_map.109
  19.8 1.6 %collective-permute-start.9 = (bf16[144,128]{1,0:T(8,128)(2,1)S(1)}, bf16[144,128]{1,0:T(8,128)(2,1)S(1)}, u32[]{:S(2)}, u32[]{:S(2)}) collective-permute-start(bf16[144,128]{1,0:T(8,128)(2,1)S(1)} %get-tuple-element.48), channel_id=1, source_target_pairs={{0,2},{2,0},{1,3},{3,1},{4,6},{6,4},{5,7},{7,5},{8,10},{10,8},{9,1... | collective-permute-start | bytes 110600 | tf_op jit(solution)/shard_map/ppermute | solution.py:277
  21.4 0.8 %shard_map.108 = f32[2,64,128]{2,1,0:T(8,128)} custom-call(f32[2,256,128]{2,1,0:T(8,128)S(1)} %get-tuple-element.39.dq_ref, bf16[2,128,128]{2,1,0:T(8,128)(2,1)S(1)} %get-tuple-element.40.wq_ref), custom_call_target="tpu_custom_call" | custom-call | tf_op jit(solution)/shard_map/pallas_call | solution.py:259
  22.2 2.0 %collective-permute-done.8.refs_2_ = bf16[144,128]{1,0:T(8,128)(2,1)S(1)} collective-permute-done((bf16[144,128]{1,0:T(8,128)(2,1)S(1)}, bf16[144,128]{1,0:T(8,128)(2,1)S(1)}, u32[]{:S(2)}, u32[]{:S(2)}) %collective-permute-start.8) | collective-permute-done | bytes 36896 | tf_op jit(solution)/shard_map/ppermute | solution.py:277
  24.2 0.8 %shard_map.110 = (f32[2,64,128]{2,1,0:T(8,128)}, f32[4,64,64]{2,1,0:T(8,128)}) custom-call(f32[128,128]{1,0:T(8,128)S(1)} %get-tuple-element.41.own_ref, f32[256,128]{1,0:T(8,128)S(1)} %get-tuple-element.44.sum_ref, bf16[144,128]{1,0:T(8,128)(2,1)S(1)} %collective-permute-done.6.refs_0_, bf16[144,128]{1,0:T(8,128)(2,1)S(1)} %collective-permute-done.7.refs_1_, ...), custom_call_target="tpu_custom_call" | custom-call | tf_op jit(solution)/shard_map/pallas_call | solution.py:259
  (6 shorter events, 0.0 us)
Async XLA Ops:
  0.6 5.8 %collective-permute-start = (bf16[4,64,64]{2,1,0:T(8,128)(2,1)}, bf16[4,64,64]{2,1,0:T(8,128)(2,1)S(1)}, u32[]{:S(2)}, u32[]{:S(2)}) collective-permute-start(bf16[4,64,64]{2,1,0:T(8,128)(2,1)} %own_ref.1), channel_id=1, source_target_pairs={{0,1},{1,0},{2,3},{3,2},{4,5},{5,4},{6,7},{7,6},{8,9},{9,8},{10,11... | collective-permute-start | bytes 98312 | tf_op jit(solution)/shard_map/ppermute | solution.py:277
  1.2 9.2 %collective-permute-start.2 = (f32[2,64,128]{2,1,0:T(8,128)}, f32[2,64,128]{2,1,0:T(8,128)S(1)}, u32[]{:S(2)}, u32[]{:S(2)}) collective-permute-start(f32[2,64,128]{2,1,0:T(8,128)} %refs_0_.1), channel_id=1, source_target_pairs={{0,4},{4,0},{8,12},{12,8},{1,5},{5,1},{9,13},{13,9},{2,6},{6,2},{1... | collective-permute-start | bytes 196616 | tf_op jit(solution)/shard_map/ppermute | solution.py:277
  3.8 7.2 %collective-permute-start.4 = (f32[2,64,128]{2,1,0:T(8,128)}, f32[2,64,128]{2,1,0:T(8,128)S(1)}, u32[]{:S(2)}, u32[]{:S(2)}) collective-permute-start(f32[2,64,128]{2,1,0:T(8,128)} %refs_0_.1), channel_id=1, source_target_pairs={{0,12},{4,8},{8,4},{12,0},{1,13},{5,9},{9,5},{13,1},{2,14},{6,10},... | collective-permute-start | bytes 196616 | tf_op jit(solution)/shard_map/ppermute | solution.py:277
  6.3 7.0 %collective-permute-start.3 = (f32[2,64,128]{2,1,0:T(8,128)}, f32[2,64,128]{2,1,0:T(8,128)S(1)}, u32[]{:S(2)}, u32[]{:S(2)}) collective-permute-start(f32[2,64,128]{2,1,0:T(8,128)} %refs_0_.1), channel_id=1, source_target_pairs={{0,8},{4,12},{8,0},{12,4},{1,9},{5,13},{9,1},{13,5},{2,10},{6,14},... | collective-permute-start | bytes 196616 | tf_op jit(solution)/shard_map/ppermute | solution.py:277
  6.4 0.8 %copy-start = (bf16[4,64,64]{2,1,0:T(8,128)(2,1)S(1)}, bf16[4,64,64]{2,1,0:T(8,128)(2,1)}, u32[]{:S(2)}) copy-start(bf16[4,64,64]{2,1,0:T(8,128)(2,1)} %own_ref.1) | copy-start | bytes 98308
  7.4 6.6 %collective-permute-start.1 = (bf16[256,128]{1,0:T(8,128)(2,1)S(1)}, bf16[256,128]{1,0:T(8,128)(2,1)S(1)}, u32[]{:S(2)}, u32[]{:S(2)}) collective-permute-start(bf16[256,128]{1,0:T(8,128)(2,1)S(1)} %shard_map.104.refs_3_), channel_id=1, source_target_pairs={{0,2},{2,0},{1,3},{3,1},{4,6},{6,4},{5,7},{7,5},{8,10},{10,8},{9,1... | collective-permute-start | bytes 196616 | tf_op jit(solution)/shard_map/ppermute | solution.py:277
  15.1 4.5 %collective-permute-start.5 = (f32[1,256,128]{2,1,0:T(8,128)S(1)}, f32[1,256,128]{2,1,0:T(8,128)S(1)}, u32[]{:S(2)}, u32[]{:S(2)}) collective-permute-start(f32[1,256,128]{2,1,0:T(8,128)S(1)} %get-tuple-element.43), channel_id=1, source_target_pairs={{0,1},{1,0},{2,3},{3,2},{4,5},{5,4},{6,7},{7,6},{8,9},{9,8},{10,11... | collective-permute-start | bytes 393224 | tf_op jit(solution)/shard_map/ppermute | solution.py:277
  15.2 7.0 %collective-permute-start.6 = (bf16[144,128]{1,0:T(8,128)(2,1)S(1)}, bf16[144,128]{1,0:T(8,128)(2,1)S(1)}, u32[]{:S(2)}, u32[]{:S(2)}) collective-permute-start(bf16[144,128]{1,0:T(8,128)(2,1)S(1)} %get-tuple-element.45), channel_id=1, source_target_pairs={{0,4},{4,0},{8,12},{12,8},{1,5},{5,1},{9,13},{13,9},{2,6},{6,2},{1... | collective-permute-start | bytes 110600 | tf_op jit(solution)/shard_map/ppermute | solution.py:277
  15.2 7.0 %collective-permute-start.7 = (bf16[144,128]{1,0:T(8,128)(2,1)S(1)}, bf16[144,128]{1,0:T(8,128)(2,1)S(1)}, u32[]{:S(2)}, u32[]{:S(2)}) collective-permute-start(bf16[144,128]{1,0:T(8,128)(2,1)S(1)} %get-tuple-element.46), channel_id=1, source_target_pairs={{0,8},{4,12},{8,0},{12,4},{1,9},{5,13},{9,1},{13,5},{2,10},{6,14},... | collective-permute-start | bytes 110600 | tf_op jit(solution)/shard_map/ppermute | solution.py:277
  18.5 5.8 %collective-permute-start.8 = (bf16[144,128]{1,0:T(8,128)(2,1)S(1)}, bf16[144,128]{1,0:T(8,128)(2,1)S(1)}, u32[]{:S(2)}, u32[]{:S(2)}) collective-permute-start(bf16[144,128]{1,0:T(8,128)(2,1)S(1)} %get-tuple-element.47), channel_id=1, source_target_pairs={{0,12},{4,8},{8,4},{12,0},{1,13},{5,9},{9,5},{13,1},{2,14},{6,10},... | collective-permute-start | bytes 110600 | tf_op jit(solution)/shard_map/ppermute | solution.py:277
  19.8 4.4 %collective-permute-start.9 = (bf16[144,128]{1,0:T(8,128)(2,1)S(1)}, bf16[144,128]{1,0:T(8,128)(2,1)S(1)}, u32[]{:S(2)}, u32[]{:S(2)}) collective-permute-start(bf16[144,128]{1,0:T(8,128)(2,1)S(1)} %get-tuple-element.48), channel_id=1, source_target_pairs={{0,2},{2,0},{1,3},{3,1},{4,6},{6,4},{5,7},{7,5},{8,10},{10,8},{9,1... | collective-permute-start | bytes 110600 | tf_op jit(solution)/shard_map/ppermute | solution.py:277

commit v6 on v5

--- a/solution.py
+++ b/solution.py
@@ -29,6 +29,10 @@
     size = b[0].shape[axis]
     both = one(a[0], jnp.concatenate(b, axis=axis), dims)
     return both[:, :size] + both[:, size:] + one(a[1], b[0], dims)
+
+
+def dot3_plain(a, b, dims):
+    return one(a[0], b[0], dims) + one(a[0], b[1], dims) + one(a[1], b[0], dims)
 
 
 def pair_of(ref, *index):
@@ -74,9 +78,12 @@
     return jnp.where(lane < width, low, high)
 
 
-def pack(own_ref, other_ref, out_ref, *, s):
+def pack(own_hbm, other_ref, out_ref, own_ref, sem, *, s):
+    copy = pltpu.make_async_copy(own_hbm, own_ref, sem.at[0])
+    copy.start()
+    out_ref[:, s.cols : s.two] = other_ref[...].reshape(s.wide, s.cols)
+    copy.wait()
     out_ref[:, 0 : s.cols] = own_ref[...].reshape(s.wide, s.cols)
-    out_ref[:, s.cols : s.two] = other_ref[...].reshape(s.wide, s.cols)
 
 
 def prep(*refs, s):
@@ -121,7 +128,7 @@
 
 
 def from_block(s, ref):
-    return lambda both: dot3(split(ref[...].reshape(s.flat, s.width)), both, NN)
+    return lambda both: dot3_plain(split(ref[...].reshape(s.flat, s.width)), both, NN)
 
 
 def scores(where_ref, *refs, s, pairs, own):
@@ -140,8 +147,8 @@
             key = split(kv_scr[p, r, :, 0 : s.proj])
             val = split(kv_scr[p, r, :, s.proj : 2 * s.proj])
             store(key_out, key, p, r)
-            score_out[p, r] = dot3(pair_of(q_ref, r), key, NT) - lse_ref[r]
-            cot_out[p, r] = dot3(pair_of(g_ref, r), val, NT) - corr_ref[r]
+            score_out[p, r] = dot3_plain(pair_of(q_ref, r), key, NT) - lse_ref[r]
+            cot_out[p, r] = dot3_plain(pair_of(g_ref, r), val, NT) - corr_ref[r]
 
 
 def back(where_ref, *refs, s, nrow):
@@ -252,10 +259,12 @@
     return pltpu.with_memory_space_constraint(x, pltpu.VMEM)
 
 
-def call(body, outs, args, scratch=(), scalar=False, inputs=pltpu.VMEM, outputs=pltpu.VMEM):
+def call(body, outs, args, scratch=(), scalar=False, inputs=pltpu.VMEM, outputs=pltpu.VMEM, far_away=False):
     specs = [pl.BlockSpec(memory_space=inputs)] * len(args)
     if scalar:
         specs[0] = pl.BlockSpec(memory_space=pltpu.SMEM)
+    if far_away:
+        specs[0] = pl.BlockSpec(memory_space=pl.ANY)
     return pl.pallas_call(
         body,
         out_shape=outs,
@@ -278,7 +287,13 @@
 
     blocks = [here(move(pair, "col", ncol, k)) for k in range(1, ncol)]
     other = here(move(bias, "sub", nsub, 1))
-    (packed,) = call(functools.partial(pack, s=s), [pltpu.VMEM((s.wide, s.two), BF16)], [here(bias), other])
+    (packed,) = call(
+        functools.partial(pack, s=s),
+        [pltpu.VMEM((s.wide, s.two), BF16)],
+        [pltpu.with_memory_space_constraint(bias, pltpu.HBM), other],
+        scratch=[pltpu.VMEM(bias.shape, BF16), pltpu.SemaphoreType.DMA((1,))],
+        far_away=True,
+    )
     groups = [here(packed)] + [here(move(packed, "row", nrow, k)) for k in range(1, nrow)]
     place = lax.axis_index("col") ^ (lax.axis_index("row") * nsub + lax.axis_index("sub"))
     place = place.reshape(1)

time: 25.3 us -> 25.3 us (level)
  local copies, waits for them, and re-layouts: 0.84 us -> 0 us
  Pallas kernels: 5.75 us -> 6.49 us
    unnamed x2 -> x0, local copies, waits for them, and re-layouts: 0.84 us -> none
    pallas_call x8, Pallas kernels: 5.75 us -> 6.49 us  [call(): pl.pallas_call(body, out_shape=outs, in_specs=specs, out_specs=[pl.BlockS...]
  transfers between devices with their start and end apart: 10 -> 10, of which waited for: 2 -> 2; matrix products, arithmetic and copies ran while one was open for 0% -> 0% of each run, Pallas kernels for 15% -> 18%
where the time goes in v6:
time: 25.3 us; the launch traced here: 25 us
  starting transfers between devices  13.4 us (53%)
  Pallas kernels  6.49 us (26%)
  waiting for transfers between devices  4.41 us (17%)
  between operations  0.72 us (3%)
    ppermute x10, starting transfers between devices, move(): return lax.ppermute(x, axis, xor_pairs(size, mask))  13.4 us
    pallas_call x8, Pallas kernels, call(): pl.pallas_call(body, out_shape=outs, in_specs=specs, out_specs=[pl.BlockS...  6.49 us
    ppermute x10, waiting for transfers between devices, move(): return lax.ppermute(x, axis, xor_pairs(size, mask))  4.41 us
  transfers between devices with their start and end apart: 10, of which 2 were waited for; matrix products, arithmetic and copies ran while one was open for 0% of the time, Pallas kernels for 18%

profile of v6, /device:TPU:0, one launch (start us, length us, event | category | flops | bytes accessed | tf_op | source)
XLA Modules:
  0.0 25.0 jit_solution(16286205882062106288)
XLA Ops:
  0.6 0.6 %collective-permute-start = (bf16[4,64,64]{2,1,0:T(8,128)(2,1)}, bf16[4,64,64]{2,1,0:T(8,128)(2,1)S(1)}, u32[]{:S(2)}, u32[]{:S(2)}) collective-permute-start(bf16[4,64,64]{2,1,0:T(8,128)(2,1)} %own_hbm.1), channel_id=1, source_target_pairs={{0,1},{1,0},{2,3},{3,2},{4,5},{5,4},{6,7},{7,6},{8,9},{9,8},{10,11... | collective-permute-start | bytes 98312 | tf_op jit(solution)/shard_map/ppermute | solution.py:286
  1.2 2.6 %collective-permute-start.2 = (f32[2,64,128]{2,1,0:T(8,128)}, f32[2,64,128]{2,1,0:T(8,128)S(1)}, u32[]{:S(2)}, u32[]{:S(2)}) collective-permute-start(f32[2,64,128]{2,1,0:T(8,128)} %refs_0_.1), channel_id=1, source_target_pairs={{0,4},{4,0},{8,12},{12,8},{1,5},{5,1},{9,13},{13,9},{2,6},{6,2},{1... | collective-permute-start | bytes 196616 | tf_op jit(solution)/shard_map/ppermute | solution.py:286
  3.8 2.5 %collective-permute-start.4 = (f32[2,64,128]{2,1,0:T(8,128)}, f32[2,64,128]{2,1,0:T(8,128)S(1)}, u32[]{:S(2)}, u32[]{:S(2)}) collective-permute-start(f32[2,64,128]{2,1,0:T(8,128)} %refs_0_.1), channel_id=1, source_target_pairs={{0,12},{4,8},{8,4},{12,0},{1,13},{5,9},{9,5},{13,1},{2,14},{6,10},... | collective-permute-start | bytes 196616 | tf_op jit(solution)/shard_map/ppermute | solution.py:286
  6.3 0.1 collective-permute-start.3
  6.4 0.0 collective-permute-done.other_ref
  6.4 0.9 %shard_map.104.refs_3_ = bf16[256,128]{1,0:T(8,128)(2,1)S(1)} custom-call(bf16[4,64,64]{2,1,0:T(8,128)(2,1)} %own_hbm.1, bf16[4,64,64]{2,1,0:T(8,128)(2,1)S(1)} %collective-permute-done.other_ref), custom_call_target="tpu_custom_call" | custom-call | tf_op jit(solution)/shard_map/pallas_call | solution.py:268
  7.3 1.6 %collective-permute-start.1 = (bf16[256,128]{1,0:T(8,128)(2,1)S(1)}, bf16[256,128]{1,0:T(8,128)(2,1)S(1)}, u32[]{:S(2)}, u32[]{:S(2)}) collective-permute-start(bf16[256,128]{1,0:T(8,128)(2,1)S(1)} %shard_map.104.refs_3_), channel_id=1, source_target_pairs={{0,2},{2,0},{1,3},{3,1},{4,6},{6,4},{5,7},{7,5},{8,10},{10,8},{9,1... | collective-permute-start | bytes 196616 | tf_op jit(solution)/shard_map/ppermute | solution.py:286
  8.8 1.4 %shard_map.103 = (bf16[2,2,256,128]{3,2,1,0:T(8,128)(2,1)S(1)}, bf16[2,2,256,128]{3,2,1,0:T(8,128)(2,1)S(1)}, bf16[2,128,128]{2,1,0:T(8,128)(2,1)S(1)}, bf16[2,1...) custom-call(f32[2,64,128]{2,1,0:T(8,128)} %refs_0_.1, ...), custom_call_target="tpu_custom_call" | custom-call | tf_op jit(solution)/shard_map/pallas_call | solution.py:268
  10.3 0.0 collective-permute-done.2.refs_6_
  10.3 0.6 %shard_map.105 = (bf16[2,1,2,128,128]{4,3,2,1,0:T(8,128)(2,1)S(1)}, f32[1,2,256,128]{3,2,1,0:T(8,128)S(1)}, f32[1,2,256,128]{3,2,1,0:T(8,128)S(1)}) custom-call(s32[1]{0:T(128)} %bitcast.where_ref, bf16[2,2,256,128]{3,2,1,0:T(8,128)(2,1)S(1)} %get-tuple-element.27.refs_0_, bf16[2,2,256,128]{3,2,1,0:T(8,128)(2,1)S(1)} %get-tuple-element.28.refs_1_, ...), custom_call_target="tpu_custom_call" | custom-call | tf_op jit(solution)/shard_map/pallas_call | solution.py:268
  10.9 2.4 %collective-permute-done.3.refs_5_ = f32[2,64,128]{2,1,0:T(8,128)S(1)} collective-permute-done((f32[2,64,128]{2,1,0:T(8,128)}, f32[2,64,128]{2,1,0:T(8,128)S(1)}, u32[]{:S(2)}, u32[]{:S(2)}) %collective-permute-start.3) | collective-permute-done | bytes 65568 | tf_op jit(solution)/shard_map/ppermute | solution.py:286
  13.3 0.6 %shard_map.106 = (bf16[2,1,2,128,128]{4,3,2,1,0:T(8,128)(2,1)S(1)}, f32[1,2,256,128]{3,2,1,0:T(8,128)S(1)}, f32[1,2,256,128]{3,2,1,0:T(8,128)S(1)}) custom-call(s32[1]{0:T(128)} %bitcast.where_ref, bf16[2,2,256,128]{3,2,1,0:T(8,128)(2,1)S(1)} %get-tuple-element.27.refs_0_, bf16[2,2,256,128]{3,2,1,0:T(8,128)(2,1)S(1)} %get-tuple-element.28.refs_1_, ...), custom_call_target="tpu_custom_call" | custom-call | tf_op jit(solution)/shard_map/pallas_call | solution.py:268
  13.9 0.0 collective-permute-done.1.refs_4_
  13.9 1.2 %shard_map.107 = (f32[128,128]{1,0:T(8,128)S(1)}, bf16[144,128]{1,0:T(8,128)(2,1)S(1)}, bf16[144,128]{1,0:T(8,128)(2,1)S(1)}, bf16[144,128]{1,0:T(8,128)(2,1)S(1...) custom-call(s32[1]{0:T(128)} %bitcast.where_ref, ...), custom_call_target="tpu_custom_call" | custom-call | tf_op jit(solution)/shard_map/pallas_call | solution.py:268
  15.1 0.1 collective-permute-start.5
  15.2 0.0 collective-permute-start.6
  15.2 3.3 %collective-permute-start.7 = (bf16[144,128]{1,0:T(8,128)(2,1)S(1)}, bf16[144,128]{1,0:T(8,128)(2,1)S(1)}, u32[]{:S(2)}, u32[]{:S(2)}) collective-permute-start(bf16[144,128]{1,0:T(8,128)(2,1)S(1)} %get-tuple-element.46), channel_id=1, source_target_pairs={{0,8},{4,12},{8,0},{12,4},{1,9},{5,13},{9,1},{13,5},{2,10},{6,14},... | collective-permute-start | bytes 110600 | tf_op jit(solution)/shard_map/ppermute | solution.py:286
  18.5 1.1 %collective-permute-start.8 = (bf16[144,128]{1,0:T(8,128)(2,1)S(1)}, bf16[144,128]{1,0:T(8,128)(2,1)S(1)}, u32[]{:S(2)}, u32[]{:S(2)}) collective-permute-start(bf16[144,128]{1,0:T(8,128)(2,1)S(1)} %get-tuple-element.47), channel_id=1, source_target_pairs={{0,12},{4,8},{8,4},{12,0},{1,13},{5,9},{9,5},{13,1},{2,14},{6,10},... | collective-permute-start | bytes 110600 | tf_op jit(solution)/shard_map/ppermute | solution.py:286
  19.6 0.0 collective-permute-done.5.got_ref
  19.6 0.2 shard_map.109
  19.8 1.6 %collective-permute-start.9 = (bf16[144,128]{1,0:T(8,128)(2,1)S(1)}, bf16[144,128]{1,0:T(8,128)(2,1)S(1)}, u32[]{:S(2)}, u32[]{:S(2)}) collective-permute-start(bf16[144,128]{1,0:T(8,128)(2,1)S(1)} %get-tuple-element.48), channel_id=1, source_target_pairs={{0,2},{2,0},{1,3},{3,1},{4,6},{6,4},{5,7},{7,5},{8,10},{10,8},{9,1... | collective-permute-start | bytes 110600 | tf_op jit(solution)/shard_map/ppermute | solution.py:286
  21.4 0.8 %shard_map.108 = f32[2,64,128]{2,1,0:T(8,128)} custom-call(f32[2,256,128]{2,1,0:T(8,128)S(1)} %get-tuple-element.39.dq_ref, bf16[2,128,128]{2,1,0:T(8,128)(2,1)S(1)} %get-tuple-element.40.wq_ref), custom_call_target="tpu_custom_call" | custom-call | tf_op jit(solution)/shard_map/pallas_call | solution.py:268
  22.2 2.0 %collective-permute-done.8.refs_2_ = bf16[144,128]{1,0:T(8,128)(2,1)S(1)} collective-permute-done((bf16[144,128]{1,0:T(8,128)(2,1)S(1)}, bf16[144,128]{1,0:T(8,128)(2,1)S(1)}, u32[]{:S(2)}, u32[]{:S(2)}) %collective-permute-start.8) | collective-permute-done | bytes 36896 | tf_op jit(solution)/shard_map/ppermute | solution.py:286
  24.3 0.8 %shard_map.110 = (f32[2,64,128]{2,1,0:T(8,128)}, f32[4,64,64]{2,1,0:T(8,128)}) custom-call(f32[128,128]{1,0:T(8,128)S(1)} %get-tuple-element.41.own_ref, f32[256,128]{1,0:T(8,128)S(1)} %get-tuple-element.44.sum_ref, bf16[144,128]{1,0:T(8,128)(2,1)S(1)} %collective-permute-done.6.refs_0_, bf16[144,128]{1,0:T(8,128)(2,1)S(1)} %collective-permute-done.7.refs_1_, ...), custom_call_target="tpu_custom_call" | custom-call | tf_op jit(solution)/shard_map/pallas_call | solution.py:268
  (4 shorter events, 0.0 us)
Async XLA Ops:
  0.6 5.8 %collective-permute-start = (bf16[4,64,64]{2,1,0:T(8,128)(2,1)}, bf16[4,64,64]{2,1,0:T(8,128)(2,1)S(1)}, u32[]{:S(2)}, u32[]{:S(2)}) collective-permute-start(bf16[4,64,64]{2,1,0:T(8,128)(2,1)} %own_hbm.1), channel_id=1, source_target_pairs={{0,1},{1,0},{2,3},{3,2},{4,5},{5,4},{6,7},{7,6},{8,9},{9,8},{10,11... | collective-permute-start | bytes 98312 | tf_op jit(solution)/shard_map/ppermute | solution.py:286
  1.2 9.1 %collective-permute-start.2 = (f32[2,64,128]{2,1,0:T(8,128)}, f32[2,64,128]{2,1,0:T(8,128)S(1)}, u32[]{:S(2)}, u32[]{:S(2)}) collective-permute-start(f32[2,64,128]{2,1,0:T(8,128)} %refs_0_.1), channel_id=1, source_target_pairs={{0,4},{4,0},{8,12},{12,8},{1,5},{5,1},{9,13},{13,9},{2,6},{6,2},{1... | collective-permute-start | bytes 196616 | tf_op jit(solution)/shard_map/ppermute | solution.py:286
  3.8 7.1 %collective-permute-start.4 = (f32[2,64,128]{2,1,0:T(8,128)}, f32[2,64,128]{2,1,0:T(8,128)S(1)}, u32[]{:S(2)}, u32[]{:S(2)}) collective-permute-start(f32[2,64,128]{2,1,0:T(8,128)} %refs_0_.1), channel_id=1, source_target_pairs={{0,12},{4,8},{8,4},{12,0},{1,13},{5,9},{9,5},{13,1},{2,14},{6,10},... | collective-permute-start | bytes 196616 | tf_op jit(solution)/shard_map/ppermute | solution.py:286
  6.3 7.0 %collective-permute-start.3 = (f32[2,64,128]{2,1,0:T(8,128)}, f32[2,64,128]{2,1,0:T(8,128)S(1)}, u32[]{:S(2)}, u32[]{:S(2)}) collective-permute-start(f32[2,64,128]{2,1,0:T(8,128)} %refs_0_.1), channel_id=1, source_target_pairs={{0,8},{4,12},{8,0},{12,4},{1,9},{5,13},{9,1},{13,5},{2,10},{6,14},... | collective-permute-start | bytes 196616 | tf_op jit(solution)/shard_map/ppermute | solution.py:286
  7.3 6.6 %collective-permute-start.1 = (bf16[256,128]{1,0:T(8,128)(2,1)S(1)}, bf16[256,128]{1,0:T(8,128)(2,1)S(1)}, u32[]{:S(2)}, u32[]{:S(2)}) collective-permute-start(bf16[256,128]{1,0:T(8,128)(2,1)S(1)} %shard_map.104.refs_3_), channel_id=1, source_target_pairs={{0,2},{2,0},{1,3},{3,1},{4,6},{6,4},{5,7},{7,5},{8,10},{10,8},{9,1... | collective-permute-start | bytes 196616 | tf_op jit(solution)/shard_map/ppermute | solution.py:286
  15.1 4.5 %collective-permute-start.5 = (f32[1,256,128]{2,1,0:T(8,128)S(1)}, f32[1,256,128]{2,1,0:T(8,128)S(1)}, u32[]{:S(2)}, u32[]{:S(2)}) collective-permute-start(f32[1,256,128]{2,1,0:T(8,128)S(1)} %get-tuple-element.43), channel_id=1, source_target_pairs={{0,1},{1,0},{2,3},{3,2},{4,5},{5,4},{6,7},{7,6},{8,9},{9,8},{10,11... | collective-permute-start | bytes 393224 | tf_op jit(solution)/shard_map/ppermute | solution.py:286
  15.2 7.0 %collective-permute-start.6 = (bf16[144,128]{1,0:T(8,128)(2,1)S(1)}, bf16[144,128]{1,0:T(8,128)(2,1)S(1)}, u32[]{:S(2)}, u32[]{:S(2)}) collective-permute-start(bf16[144,128]{1,0:T(8,128)(2,1)S(1)} %get-tuple-element.45), channel_id=1, source_target_pairs={{0,4},{4,0},{8,12},{12,8},{1,5},{5,1},{9,13},{13,9},{2,6},{6,2},{1... | collective-permute-start | bytes 110600 | tf_op jit(solution)/shard_map/ppermute | solution.py:286
  15.2 7.0 %collective-permute-start.7 = (bf16[144,128]{1,0:T(8,128)(2,1)S(1)}, bf16[144,128]{1,0:T(8,128)(2,1)S(1)}, u32[]{:S(2)}, u32[]{:S(2)}) collective-permute-start(bf16[144,128]{1,0:T(8,128)(2,1)S(1)} %get-tuple-element.46), channel_id=1, source_target_pairs={{0,8},{4,12},{8,0},{12,4},{1,9},{5,13},{9,1},{13,5},{2,10},{6,14},... | collective-permute-start | bytes 110600 | tf_op jit(solution)/shard_map/ppermute | solution.py:286
  18.5 5.8 %collective-permute-start.8 = (bf16[144,128]{1,0:T(8,128)(2,1)S(1)}, bf16[144,128]{1,0:T(8,128)(2,1)S(1)}, u32[]{:S(2)}, u32[]{:S(2)}) collective-permute-start(bf16[144,128]{1,0:T(8,128)(2,1)S(1)} %get-tuple-element.47), channel_id=1, source_target_pairs={{0,12},{4,8},{8,4},{12,0},{1,13},{5,9},{9,5},{13,1},{2,14},{6,10},... | collective-permute-start | bytes 110600 | tf_op jit(solution)/shard_map/ppermute | solution.py:286
  19.8 4.4 %collective-permute-start.9 = (bf16[144,128]{1,0:T(8,128)(2,1)S(1)}, bf16[144,128]{1,0:T(8,128)(2,1)S(1)}, u32[]{:S(2)}, u32[]{:S(2)}) collective-permute-start(bf16[144,128]{1,0:T(8,128)(2,1)S(1)} %get-tuple-element.48), channel_id=1, source_target_pairs={{0,2},{2,0},{1,3},{3,1},{4,6},{6,4},{5,7},{7,5},{8,10},{10,8},{9,1... | collective-permute-start | bytes 110600 | tf_op jit(solution)/shard_map/ppermute | solution.py:286

commit v7 on v5

--- a/solution.py
+++ b/solution.py
@@ -220,9 +220,16 @@
     out_ref[...] = dot3(split(dq), pair_of(wq_ref), NT).reshape(s.rows, s.cols, s.width)
 
 
-def finish(own_ref, sum_ref, *refs, s, ncol, nrow):
-    terms, parts = refs[: ncol - 1], refs[ncol - 1 : ncol + nrow - 2]
-    key_hbm, bias_hbm, key_out, bias_out, sem = refs[ncol + nrow - 2 :]
+def gather_up(own_ref, *refs):
+    total = own_ref[...]
+    for ref in refs[:-1]:
+        total = total + decode(ref)
+    refs[-1][...] = total
+
+
+def finish(own_ref, sum_ref, *refs, s, nrow):
+    terms, parts = refs[:1], refs[1:nrow]
+    key_hbm, bias_hbm, key_out, bias_out, sem = refs[nrow:]
     total = own_ref[...]
     for ref in terms:
         total = total + decode(ref)
@@ -344,10 +351,11 @@
     dgot = [here(move(sums[k - 1], "row", nrow, k)) for k in range(1, nrow)]
     part = jax.ShapeDtypeStruct((rows, cols, width), F32)
     (query_grad,) = call(functools.partial(tail, s=s), [part], [here(dq), wq])
+    (most,) = call(gather_up, [own_shape], [here(own), *got[1:]])
     key_grad, bias_grad = call(
-        functools.partial(finish, s=s, ncol=ncol, nrow=nrow),
+        functools.partial(finish, s=s, nrow=nrow),
         [pltpu.HBM((rows, cols, width), F32), pltpu.HBM((heads, cols, cols), F32)],
-        [here(own), here(summed), *got, *dgot],
+        [here(most), here(summed), got[0], *dgot],
         scratch=[
             pltpu.VMEM((rows, cols, width), F32),
             pltpu.VMEM((heads, cols, cols), F32),

time: 25.3 us -> 23.9 us (0.945)
  starting transfers between devices: 13.4 us -> 12.5 us
  waiting for transfers between devices: 4.31 us -> 3.85 us
    ppermute x10, starting transfers between devices: 13.4 us -> 12.5 us  [move(): return lax.ppermute(x, axis, xor_pairs(size, mask))]
    ppermute x10, waiting for transfers between devices: 4.31 us -> 3.85 us  [move(): return lax.ppermute(x, axis, xor_pairs(size, mask))]
    pallas_call x8 -> x9, Pallas kernels: 5.75 us -> 5.78 us  [call(): pl.pallas_call(body, out_shape=outs, in_specs=specs, out_specs=[pl.BlockS...]
  transfers between devices with their start and end apart: 10 -> 10, of which waited for: 2 -> 3; matrix products, arithmetic and copies ran while one was open for 0% -> 0% of each run, Pallas kernels for 15% -> 16%
where the time goes in v7:
time: 23.9 us; the launch traced here: 23.7 us
  starting transfers between devices  12.5 us (52%)
  Pallas kernels  5.78 us (24%)
  waiting for transfers between devices  3.85 us (16%)
  local copies, waits for them, and re-layouts  0.84 us (4%)
  between operations  0.72 us (3%)
    ppermute x10, starting transfers between devices, move(): return lax.ppermute(x, axis, xor_pairs(size, mask))  12.5 us
    pallas_call x9, Pallas kernels, call(): pl.pallas_call(body, out_shape=outs, in_specs=specs, out_specs=[pl.BlockS...  5.78 us
    ppermute x10, waiting for transfers between devices, move(): return lax.ppermute(x, axis, xor_pairs(size, mask))  3.85 us
    unnamed x2, local copies, waits for them, and re-layouts  0.84 us
  transfers between devices with their start and end apart: 10, of which 3 were waited for; matrix products, arithmetic and copies ran while one was open for 0% of the time, Pallas kernels for 16%

profile of v7, /device:TPU:0, one launch (start us, length us, event | category | flops | bytes accessed | tf_op | source)
XLA Modules:
  0.0 23.7 jit_solution(2178824727196151012)
XLA Ops:
  0.6 0.6 %collective-permute-start = (bf16[4,64,64]{2,1,0:T(8,128)(2,1)}, bf16[4,64,64]{2,1,0:T(8,128)(2,1)S(1)}, u32[]{:S(2)}, u32[]{:S(2)}) collective-permute-start(bf16[4,64,64]{2,1,0:T(8,128)(2,1)} %own_ref.1), channel_id=1, source_target_pairs={{0,1},{1,0},{2,3},{3,2},{4,5},{5,4},{6,7},{7,6},{8,9},{9,8},{10,11... | collective-permute-start | bytes 98312 | tf_op jit(solution)/shard_map/ppermute | solution.py:284
  1.2 2.6 %collective-permute-start.2 = (f32[2,64,128]{2,1,0:T(8,128)}, f32[2,64,128]{2,1,0:T(8,128)S(1)}, u32[]{:S(2)}, u32[]{:S(2)}) collective-permute-start(f32[2,64,128]{2,1,0:T(8,128)} %refs_0_.1), channel_id=1, source_target_pairs={{0,4},{4,0},{8,12},{12,8},{1,5},{5,1},{9,13},{13,9},{2,6},{6,2},{1... | collective-permute-start | bytes 196616 | tf_op jit(solution)/shard_map/ppermute | solution.py:284
  3.8 2.5 %collective-permute-start.4 = (f32[2,64,128]{2,1,0:T(8,128)}, f32[2,64,128]{2,1,0:T(8,128)S(1)}, u32[]{:S(2)}, u32[]{:S(2)}) collective-permute-start(f32[2,64,128]{2,1,0:T(8,128)} %refs_0_.1), channel_id=1, source_target_pairs={{0,12},{4,8},{8,4},{12,0},{1,13},{5,9},{9,5},{13,1},{2,14},{6,10},... | collective-permute-start | bytes 196616 | tf_op jit(solution)/shard_map/ppermute | solution.py:284
  6.3 0.1 collective-permute-start.3
  6.4 0.0 collective-permute-done.other_ref
  6.4 0.8 %copy-done = bf16[4,64,64]{2,1,0:T(8,128)(2,1)S(1)} copy-done((bf16[4,64,64]{2,1,0:T(8,128)(2,1)S(1)}, bf16[4,64,64]{2,1,0:T(8,128)(2,1)}, u32[]{:S(2)}) %copy-start) | copy-done | bytes 32792
  7.3 0.1 shard_map.104.refs_3_
  7.4 1.6 %collective-permute-start.1 = (bf16[256,128]{1,0:T(8,128)(2,1)S(1)}, bf16[256,128]{1,0:T(8,128)(2,1)S(1)}, u32[]{:S(2)}, u32[]{:S(2)}) collective-permute-start(bf16[256,128]{1,0:T(8,128)(2,1)S(1)} %shard_map.104.refs_3_), channel_id=1, source_target_pairs={{0,2},{2,0},{1,3},{3,1},{4,6},{6,4},{5,7},{7,5},{8,10},{10,8},{9,1... | collective-permute-start | bytes 196616 | tf_op jit(solution)/shard_map/ppermute | solution.py:284
  8.9 1.4 %shard_map.103 = (bf16[2,2,256,128]{3,2,1,0:T(8,128)(2,1)S(1)}, bf16[2,2,256,128]{3,2,1,0:T(8,128)(2,1)S(1)}, bf16[2,128,128]{2,1,0:T(8,128)(2,1)S(1)}, bf16[2,1...) custom-call(f32[2,64,128]{2,1,0:T(8,128)} %refs_0_.1, ...), custom_call_target="tpu_custom_call" | custom-call | tf_op jit(solution)/shard_map/pallas_call | solution.py:266
  10.4 0.6 %shard_map.105 = (bf16[2,1,2,128,128]{4,3,2,1,0:T(8,128)(2,1)S(1)}, f32[1,2,256,128]{3,2,1,0:T(8,128)S(1)}, f32[1,2,256,128]{3,2,1,0:T(8,128)S(1)}) custom-call(s32[1]{0:T(128)} %bitcast.where_ref, bf16[2,2,256,128]{3,2,1,0:T(8,128)(2,1)S(1)} %get-tuple-element.27.refs_0_, bf16[2,2,256,128]{3,2,1,0:T(8,128)(2,1)S(1)} %get-tuple-element.28.refs_1_, ...), custom_call_target="tpu_custom_call" | custom-call | tf_op jit(solution)/shard_map/pallas_call | solution.py:266
  11.0 2.3 %collective-permute-done.3.refs_5_ = f32[2,64,128]{2,1,0:T(8,128)S(1)} collective-permute-done((f32[2,64,128]{2,1,0:T(8,128)}, f32[2,64,128]{2,1,0:T(8,128)S(1)}, u32[]{:S(2)}, u32[]{:S(2)}) %collective-permute-start.3) | collective-permute-done | bytes 65568 | tf_op jit(solution)/shard_map/ppermute | solution.py:284
  13.3 0.6 %shard_map.106 = (bf16[2,1,2,128,128]{4,3,2,1,0:T(8,128)(2,1)S(1)}, f32[1,2,256,128]{3,2,1,0:T(8,128)S(1)}, f32[1,2,256,128]{3,2,1,0:T(8,128)S(1)}) custom-call(s32[1]{0:T(128)} %bitcast.where_ref, bf16[2,2,256,128]{3,2,1,0:T(8,128)(2,1)S(1)} %get-tuple-element.27.refs_0_, bf16[2,2,256,128]{3,2,1,0:T(8,128)(2,1)S(1)} %get-tuple-element.28.refs_1_, ...), custom_call_target="tpu_custom_call" | custom-call | tf_op jit(solution)/shard_map/pallas_call | solution.py:266
  13.9 1.1 %shard_map.107 = (f32[128,128]{1,0:T(8,128)S(1)}, bf16[144,128]{1,0:T(8,128)(2,1)S(1)}, bf16[144,128]{1,0:T(8,128)(2,1)S(1)}, bf16[144,128]{1,0:T(8,128)(2,1)S(1...) custom-call(s32[1]{0:T(128)} %bitcast.where_ref, ...), custom_call_target="tpu_custom_call" | custom-call | tf_op jit(solution)/shard_map/pallas_call | solution.py:266
  15.1 0.1 collective-permute-start.7
  15.2 1.1 %collective-permute-start.5 = (bf16[144,128]{1,0:T(8,128)(2,1)S(1)}, bf16[144,128]{1,0:T(8,128)(2,1)S(1)}, u32[]{:S(2)}, u32[]{:S(2)}) collective-permute-start(bf16[144,128]{1,0:T(8,128)(2,1)S(1)} %get-tuple-element.42), channel_id=1, source_target_pairs={{0,8},{4,12},{8,0},{12,4},{1,9},{5,13},{9,1},{13,5},{2,10},{6,14},... | collective-permute-start | bytes 110600 | tf_op jit(solution)/shard_map/ppermute | solution.py:284
  16.3 1.7 %collective-permute-start.6 = (bf16[144,128]{1,0:T(8,128)(2,1)S(1)}, bf16[144,128]{1,0:T(8,128)(2,1)S(1)}, u32[]{:S(2)}, u32[]{:S(2)}) collective-permute-start(bf16[144,128]{1,0:T(8,128)(2,1)S(1)} %get-tuple-element.43), channel_id=1, source_target_pairs={{0,12},{4,8},{8,4},{12,0},{1,13},{5,9},{9,5},{13,1},{2,14},{6,10},... | collective-permute-start | bytes 110600 | tf_op jit(solution)/shard_map/ppermute | solution.py:284
  18.0 0.7 %collective-permute-start.8 = (bf16[144,128]{1,0:T(8,128)(2,1)S(1)}, bf16[144,128]{1,0:T(8,128)(2,1)S(1)}, u32[]{:S(2)}, u32[]{:S(2)}) collective-permute-start(bf16[144,128]{1,0:T(8,128)(2,1)S(1)} %get-tuple-element.47), channel_id=1, source_target_pairs={{0,4},{4,0},{8,12},{12,8},{1,5},{5,1},{9,13},{13,9},{2,6},{6,2},{1... | collective-permute-start | bytes 110600 | tf_op jit(solution)/shard_map/ppermute | solution.py:284
  18.7 0.2 shard_map.110
  18.9 1.6 %collective-permute-start.9 = (bf16[144,128]{1,0:T(8,128)(2,1)S(1)}, bf16[144,128]{1,0:T(8,128)(2,1)S(1)}, u32[]{:S(2)}, u32[]{:S(2)}) collective-permute-start(bf16[144,128]{1,0:T(8,128)(2,1)S(1)} %get-tuple-element.48), channel_id=1, source_target_pairs={{0,2},{2,0},{1,3},{3,1},{4,6},{6,4},{5,7},{7,5},{8,10},{10,8},{9,1... | collective-permute-start | bytes 110600 | tf_op jit(solution)/shard_map/ppermute | solution.py:284
  20.5 0.8 %shard_map.108 = f32[2,64,128]{2,1,0:T(8,128)} custom-call(f32[2,256,128]{2,1,0:T(8,128)S(1)} %get-tuple-element.39.dq_ref, bf16[2,128,128]{2,1,0:T(8,128)(2,1)S(1)} %get-tuple-element.40.wq_ref), custom_call_target="tpu_custom_call" | custom-call | tf_op jit(solution)/shard_map/pallas_call | solution.py:266
  21.3 1.0 %collective-permute-done.6.refs_1_ = bf16[144,128]{1,0:T(8,128)(2,1)S(1)} collective-permute-done((bf16[144,128]{1,0:T(8,128)(2,1)S(1)}, bf16[144,128]{1,0:T(8,128)(2,1)S(1)}, u32[]{:S(2)}, u32[]{:S(2)}) %collective-permute-start.6) | collective-permute-done | bytes 36896 | tf_op jit(solution)/shard_map/ppermute | solution.py:284
  22.3 0.1 shard_map.109.own_ref
  22.4 0.6 %collective-permute-done.9.refs_1_ = bf16[144,128]{1,0:T(8,128)(2,1)S(1)} collective-permute-done((bf16[144,128]{1,0:T(8,128)(2,1)S(1)}, bf16[144,128]{1,0:T(8,128)(2,1)S(1)}, u32[]{:S(2)}, u32[]{:S(2)}) %collective-permute-start.9) | collective-permute-done | bytes 36896 | tf_op jit(solution)/shard_map/ppermute | solution.py:284
  22.9 0.8 %shard_map.111 = (f32[2,64,128]{2,1,0:T(8,128)}, f32[4,64,64]{2,1,0:T(8,128)}) custom-call(f32[128,128]{1,0:T(8,128)S(1)} %shard_map.109.own_ref, f32[256,128]{1,0:T(8,128)S(1)} %get-tuple-element.46.sum_ref, bf16[144,128]{1,0:T(8,128)(2,1)S(1)} %collective-permute-done.8.refs_0_, bf16[144,128]{1,0:T(8,128)(2,1)S(1)} %collective-permute-done.9.refs_1_), custom_call_target="tpu_custom_call" | custom-call | tf_op jit(solution)/shard_map/pallas_call | solution.py:266
  (7 shorter events, 0.0 us)
Async XLA Ops:
  0.6 5.8 %collective-permute-start = (bf16[4,64,64]{2,1,0:T(8,128)(2,1)}, bf16[4,64,64]{2,1,0:T(8,128)(2,1)S(1)}, u32[]{:S(2)}, u32[]{:S(2)}) collective-permute-start(bf16[4,64,64]{2,1,0:T(8,128)(2,1)} %own_ref.1), channel_id=1, source_target_pairs={{0,1},{1,0},{2,3},{3,2},{4,5},{5,4},{6,7},{7,6},{8,9},{9,8},{10,11... | collective-permute-start | bytes 98312 | tf_op jit(solution)/shard_map/ppermute | solution.py:284
  1.2 9.2 %collective-permute-start.2 = (f32[2,64,128]{2,1,0:T(8,128)}, f32[2,64,128]{2,1,0:T(8,128)S(1)}, u32[]{:S(2)}, u32[]{:S(2)}) collective-permute-start(f32[2,64,128]{2,1,0:T(8,128)} %refs_0_.1), channel_id=1, source_target_pairs={{0,4},{4,0},{8,12},{12,8},{1,5},{5,1},{9,13},{13,9},{2,6},{6,2},{1... | collective-permute-start | bytes 196616 | tf_op jit(solution)/shard_map/ppermute | solution.py:284
  3.8 7.2 %collective-permute-start.4 = (f32[2,64,128]{2,1,0:T(8,128)}, f32[2,64,128]{2,1,0:T(8,128)S(1)}, u32[]{:S(2)}, u32[]{:S(2)}) collective-permute-start(f32[2,64,128]{2,1,0:T(8,128)} %refs_0_.1), channel_id=1, source_target_pairs={{0,12},{4,8},{8,4},{12,0},{1,13},{5,9},{9,5},{13,1},{2,14},{6,10},... | collective-permute-start | bytes 196616 | tf_op jit(solution)/shard_map/ppermute | solution.py:284
  6.3 7.0 %collective-permute-start.3 = (f32[2,64,128]{2,1,0:T(8,128)}, f32[2,64,128]{2,1,0:T(8,128)S(1)}, u32[]{:S(2)}, u32[]{:S(2)}) collective-permute-start(f32[2,64,128]{2,1,0:T(8,128)} %refs_0_.1), channel_id=1, source_target_pairs={{0,8},{4,12},{8,0},{12,4},{1,9},{5,13},{9,1},{13,5},{2,10},{6,14},... | collective-permute-start | bytes 196616 | tf_op jit(solution)/shard_map/ppermute | solution.py:284
  6.4 0.8 %copy-start = (bf16[4,64,64]{2,1,0:T(8,128)(2,1)S(1)}, bf16[4,64,64]{2,1,0:T(8,128)(2,1)}, u32[]{:S(2)}) copy-start(bf16[4,64,64]{2,1,0:T(8,128)(2,1)} %own_ref.1) | copy-start | bytes 98308
  7.4 6.6 %collective-permute-start.1 = (bf16[256,128]{1,0:T(8,128)(2,1)S(1)}, bf16[256,128]{1,0:T(8,128)(2,1)S(1)}, u32[]{:S(2)}, u32[]{:S(2)}) collective-permute-start(bf16[256,128]{1,0:T(8,128)(2,1)S(1)} %shard_map.104.refs_3_), channel_id=1, source_target_pairs={{0,2},{2,0},{1,3},{3,1},{4,6},{6,4},{5,7},{7,5},{8,10},{10,8},{9,1... | collective-permute-start | bytes 196616 | tf_op jit(solution)/shard_map/ppermute | solution.py:284
  15.1 3.6 %collective-permute-start.7 = (f32[1,256,128]{2,1,0:T(8,128)S(1)}, f32[1,256,128]{2,1,0:T(8,128)S(1)}, u32[]{:S(2)}, u32[]{:S(2)}) collective-permute-start(f32[1,256,128]{2,1,0:T(8,128)S(1)} %get-tuple-element.45), channel_id=1, source_target_pairs={{0,1},{1,0},{2,3},{3,2},{4,5},{5,4},{6,7},{7,6},{8,9},{9,8},{10,11... | collective-permute-start | bytes 393224 | tf_op jit(solution)/shard_map/ppermute | solution.py:284
  15.2 6.1 %collective-permute-start.5 = (bf16[144,128]{1,0:T(8,128)(2,1)S(1)}, bf16[144,128]{1,0:T(8,128)(2,1)S(1)}, u32[]{:S(2)}, u32[]{:S(2)}) collective-permute-start(bf16[144,128]{1,0:T(8,128)(2,1)S(1)} %get-tuple-element.42), channel_id=1, source_target_pairs={{0,8},{4,12},{8,0},{12,4},{1,9},{5,13},{9,1},{13,5},{2,10},{6,14},... | collective-permute-start | bytes 110600 | tf_op jit(solution)/shard_map/ppermute | solution.py:284
  16.3 6.0 %collective-permute-start.6 = (bf16[144,128]{1,0:T(8,128)(2,1)S(1)}, bf16[144,128]{1,0:T(8,128)(2,1)S(1)}, u32[]{:S(2)}, u32[]{:S(2)}) collective-permute-start(bf16[144,128]{1,0:T(8,128)(2,1)S(1)} %get-tuple-element.43), channel_id=1, source_target_pairs={{0,12},{4,8},{8,4},{12,0},{1,13},{5,9},{9,5},{13,1},{2,14},{6,10},... | collective-permute-start | bytes 110600 | tf_op jit(solution)/shard_map/ppermute | solution.py:284
  18.0 4.4 %collective-permute-start.8 = (bf16[144,128]{1,0:T(8,128)(2,1)S(1)}, bf16[144,128]{1,0:T(8,128)(2,1)S(1)}, u32[]{:S(2)}, u32[]{:S(2)}) collective-permute-start(bf16[144,128]{1,0:T(8,128)(2,1)S(1)} %get-tuple-element.47), channel_id=1, source_target_pairs={{0,4},{4,0},{8,12},{12,8},{1,5},{5,1},{9,13},{13,9},{2,6},{6,2},{1... | collective-permute-start | bytes 110600 | tf_op jit(solution)/shard_map/ppermute | solution.py:284
  18.9 4.0 %collective-permute-start.9 = (bf16[144,128]{1,0:T(8,128)(2,1)S(1)}, bf16[144,128]{1,0:T(8,128)(2,1)S(1)}, u32[]{:S(2)}, u32[]{:S(2)}) collective-permute-start(bf16[144,128]{1,0:T(8,128)(2,1)S(1)} %get-tuple-element.48), channel_id=1, source_target_pairs={{0,2},{2,0},{1,3},{3,1},{4,6},{6,4},{5,7},{7,5},{8,10},{10,8},{9,1... | collective-permute-start | bytes 110600 | tf_op jit(solution)/shard_map/ppermute | solution.py:284

commit v8 on v7

--- a/solution.py
+++ b/solution.py
@@ -29,6 +29,10 @@
     size = b[0].shape[axis]
     both = one(a[0], jnp.concatenate(b, axis=axis), dims)
     return both[:, :size] + both[:, size:] + one(a[1], b[0], dims)
+
+
+def dot3_plain(a, b, dims):
+    return one(a[0], b[0], dims) + one(a[0], b[1], dims) + one(a[1], b[0], dims)
 
 
 def pair_of(ref, *index):
@@ -121,7 +125,7 @@
 
 
 def from_block(s, ref):
-    return lambda both: dot3(split(ref[...].reshape(s.flat, s.width)), both, NN)
+    return lambda both: dot3_plain(split(ref[...].reshape(s.flat, s.width)), both, NN)
 
 
 def scores(where_ref, *refs, s, pairs, own):
@@ -140,8 +144,8 @@
             key = split(kv_scr[p, r, :, 0 : s.proj])
             val = split(kv_scr[p, r, :, s.proj : 2 * s.proj])
             store(key_out, key, p, r)
-            score_out[p, r] = dot3(pair_of(q_ref, r), key, NT) - lse_ref[r]
-            cot_out[p, r] = dot3(pair_of(g_ref, r), val, NT) - corr_ref[r]
+            score_out[p, r] = dot3_plain(pair_of(q_ref, r), key, NT) - lse_ref[r]
+            cot_out[p, r] = dot3_plain(pair_of(g_ref, r), val, NT) - corr_ref[r]
 
 
 def back(where_ref, *refs, s, nrow):

time: 23.9 us -> 23.9 us (level)
  no operation moved by 1% of the time
where the time goes in v8:
time: 23.9 us; the launch traced here: 23.7 us
  starting transfers between devices  12.5 us (52%)
  Pallas kernels  5.76 us (24%)
  waiting for transfers between devices  3.88 us (16%)
  local copies, waits for them, and re-layouts  0.84 us (4%)
  between operations  0.71 us (3%)
    ppermute x10, starting transfers between devices, move(): return lax.ppermute(x, axis, xor_pairs(size, mask))  12.5 us
    pallas_call x9, Pallas kernels, call(): pl.pallas_call(body, out_shape=outs, in_specs=specs, out_specs=[pl.BlockS...  5.76 us
    ppermute x10, waiting for transfers between devices, move(): return lax.ppermute(x, axis, xor_pairs(size, mask))  3.88 us
    unnamed x2, local copies, waits for them, and re-layouts  0.84 us
  transfers between devices with their start and end apart: 10, of which 3 were waited for; matrix products, arithmetic and copies ran while one was open for 0% of the time, Pallas kernels for 16%

profile of v8, /device:TPU:0, one launch (start us, length us, event | category | flops | bytes accessed | tf_op | source)
XLA Modules:
  0.0 23.7 jit_solution(7302226365362288229)
XLA Ops:
  0.6 0.6 %collective-permute-start = (bf16[4,64,64]{2,1,0:T(8,128)(2,1)}, bf16[4,64,64]{2,1,0:T(8,128)(2,1)S(1)}, u32[]{:S(2)}, u32[]{:S(2)}) collective-permute-start(bf16[4,64,64]{2,1,0:T(8,128)(2,1)} %own_ref.1), channel_id=1, source_target_pairs={{0,1},{1,0},{2,3},{3,2},{4,5},{5,4},{6,7},{7,6},{8,9},{9,8},{10,11... | collective-permute-start | bytes 98312 | tf_op jit(solution)/shard_map/ppermute | solution.py:288
  1.2 2.6 %collective-permute-start.2 = (f32[2,64,128]{2,1,0:T(8,128)}, f32[2,64,128]{2,1,0:T(8,128)S(1)}, u32[]{:S(2)}, u32[]{:S(2)}) collective-permute-start(f32[2,64,128]{2,1,0:T(8,128)} %refs_0_.1), channel_id=1, source_target_pairs={{0,4},{4,0},{8,12},{12,8},{1,5},{5,1},{9,13},{13,9},{2,6},{6,2},{1... | collective-permute-start | bytes 196616 | tf_op jit(solution)/shard_map/ppermute | solution.py:288
  3.8 2.5 %collective-permute-start.4 = (f32[2,64,128]{2,1,0:T(8,128)}, f32[2,64,128]{2,1,0:T(8,128)S(1)}, u32[]{:S(2)}, u32[]{:S(2)}) collective-permute-start(f32[2,64,128]{2,1,0:T(8,128)} %refs_0_.1), channel_id=1, source_target_pairs={{0,12},{4,8},{8,4},{12,0},{1,13},{5,9},{9,5},{13,1},{2,14},{6,10},... | collective-permute-start | bytes 196616 | tf_op jit(solution)/shard_map/ppermute | solution.py:288
  6.3 0.1 collective-permute-start.3
  6.4 0.8 %copy-done = bf16[4,64,64]{2,1,0:T(8,128)(2,1)S(1)} copy-done((bf16[4,64,64]{2,1,0:T(8,128)(2,1)S(1)}, bf16[4,64,64]{2,1,0:T(8,128)(2,1)}, u32[]{:S(2)}) %copy-start) | copy-done | bytes 32792
  7.3 0.1 shard_map.104.refs_3_
  7.4 1.6 %collective-permute-start.1 = (bf16[256,128]{1,0:T(8,128)(2,1)S(1)}, bf16[256,128]{1,0:T(8,128)(2,1)S(1)}, u32[]{:S(2)}, u32[]{:S(2)}) collective-permute-start(bf16[256,128]{1,0:T(8,128)(2,1)S(1)} %shard_map.104.refs_3_), channel_id=1, source_target_pairs={{0,2},{2,0},{1,3},{3,1},{4,6},{6,4},{5,7},{7,5},{8,10},{10,8},{9,1... | collective-permute-start | bytes 196616 | tf_op jit(solution)/shard_map/ppermute | solution.py:288
  8.9 1.4 %shard_map.103 = (bf16[2,2,256,128]{3,2,1,0:T(8,128)(2,1)S(1)}, bf16[2,2,256,128]{3,2,1,0:T(8,128)(2,1)S(1)}, bf16[2,128,128]{2,1,0:T(8,128)(2,1)S(1)}, bf16[2,1...) custom-call(f32[2,64,128]{2,1,0:T(8,128)} %refs_0_.1, ...), custom_call_target="tpu_custom_call" | custom-call | tf_op jit(solution)/shard_map/pallas_call | solution.py:270
  10.4 0.6 %shard_map.105 = (bf16[2,1,2,128,128]{4,3,2,1,0:T(8,128)(2,1)S(1)}, f32[1,2,256,128]{3,2,1,0:T(8,128)S(1)}, f32[1,2,256,128]{3,2,1,0:T(8,128)S(1)}) custom-call(s32[1]{0:T(128)} %bitcast.where_ref, bf16[2,2,256,128]{3,2,1,0:T(8,128)(2,1)S(1)} %get-tuple-element.27.refs_0_, bf16[2,2,256,128]{3,2,1,0:T(8,128)(2,1)S(1)} %get-tuple-element.28.refs_1_, ...), custom_call_target="tpu_custom_call" | custom-call | tf_op jit(solution)/shard_map/pallas_call | solution.py:270
  11.0 2.3 %collective-permute-done.3.refs_5_ = f32[2,64,128]{2,1,0:T(8,128)S(1)} collective-permute-done((f32[2,64,128]{2,1,0:T(8,128)}, f32[2,64,128]{2,1,0:T(8,128)S(1)}, u32[]{:S(2)}, u32[]{:S(2)}) %collective-permute-start.3) | collective-permute-done | bytes 65568 | tf_op jit(solution)/shard_map/ppermute | solution.py:288
  13.3 0.6 %shard_map.106 = (bf16[2,1,2,128,128]{4,3,2,1,0:T(8,128)(2,1)S(1)}, f32[1,2,256,128]{3,2,1,0:T(8,128)S(1)}, f32[1,2,256,128]{3,2,1,0:T(8,128)S(1)}) custom-call(s32[1]{0:T(128)} %bitcast.where_ref, bf16[2,2,256,128]{3,2,1,0:T(8,128)(2,1)S(1)} %get-tuple-element.27.refs_0_, bf16[2,2,256,128]{3,2,1,0:T(8,128)(2,1)S(1)} %get-tuple-element.28.refs_1_, ...), custom_call_target="tpu_custom_call" | custom-call | tf_op jit(solution)/shard_map/pallas_call | solution.py:270
  13.9 1.2 %shard_map.107 = (f32[128,128]{1,0:T(8,128)S(1)}, bf16[144,128]{1,0:T(8,128)(2,1)S(1)}, bf16[144,128]{1,0:T(8,128)(2,1)S(1)}, bf16[144,128]{1,0:T(8,128)(2,1)S(1...) custom-call(s32[1]{0:T(128)} %bitcast.where_ref, ...), custom_call_target="tpu_custom_call" | custom-call | tf_op jit(solution)/shard_map/pallas_call | solution.py:270
  15.1 0.1 collective-permute-start.7
  15.2 1.1 %collective-permute-start.5 = (bf16[144,128]{1,0:T(8,128)(2,1)S(1)}, bf16[144,128]{1,0:T(8,128)(2,1)S(1)}, u32[]{:S(2)}, u32[]{:S(2)}) collective-permute-start(bf16[144,128]{1,0:T(8,128)(2,1)S(1)} %get-tuple-element.42), channel_id=1, source_target_pairs={{0,8},{4,12},{8,0},{12,4},{1,9},{5,13},{9,1},{13,5},{2,10},{6,14},... | collective-permute-start | bytes 110600 | tf_op jit(solution)/shard_map/ppermute | solution.py:288
  16.3 1.7 %collective-permute-start.6 = (bf16[144,128]{1,0:T(8,128)(2,1)S(1)}, bf16[144,128]{1,0:T(8,128)(2,1)S(1)}, u32[]{:S(2)}, u32[]{:S(2)}) collective-permute-start(bf16[144,128]{1,0:T(8,128)(2,1)S(1)} %get-tuple-element.43), channel_id=1, source_target_pairs={{0,12},{4,8},{8,4},{12,0},{1,13},{5,9},{9,5},{13,1},{2,14},{6,10},... | collective-permute-start | bytes 110600 | tf_op jit(solution)/shard_map/ppermute | solution.py:288
  18.0 0.7 %collective-permute-start.8 = (bf16[144,128]{1,0:T(8,128)(2,1)S(1)}, bf16[144,128]{1,0:T(8,128)(2,1)S(1)}, u32[]{:S(2)}, u32[]{:S(2)}) collective-permute-start(bf16[144,128]{1,0:T(8,128)(2,1)S(1)} %get-tuple-element.47), channel_id=1, source_target_pairs={{0,4},{4,0},{8,12},{12,8},{1,5},{5,1},{9,13},{13,9},{2,6},{6,2},{1... | collective-permute-start | bytes 110600 | tf_op jit(solution)/shard_map/ppermute | solution.py:288
  18.7 0.2 shard_map.110
  18.9 1.6 %collective-permute-start.9 = (bf16[144,128]{1,0:T(8,128)(2,1)S(1)}, bf16[144,128]{1,0:T(8,128)(2,1)S(1)}, u32[]{:S(2)}, u32[]{:S(2)}) collective-permute-start(bf16[144,128]{1,0:T(8,128)(2,1)S(1)} %get-tuple-element.48), channel_id=1, source_target_pairs={{0,2},{2,0},{1,3},{3,1},{4,6},{6,4},{5,7},{7,5},{8,10},{10,8},{9,1... | collective-permute-start | bytes 110600 | tf_op jit(solution)/shard_map/ppermute | solution.py:288
  20.5 0.8 %shard_map.108 = f32[2,64,128]{2,1,0:T(8,128)} custom-call(f32[2,256,128]{2,1,0:T(8,128)S(1)} %get-tuple-element.39.dq_ref, bf16[2,128,128]{2,1,0:T(8,128)(2,1)S(1)} %get-tuple-element.40.wq_ref), custom_call_target="tpu_custom_call" | custom-call | tf_op jit(solution)/shard_map/pallas_call | solution.py:270
  21.3 1.0 %collective-permute-done.6.refs_1_ = bf16[144,128]{1,0:T(8,128)(2,1)S(1)} collective-permute-done((bf16[144,128]{1,0:T(8,128)(2,1)S(1)}, bf16[144,128]{1,0:T(8,128)(2,1)S(1)}, u32[]{:S(2)}, u32[]{:S(2)}) %collective-permute-start.6) | collective-permute-done | bytes 36896 | tf_op jit(solution)/shard_map/ppermute | solution.py:288
  22.3 0.1 shard_map.109.own_ref
  22.4 0.0 collective-permute-done.8.refs_0_
  22.4 0.6 %collective-permute-done.9.refs_1_ = bf16[144,128]{1,0:T(8,128)(2,1)S(1)} collective-permute-done((bf16[144,128]{1,0:T(8,128)(2,1)S(1)}, bf16[144,128]{1,0:T(8,128)(2,1)S(1)}, u32[]{:S(2)}, u32[]{:S(2)}) %collective-permute-start.9) | collective-permute-done | bytes 36896 | tf_op jit(solution)/shard_map/ppermute | solution.py:288
  23.0 0.8 %shard_map.111 = (f32[2,64,128]{2,1,0:T(8,128)}, f32[4,64,64]{2,1,0:T(8,128)}) custom-call(f32[128,128]{1,0:T(8,128)S(1)} %shard_map.109.own_ref, f32[256,128]{1,0:T(8,128)S(1)} %get-tuple-element.46.sum_ref, bf16[144,128]{1,0:T(8,128)(2,1)S(1)} %collective-permute-done.8.refs_0_, bf16[144,128]{1,0:T(8,128)(2,1)S(1)} %collective-permute-done.9.refs_1_), custom_call_target="tpu_custom_call" | custom-call | tf_op jit(solution)/shard_map/pallas_call | solution.py:270
  (7 shorter events, 0.0 us)
Async XLA Ops:
  0.6 5.8 %collective-permute-start = (bf16[4,64,64]{2,1,0:T(8,128)(2,1)}, bf16[4,64,64]{2,1,0:T(8,128)(2,1)S(1)}, u32[]{:S(2)}, u32[]{:S(2)}) collective-permute-start(bf16[4,64,64]{2,1,0:T(8,128)(2,1)} %own_ref.1), channel_id=1, source_target_pairs={{0,1},{1,0},{2,3},{3,2},{4,5},{5,4},{6,7},{7,6},{8,9},{9,8},{10,11... | collective-permute-start | bytes 98312 | tf_op jit(solution)/shard_map/ppermute | solution.py:288
  1.2 9.2 %collective-permute-start.2 = (f32[2,64,128]{2,1,0:T(8,128)}, f32[2,64,128]{2,1,0:T(8,128)S(1)}, u32[]{:S(2)}, u32[]{:S(2)}) collective-permute-start(f32[2,64,128]{2,1,0:T(8,128)} %refs_0_.1), channel_id=1, source_target_pairs={{0,4},{4,0},{8,12},{12,8},{1,5},{5,1},{9,13},{13,9},{2,6},{6,2},{1... | collective-permute-start | bytes 196616 | tf_op jit(solution)/shard_map/ppermute | solution.py:288
  3.8 7.2 %collective-permute-start.4 = (f32[2,64,128]{2,1,0:T(8,128)}, f32[2,64,128]{2,1,0:T(8,128)S(1)}, u32[]{:S(2)}, u32[]{:S(2)}) collective-permute-start(f32[2,64,128]{2,1,0:T(8,128)} %refs_0_.1), channel_id=1, source_target_pairs={{0,12},{4,8},{8,4},{12,0},{1,13},{5,9},{9,5},{13,1},{2,14},{6,10},... | collective-permute-start | bytes 196616 | tf_op jit(solution)/shard_map/ppermute | solution.py:288
  6.3 7.0 %collective-permute-start.3 = (f32[2,64,128]{2,1,0:T(8,128)}, f32[2,64,128]{2,1,0:T(8,128)S(1)}, u32[]{:S(2)}, u32[]{:S(2)}) collective-permute-start(f32[2,64,128]{2,1,0:T(8,128)} %refs_0_.1), channel_id=1, source_target_pairs={{0,8},{4,12},{8,0},{12,4},{1,9},{5,13},{9,1},{13,5},{2,10},{6,14},... | collective-permute-start | bytes 196616 | tf_op jit(solution)/shard_map/ppermute | solution.py:288
  6.4 0.8 %copy-start = (bf16[4,64,64]{2,1,0:T(8,128)(2,1)S(1)}, bf16[4,64,64]{2,1,0:T(8,128)(2,1)}, u32[]{:S(2)}) copy-start(bf16[4,64,64]{2,1,0:T(8,128)(2,1)} %own_ref.1) | copy-start | bytes 98308
  7.4 6.6 %collective-permute-start.1 = (bf16[256,128]{1,0:T(8,128)(2,1)S(1)}, bf16[256,128]{1,0:T(8,128)(2,1)S(1)}, u32[]{:S(2)}, u32[]{:S(2)}) collective-permute-start(bf16[256,128]{1,0:T(8,128)(2,1)S(1)} %shard_map.104.refs_3_), channel_id=1, source_target_pairs={{0,2},{2,0},{1,3},{3,1},{4,6},{6,4},{5,7},{7,5},{8,10},{10,8},{9,1... | collective-permute-start | bytes 196616 | tf_op jit(solution)/shard_map/ppermute | solution.py:288
  15.1 3.6 %collective-permute-start.7 = (f32[1,256,128]{2,1,0:T(8,128)S(1)}, f32[1,256,128]{2,1,0:T(8,128)S(1)}, u32[]{:S(2)}, u32[]{:S(2)}) collective-permute-start(f32[1,256,128]{2,1,0:T(8,128)S(1)} %get-tuple-element.45), channel_id=1, source_target_pairs={{0,1},{1,0},{2,3},{3,2},{4,5},{5,4},{6,7},{7,6},{8,9},{9,8},{10,11... | collective-permute-start | bytes 393224 | tf_op jit(solution)/shard_map/ppermute | solution.py:288
  15.2 6.1 %collective-permute-start.5 = (bf16[144,128]{1,0:T(8,128)(2,1)S(1)}, bf16[144,128]{1,0:T(8,128)(2,1)S(1)}, u32[]{:S(2)}, u32[]{:S(2)}) collective-permute-start(bf16[144,128]{1,0:T(8,128)(2,1)S(1)} %get-tuple-element.42), channel_id=1, source_target_pairs={{0,8},{4,12},{8,0},{12,4},{1,9},{5,13},{9,1},{13,5},{2,10},{6,14},... | collective-permute-start | bytes 110600 | tf_op jit(solution)/shard_map/ppermute | solution.py:288
  16.3 6.0 %collective-permute-start.6 = (bf16[144,128]{1,0:T(8,128)(2,1)S(1)}, bf16[144,128]{1,0:T(8,128)(2,1)S(1)}, u32[]{:S(2)}, u32[]{:S(2)}) collective-permute-start(bf16[144,128]{1,0:T(8,128)(2,1)S(1)} %get-tuple-element.43), channel_id=1, source_target_pairs={{0,12},{4,8},{8,4},{12,0},{1,13},{5,9},{9,5},{13,1},{2,14},{6,10},... | collective-permute-start | bytes 110600 | tf_op jit(solution)/shard_map/ppermute | solution.py:288
  18.0 4.4 %collective-permute-start.8 = (bf16[144,128]{1,0:T(8,128)(2,1)S(1)}, bf16[144,128]{1,0:T(8,128)(2,1)S(1)}, u32[]{:S(2)}, u32[]{:S(2)}) collective-permute-start(bf16[144,128]{1,0:T(8,128)(2,1)S(1)} %get-tuple-element.47), channel_id=1, source_target_pairs={{0,4},{4,0},{8,12},{12,8},{1,5},{5,1},{9,13},{13,9},{2,6},{6,2},{1... | collective-permute-start | bytes 110600 | tf_op jit(solution)/shard_map/ppermute | solution.py:288
  18.9 4.0 %collective-permute-start.9 = (bf16[144,128]{1,0:T(8,128)(2,1)S(1)}, bf16[144,128]{1,0:T(8,128)(2,1)S(1)}, u32[]{:S(2)}, u32[]{:S(2)}) collective-permute-start(bf16[144,128]{1,0:T(8,128)(2,1)S(1)} %get-tuple-element.48), channel_id=1, source_target_pairs={{0,2},{2,0},{1,3},{3,1},{4,6},{6,4},{5,7},{7,5},{8,10},{10,8},{9,1... | collective-permute-start | bytes 110600 | tf_op jit(solution)/shard_map/ppermute | solution.py:288
